TPU v7x, 32 devices: a whole 2x2x4 slice. The times are simulated.
32 devices in a mesh: cfg: 4 (over y, core), dom: 8 (over z, x).
Axes of the slice: x: 2, y: 2, z: 4, core: 2. Of those that a mesh axis runs over, the one named last changes fastest.
Arguments:
- features: bfloat16 [4, 12288, 512], P('cfg', 'dom'), may hold values from -6 to 6
- cotangent: bfloat16 [4, 12288, 512], P('cfg', 'dom'), may hold values from -6 to 6
- w_self: bfloat16 [512, 512], P('cfg'), may hold values from -0.25 to 0.25
- w_neigh: bfloat16 [512, 512], P('cfg'), may hold values from -0.25 to 0.25
- tiles: bfloat16 [64, 128, 128], P('dom'), may hold values from -0.3125 to 0.3125
- edge_peer: int32 [256, 1], P('dom'), may hold values from 0 to 7; in each aligned block of 32 rows (0 to 31, 32 to 63, ...) at most 8 rows name the same one
- edge_src: int32 [256], P('dom'), may hold values from 0 to 11
- edge_dst: int32 [256], P('dom'), may hold values from 0 to 11
- edge_tile: int32 [256], P('dom'), may hold values from 0 to 7
Outputs:
- hidden: bfloat16 [4, 12288, 512], P('cfg', 'dom')
- grad_self: float32 [512, 512], P('cfg')
- grad_neigh: float32 [512, 512], P('cfg')
Inputs may be any that keep to these rules, and one draw needn't show every extreme that they name: `edge_peer`: among the 32 edge blocks of one partition at most 8 have their destination on any one partition, and some destination partition takes exactly 8 of them.
All inputs are finite; a program needn't handle non-finite values.
Results may differ from a plain program's by a relative error of at most 0.0061.
Values may be sent and summed in bfloat16 or wider, within the bound.
No kernel may reach another device: no remote copies, remote signals or barrier semaphores. Data moves between devices by JAX's collectives and lax.ppermute only.
A program may use at most 128 MiB of HBM per device.

v0:
```python
import jax
import jax.numpy as jnp
from jax import lax
from jax.sharding import PartitionSpec as P


def head(pre):
    normed = pre * lax.rsqrt(jnp.mean(pre * pre, -1, keepdims=True) + 1e-05)
    return normed * jax.nn.sigmoid(normed)


def local(features, cotangent, w_self, w_neigh, tiles, edge_peer, edge_src, edge_dst, edge_tile):
    feats = features[0]
    rows, width = feats.shape
    tile = tiles.shape[1]
    blocks = rows // tile
    peers = lax.axis_size("dom")
    edges = edge_src.shape[0]
    per_peer = max(2, 2 * edges // peers)
    slots = peers * per_peer
    target = edge_peer[:, 0]
    peer_hot = (target[:, None] == jnp.arange(peers, dtype=jnp.int32)[None, :]).astype(jnp.int32)
    rank = jnp.sum((jnp.cumsum(peer_hot, 0) - 1) * peer_hot, 1)
    slot = target * per_peer + rank
    slot_hit = slot[:, None] == jnp.arange(slots, dtype=jnp.int32)[None, :]
    place = slot_hit.astype(jnp.bfloat16)
    labels = jnp.sum(jnp.where(slot_hit, (edge_dst + 1)[:, None], 0), 0)
    blocks_x = feats.reshape(blocks, tile, width)
    chosen = blocks_x[edge_src]
    chosen_tiles = tiles[edge_tile]
    partial_value = jnp.einsum(
        "etk,ekd->etd", chosen_tiles, chosen, preferred_element_type=jnp.float32
    ).astype(jnp.bfloat16)
    outgoing = jnp.einsum(
        "es,etd->std", place, partial_value, preferred_element_type=jnp.float32
    ).astype(jnp.bfloat16)
    got, got_labels = (
        lax.all_to_all(
            outgoing.reshape(peers, per_peer, tile, width),
            "dom",
            split_axis=0,
            concat_axis=0,
            tiled=True,
        ),
        lax.all_to_all(
            labels.reshape(peers, per_peer), "dom", split_axis=0, concat_axis=0, tiled=True
        ),
    )
    arrived = got.reshape(slots, tile, width)
    owner_hot = (
        got_labels.reshape(slots)[:, None] - 1 == jnp.arange(blocks, dtype=jnp.int32)[None, :]
    ).astype(jnp.bfloat16)
    aggregate = (
        jnp.einsum("sb,std->btd", owner_hot, arrived, preferred_element_type=jnp.float32)
        .reshape(rows, width)
        .astype(jnp.bfloat16)
    )
    total = jnp.dot(
        feats, lax.all_gather(w_self, "cfg", axis=0, tiled=True), preferred_element_type=jnp.float32
    )
    pre = total + jnp.dot(
        aggregate,
        lax.all_gather(w_neigh, "cfg", axis=0, tiled=True),
        preferred_element_type=jnp.float32,
    )
    out, pullback = jax.vjp(head, pre)
    grad_pre = pullback(cotangent[0].astype(jnp.float32))[0].astype(jnp.bfloat16)
    term_s = lax.dot_general(
        feats, grad_pre, (((0,), (0,)), ((), ())), preferred_element_type=jnp.float32
    )
    term_n = lax.dot_general(
        aggregate, grad_pre, (((0,), (0,)), ((), ())), preferred_element_type=jnp.float32
    )
    total_s, total_n = lax.psum((term_s, term_n), "dom")
    share_s, share_n = (
        lax.psum_scatter(total_s, "cfg", scatter_dimension=0, tiled=True),
        lax.psum_scatter(total_n, "cfg", scatter_dimension=0, tiled=True),
    )
    factor = float(lax.axis_size("cfg") * peers * rows) ** (-0.5)
    return (out.astype(jnp.bfloat16)[None], share_s * factor, share_n * factor)


def solution(mesh):
    placed = (
        P("cfg", "dom", None),
        P("cfg", "dom", None),
        P("cfg", None),
        P("cfg", None),
        P("dom", None, None),
        P("dom", None),
        P("dom"),
        P("dom"),
        P("dom"),
    )
    return jax.shard_map(
        local,
        mesh=mesh,
        in_specs=placed,
        out_specs=(P("cfg", "dom", None), P("cfg", None), P("cfg", None)),
        check_vma=False,
    )
```

profile of v0, /device:TPU:0, one launch (start us, length us, event | category | flops | bytes accessed | tf_op | source)
XLA Modules:
  0.0 381.3 jit_solution(4688032224034469824)
XLA Ops:
  7.2 0.0 copy-start
  7.2 0.8 fusion.19
  8.0 0.1 reduce_window_sum.11
  8.1 0.8 select_reduce_fusion.1
  8.9 0.7 fusion.26
  9.6 0.7 broadcast_add_fusion
  10.2 0.1 select_reduce_fusion
  10.3 0.7 all_to_all.9
  11.0 7.3 %all-to-all-start = ((s32[8,1,8]{2,1,0:T(1,128)}), s32[8,1,8]{2,1,0:T(1,128)S(1)}, u32[]{:S(2)}, u32[]{:S(2)}) async-start(s32[8,1,8]{2,1,0:T(1,128)} %bitcast.4), calls=%async_computation | async-start | bytes 8192 | tf_op jit(solution)/shard_map/all_to_all | solution.py:45
  18.3 0.7 compare_select_fusion
  19.0 0.7 compare_select_fusion.1
  19.6 0.0 copy-done
  19.6 0.0 copy-start.3
  19.6 2.7 gather_fusion.1
  22.4 0.0 copy-done.3
  22.4 0.7 gather_fusion
  23.1 3.4 convolution_convert_fusion
  26.6 6.5 %convert_bitcast_fusion = bf16[8,8,128,512]{3,1,0,2:T(8,128)(2,1)} fusion(bf16[32,128,512]{2,1,0:T(8,128)(2,1)S(1)} %convolution_convert_fusion, s32[32]{0:T(128)S(1)} %fusion.26), kind=kOutput, calls=%fused_computation.5 | convolution fusion | flops 272631808 | bytes 12583040 | tf_op jit(solution)/shard_map/es,etd->std/dot_general | solution.py:34
  33.1 7.4 %copy.25 = bf16[8,8,128,512]{3,1,2,0:T(8,128)(2,1)} copy(bf16[8,8,128,512]{3,1,0,2:T(8,128)(2,1)} %convert_bitcast_fusion) | data formatting | bytes 16777216 | tf_op jit(solution)/shard_map/reshape | solution.py:39
  40.5 0.0 all-to-all-done
  40.5 6.0 %all-to-all-start.1 = ((bf16[8,8,128,512]{3,1,2,0:T(8,128)(2,1)}), bf16[8,8,128,512]{3,1,2,0:T(8,128)(2,1)}, u32[]{:S(2)}, u32[]{:S(2)}) async-start(bf16[8,8,128,512]{3,1,2,0:T(8,128)(2,1)} %copy.25), calls=%async_computation.1 | async-start | bytes 16777216 | tf_op jit(solution)/shard_map/all_to_all | solution.py:38
  46.5 0.0 copy-start.6
  46.5 0.0 copy-start.7
  46.5 0.0 reduce-scatter.5.cloned.1.call-start
  46.6 1.8 copy.28
  48.4 0.0 copy-done.6
  48.4 7.2 %all_gather.6 = bf16[512,512]{1,0:T(8,128)(2,1)S(1)} all-gather(bf16[128,512]{1,0:T(8,128)(2,1)S(1)} %copy-done.6), channel_id=1, replica_groups=mesh['cfg'=4,'dom'=8] {'cfg'}, dimensions={0}, use_global_device_ids=true | all-gather | bytes 655360 | tf_op jit(solution)/shard_map/all_gather | solution.py:59
  55.6 0.0 copy-done.7
  55.6 7.9 %all_gather.7 = bf16[512,512]{1,0:T(8,128)(2,1)} all-gather(bf16[128,512]{1,0:T(8,128)(2,1)S(1)} %copy-done.7), channel_id=1, replica_groups=mesh['cfg'=4,'dom'=8] {'cfg'}, dimensions={0}, use_global_device_ids=true | all-gather | bytes 655360 | tf_op jit(solution)/shard_map/all_gather | solution.py:63
  63.5 2.7 fusion.12
  66.2 0.1 sub.15
  66.3 162.9 %all-to-all-done.1 = bf16[8,8,128,512]{3,1,2,0:T(8,128)(2,1)} async-done(((bf16[8,8,128,512]{3,1,2,0:T(8,128)(2,1)}), bf16[8,8,128,512]{3,1,2,0:T(8,128)(2,1)}, u32[]{:S(2)}, u32[]{:S(2)}) %all-to-all-start.1) | async-done | bytes 8388640 | tf_op jit(solution)/shard_map/all_to_all | solution.py:38
  229.1 4.6 %fusion.7 = bf16[12,128,512]{2,0,1:T(8,128)(2,1)S(1)} fusion(bf16[8,8,128,512]{3,1,2,0:T(8,128)(2,1)} %all-to-all-done.1, s32[64]{0:T(128)S(1)} %sub.15), kind=kOutput, calls=%fused_computation.20 | convolution fusion | flops 101450496 | bytes 9961728 | tf_op jit(solution)/shard_map/sb,std->btd/dot_general | solution.py:54
  233.7 0.0 copy-start.1
  233.7 0.0 copy-start.4
  233.7 0.9 copy.27
  234.6 1.0 copy-done.1
  235.6 0.1 copy-done.4
  235.7 1.1 multiply_reduce_fusion.1
  236.8 1.5 multiply_reduce_fusion
  238.3 2.9 fusion.6
  241.2 0.0 copy-start.5
  241.2 1.2 copy-done.5
  242.3 1.9 fusion.27
  244.3 0.0 reduce-scatter.5.cloned.1.call-update
  244.3 0.0 copy-start.2
  244.3 0.0 reduce-scatter.3.cloned.1.call-start
  244.4 3.5 fusion.15
  247.9 0.0 reduce-scatter.3.cloned.1.call-update
  247.9 0.0 all-reduce.3.cloned.1.call-start
  247.9 20.4 %reduce-scatter.5.cloned.1.call-done = f32[128,512]{0,1:T(8,128)} async-done(((f32[512,512]{0,1:T(8,128)}), f32[128,512]{0,1:T(8,128)}) %reduce-scatter.5.cloned.1.call-update) | async-done | bytes 262160 | tf_op jit(solution)/shard_map/reduce_scatter | solution.py:77
  268.4 27.3 %reduce-scatter.3.cloned.1.call-done = f32[128,512]{0,1:T(8,128)} async-done(((f32[512,512]{0,1:T(8,128)}), f32[128,512]{0,1:T(8,128)}) %reduce-scatter.3.cloned.1.call-update) | async-done | bytes 262160 | tf_op jit(solution)/shard_map/reduce_scatter | solution.py:76
  295.7 0.0 all-reduce.3.cloned.1.call-update
  295.7 0.0 copy-done.2
  295.7 1.6 copy.30
  297.3 74.7 %all-reduce.3.cloned.1.call-done = (f32[128,512]{0,1:T(8,128)}, f32[128,512]{0,1:T(8,128)}) async-done(((f32[128,512]{0,1:T(8,128)}, f32[128,512]{0,1:T(8,128)}), (f32[128,512]{0,1:T(8,128)}, f32[128,512]{0,1:T(8,128)})) %all-reduce.3.cloned.1.call-update) | async-done | bytes 524304 | tf_op jit(solution)/shard_map/psum | solution.py:74
  372.0 1.1 broadcast_multiply_fusion
  373.1 0.8 copy.31
  373.9 0.8 copy.32
  (5 shorter events, 0.1 us)
Async XLA Ops:
  7.2 12.5 %copy-start = (bf16[1,1536,512]{2,1,0:T(8,128)(2,1)S(1)}, bf16[1,1536,512]{2,1,0:T(8,128)(2,1)}, u32[]{:S(2)}) copy-start(bf16[1,1536,512]{2,1,0:T(8,128)(2,1)} %param.9) | copy-start | bytes 4718596
  11.0 29.5 %all-to-all-start = ((s32[8,1,8]{2,1,0:T(1,128)}), s32[8,1,8]{2,1,0:T(1,128)S(1)}, u32[]{:S(2)}, u32[]{:S(2)}) async-start(s32[8,1,8]{2,1,0:T(1,128)} %bitcast.4), calls=%async_computation | async-start | bytes 8192 | tf_op jit(solution)/shard_map/all_to_all | solution.py:45
  19.6 2.8 copy-start.3
  40.5 188.6 %all-to-all-start.1 = ((bf16[8,8,128,512]{3,1,2,0:T(8,128)(2,1)}), bf16[8,8,128,512]{3,1,2,0:T(8,128)(2,1)}, u32[]{:S(2)}, u32[]{:S(2)}) async-start(bf16[8,8,128,512]{3,1,2,0:T(8,128)(2,1)} %copy.25), calls=%async_computation.1 | async-start | bytes 16777216 | tf_op jit(solution)/shard_map/all_to_all | solution.py:38
  46.5 1.8 copy-start.6
  46.5 9.0 %copy-start.7 = (bf16[128,512]{1,0:T(8,128)(2,1)S(1)}, bf16[128,512]{1,0:T(8,128)(2,1)}, u32[]{:S(2)}) copy-start(bf16[128,512]{1,0:T(8,128)(2,1)} %param.12) | copy-start | bytes 393220
  46.5 221.8 %reduce-scatter.5.cloned.1.call-start = ((), (), s32[]{:S(2)}) async-start(), calls=%async_computation.5 | async-start | bytes 1310720 | tf_op jit(solution)/shard_map/reduce_scatter | solution.py:77
  233.7 1.9 copy-start.1
  233.7 2.0 copy-start.4
  241.2 1.2 copy-start.5
  244.3 51.4 %copy-start.2 = (bf16[1,1536,512]{1,2,0:T(8,128)(2,1)S(1)}, bf16[1,1536,512]{1,2,0:T(8,128)(2,1)}, u32[]{:S(2)}) copy-start(bf16[1,1536,512]{1,2,0:T(8,128)(2,1)} %get-tuple-element.15) | copy-start | bytes 4718596
  244.3 51.4 %reduce-scatter.3.cloned.1.call-start = ((), (), s32[]{:S(2)}) async-start(), calls=%async_computation.4 | async-start | bytes 1310720 | tf_op jit(solution)/shard_map/reduce_scatter | solution.py:76
  247.9 124.1 %all-reduce.3.cloned.1.call-start = ((), (), s32[]{:S(2)}) async-start(), calls=%async_computation.6 | async-start | bytes 1048576 | tf_op jit(solution)/shard_map/psum | solution.py:74
Sparse Core Ops, SparseCore 0:
  244.4 23.8 reduce-scatter.4
  270.9 24.7 reduce-scatter.2
  299.2 72.7 all-reduce.2
where the time goes:
time: 382 us; the launch traced here: 381 us
  waiting for transfers between devices  285 us (75%)
  matrix products  23.8 us (6%)
  local copies, waits for them, and re-layouts  19.8 us (5%)
  blocking collectives  15.1 us (4%)
  between operations  13.9 us (4%)
  starting transfers between devices  13.4 us (4%)
  other arithmetic  9.93 us (3%)
    all_to_all x1, waiting for transfers between devices, local(): lax.all_to_all(outgoing.reshape(peers, per_peer, tile, width), 'dom', spl...  163 us
    psum x1, waiting for transfers between devices, local(): total_s, total_n = lax.psum((term_s, term_n), 'dom')  74.7 us
    reduce_scatter x1, waiting for transfers between devices, local(): lax.psum_scatter(total_s, 'cfg', scatter_dimension=0, tiled=True)  27.3 us
    reduce_scatter x1, waiting for transfers between devices, local(): lax.psum_scatter(total_n, 'cfg', scatter_dimension=0, tiled=True)  20.4 us
    all_gather x1, blocking collectives, local(): lax.all_gather(w_neigh, 'cfg', axis=0, tiled=True)  7.89 us
  transfers between devices with their start and end apart: 5, of which 4 were waited for; matrix products, arithmetic and copies ran while one was open for 8% of the time, Pallas kernels for 0%

commit v1 on v0

v1 whole, which is shorter than its diff:
```python
import functools

import jax
import jax.numpy as jnp
from jax import lax
from jax.experimental import pallas as pl
from jax.experimental.pallas import tpu as pltpu
from jax.sharding import PartitionSpec as P


BF16, F32, I32 = jnp.bfloat16, jnp.float32, jnp.int32
WHOLE = pl.BlockSpec(memory_space=pltpu.VMEM)
LANES = 128


def swap(value, axis, bits):
    size = lax.axis_size(axis)
    return lax.ppermute(value, axis, [(i, i ^ bits) for i in range(size)])


def bits_of(axis):
    size = lax.axis_size(axis)
    assert size & (size - 1) == 0
    return [1 << k for k in range(size.bit_length() - 1)]


def pack_kernel(at, tiles_ref, peer_ref, src_ref, dst_ref, tile_ref, packed_ref, turned_ref, info_ref):
    count, tile, _ = tiles_ref.shape
    piece = packed_ref.shape[0] - info_ref.shape[0]
    edges = src_ref.shape[1]
    if piece % tile == 0:
        for i in range(piece // tile):
            packed_ref[i * tile : (i + 1) * tile] = tiles_ref[at[1] * (piece // tile) + i].T
    else:
        for i in range(count):
            turned_ref[i * tile : (i + 1) * tile] = tiles_ref[i].T
        packed_ref[:piece] = turned_ref[pl.ds(pl.multiple_of(at[1] * piece, piece), piece)]
    info_ref[...] = jnp.zeros_like(info_ref)
    for row, ref in enumerate((peer_ref, src_ref, dst_ref, tile_ref)):
        info_ref[row : row + 1, :edges] = ref[...].astype(F32)
    packed_ref[piece:] = info_ref[...].astype(BF16)


def turn_kernel(at, feats_ref, *refs):
    *out_refs, turned_ref = refs
    rows, half = feats_ref.shape
    slots = len(out_refs)
    part = half // slots
    step = 256 if rows % 256 == 0 else rows
    for i in range(rows // step):
        turned_ref[:, i * step : (i + 1) * step] = feats_ref[i * step : (i + 1) * step].T
    for k, out_ref in enumerate(out_refs):
        start = pl.multiple_of(((at[0] % slots) ^ k) * part, part)
        out_ref[...] = turned_ref[pl.ds(start, part)]


def turn_half(at, feats, peers, far):
    rows, width = feats.shape
    slots = peers // 2
    return pl.pallas_call(
        turn_kernel,
        out_shape=[jax.ShapeDtypeStruct((width // peers, rows), BF16)] * slots,
        grid_spec=pltpu.PrefetchScalarGridSpec(
            num_scalar_prefetch=1,
            grid=(1,),
            in_specs=[pl.BlockSpec((rows, width // 2), lambda i, at: (0, (at[0] // slots) ^ far))],
            out_specs=[WHOLE] * slots,
            scratch_shapes=[pltpu.VMEM((width // 2, rows), BF16)],
        ),
        compiler_params=pltpu.CompilerParams(vmem_limit_bytes=12 << 20),
        cost_estimate=pl.CostEstimate(flops=0, bytes_accessed=2 * rows * width, transcendentals=0),
    )(at, feats)


def reverse_bits(value, size):
    out = jnp.zeros_like(value)
    bit = 1
    while bit < size:
        out = out * 2 + (value // bit) % 2
        bit *= 2
    return out


def edges_kernel(slots, first, chunks, at, meta, *refs):
    x_refs = refs[: len(slots)]
    tiles_ref = refs[len(slots)]
    rest = refs[len(slots) + 1 :]
    tile = LANES
    edges = meta.shape[2]
    _, rows = x_refs[0].shape
    blocks = rows // tile
    if first and chunks:
        out_refs, acc_ref = rest[:-1], rest[-1]
        acc_ref[...] = jnp.zeros_like(acc_ref)
    elif first:
        acc_ref = rest[0]
        acc_ref[...] = jnp.zeros_like(acc_ref)
    else:
        out_refs, acc_ref = rest[1:-1], rest[-1]
        acc_ref[...] = rest[0][...]
    for slot, x_ref in zip(slots, x_refs):
        for base in range(0, edges, 32):
            values = []
            for e in range(base, min(base + 32, edges)):
                source = x_ref[:, pl.ds(pl.multiple_of(meta[slot, 0, e], tile), tile)]
                value = jnp.dot(source, tiles_ref[meta[slot, 2, e]], preferred_element_type=F32)
                values.append(value.astype(BF16).astype(F32))
            for i, value in enumerate(values):
                acc_ref[meta[slot, 1, base + i]] += value
    span = blocks // max(chunks, 1)
    peers = meta.shape[0]
    for chunk in range(chunks):
        for k in range(peers):
            start = (at[0] ^ k) * blocks + chunk * span
            for block in range(span):
                out_refs[chunk * peers + k][:, block * tile : (block + 1) * tile] = acc_ref[
                    start + block
                ].astype(BF16)


def sum_edges(at, meta, xs, slots, tiles, held, chunks):
    part, rows = xs[0].shape
    peers, _, edges = meta.shape
    total = (peers * (rows // LANES), part, LANES)
    if chunks:
        shapes = [jax.ShapeDtypeStruct((part, rows // chunks), BF16)] * (chunks * peers)
        scratch = [pltpu.VMEM(total, F32)]
    else:
        shapes, scratch = [jax.ShapeDtypeStruct(total, F32)], []
    operands = list(xs) + [tiles] + ([] if held is None else [held])
    return pl.pallas_call(
        functools.partial(edges_kernel, slots, held is None, chunks),
        out_shape=shapes,
        grid_spec=pltpu.PrefetchScalarGridSpec(
            num_scalar_prefetch=2,
            grid=(),
            in_specs=[WHOLE] * len(operands),
            out_specs=[WHOLE] * len(shapes),
            scratch_shapes=scratch,
        ),
        compiler_params=pltpu.CompilerParams(vmem_limit_bytes=24 << 20),
        cost_estimate=pl.CostEstimate(
            flops=2 * len(slots) * edges * LANES * LANES * part,
            bytes_accessed=2 * len(slots) * (part * rows + 8 * LANES * LANES),
            transcendentals=0,
        ),
    )(at, meta, *operands)


def head_kernel(peers, first, last, at, *refs):
    a_refs = refs[:peers]
    feats_ref, cot_ref, weights_ref = refs[peers : peers + 3]
    refs = refs[peers + 3 :]
    if not first:
        held_s, held_n = refs[1:3]
        refs = refs[3:]
    if last:
        out_ref, keep_s, keep_n, give_s, give_n, agg_ref, sum_s, sum_n = refs
    else:
        out_ref, sum_s, sum_n, agg_ref = refs
    width = feats_ref.shape[1]
    step = feats_ref.shape[0]
    i = pl.program_id(0)

    @pl.when(i == 0)
    def _():
        part = width // peers
        for k in range(peers):
            agg_ref[pl.ds(pl.multiple_of((at[0] ^ k) * part, part), part)] = a_refs[k][...]
        sum_s[...] = jnp.zeros_like(sum_s) if first else held_s[...]
        sum_n[...] = jnp.zeros_like(sum_n) if first else held_n[...]

    feats = feats_ref[...]
    agg = agg_ref[:, pl.ds(pl.multiple_of(i * step, step), step)]
    over_rows = (((0,), (0,)), ((), ()))
    pre = jnp.dot(feats, weights_ref[:, :width], preferred_element_type=F32)
    pre += lax.dot_general(agg, weights_ref[:, width:], over_rows, preferred_element_type=F32)
    scale = lax.rsqrt(jnp.mean(pre * pre, -1, keepdims=True) + 1e-05)
    normed = pre * scale
    gate = jax.nn.sigmoid(normed)
    out_ref[...] = (normed * gate).astype(BF16)
    slope = cot_ref[...].astype(F32) * (gate * (1.0 + normed * (1.0 - gate)))
    grad = scale * (slope - normed * jnp.mean(slope * normed, -1, keepdims=True))
    grad = grad.astype(BF16)
    sum_s[...] += lax.dot_general(feats, grad, over_rows, preferred_element_type=F32)
    sum_n[...] += jnp.dot(agg, grad, preferred_element_type=F32)

    if last:

        @pl.when(i == pl.num_programs(0) - 1)
        def _():
            pairs, share, _ = keep_s.shape
            side = at[1] % 2
            for total, keep, give in ((sum_s, keep_s, give_s), (sum_n, keep_n, give_n)):
                for pair in range(pairs):
                    here = pl.multiple_of((2 * pair + side) * share, share)
                    there = pl.multiple_of((2 * pair + 1 - side) * share, share)
                    keep[pair] = total[pl.ds(here, share)]
                    give[pair] = total[pl.ds(there, share)].astype(BF16)


def run_head(at, parts, feats, cot, weights, hidden, held, chunk, chunks, configs):
    rows, width = feats.shape
    span = rows // chunks
    step = 256 if span % 256 == 0 else 128
    steps = span // step
    base = chunk * steps
    by_rows = pl.BlockSpec((step, width), lambda i, at: (base + i, 0))
    first, last = chunk == 0, chunk == chunks - 1
    shapes = [jax.ShapeDtypeStruct((rows, width), BF16)]
    out_specs = [by_rows]
    sums = (width, width)
    scratch = [pltpu.VMEM((width, span), BF16)]
    peers = len(parts)
    if last:
        share = (configs // 2, width // configs, width)
        shapes += [jax.ShapeDtypeStruct(share, F32)] * 2 + [jax.ShapeDtypeStruct(share, BF16)] * 2
        out_specs += [WHOLE] * 4
        scratch += [pltpu.VMEM(sums, F32)] * 2
    else:
        shapes += [jax.ShapeDtypeStruct(sums, F32)] * 2
        out_specs += [WHOLE] * 2
    return pl.pallas_call(
        functools.partial(head_kernel, peers, first, last),
        out_shape=shapes,
        grid_spec=pltpu.PrefetchScalarGridSpec(
            num_scalar_prefetch=1,
            grid=(steps,),
            in_specs=[WHOLE] * peers
            + [by_rows, by_rows, WHOLE]
            + ([] if first else [pl.BlockSpec(memory_space=pl.ANY), WHOLE, WHOLE]),
            out_specs=out_specs,
            scratch_shapes=scratch,
        ),
        input_output_aliases={} if first else {peers + 4: 0},
        compiler_params=pltpu.CompilerParams(vmem_limit_bytes=24 << 20),
        cost_estimate=pl.CostEstimate(
            flops=8 * span * width * width, bytes_accessed=8 * span * width, transcendentals=span * width
        ),
    )(at, *parts, feats, cot, weights, *(() if first else (hidden, *held)))


def local(features, cotangent, w_self, w_neigh, tiles, edge_peer, edge_src, edge_dst, edge_tile):
    return layer(
        features[0], cotangent[0], w_self, w_neigh, tiles, edge_peer, edge_src, edge_dst, edge_tile
    )


def layer(feats, cot, w_self, w_neigh, tiles, edge_peer, edge_src, edge_dst, edge_tile):
    rows, width = feats.shape
    count, tile, _ = tiles.shape
    edges = edge_src.shape[0]
    assert tile == LANES and edges <= LANES
    peers = lax.axis_size("dom")
    configs = lax.axis_size("cfg")
    assert configs % 2 == 0 and peers % 2 == 0
    own = lax.axis_index("cfg")
    at = jnp.stack([lax.axis_index("dom"), own]).astype(I32)
    blocks = rows // tile
    chunks = 2 if blocks % 2 == 0 else 1
    dom_bits, cfg_bits = bits_of("dom"), bits_of("cfg")
    middle = peers // 2

    piece = count * tile // configs
    packed = pl.pallas_call(
        pack_kernel,
        out_shape=jax.ShapeDtypeStruct((piece + 16, tile), BF16),
        grid_spec=pltpu.PrefetchScalarGridSpec(
            num_scalar_prefetch=1,
            grid=(),
            in_specs=[WHOLE] * 5,
            out_specs=WHOLE,
            scratch_shapes=[pltpu.VMEM((count * tile, tile), BF16), pltpu.VMEM((16, tile), F32)],
        ),
        compiler_params=pltpu.CompilerParams(vmem_limit_bytes=8 << 20),
        name="pack",
    )(
        at,
        tiles,
        edge_peer.reshape(1, edges),
        edge_src.reshape(1, edges),
        edge_dst.reshape(1, edges),
        edge_tile.reshape(1, edges),
    )
    far_turned = turn_half(at, feats, peers, 1)
    near_turned = turn_half(at, feats, peers, 0)

    held, offsets = packed[None], [0]
    for bit in dom_bits[::-1]:
        held = jnp.concatenate([held, swap(held, "dom", bit)], 0)
        offsets = offsets + [k ^ bit for k in offsets]
    slot = {k: offsets.index(k) for k in range(peers)}
    quarters = held[:, :piece]
    pieces = jnp.concatenate([quarters[None], swap(quarters[None], "cfg", cfg_bits[-1])], 0)
    for bit in cfg_bits[:-1][::-1]:
        pieces = jnp.concatenate([pieces, swap(pieces, "cfg", bit)], 0)

    infos = held[:, piece : piece + 4, :edges].astype(I32)
    slot_of = jnp.arange(peers, dtype=I32)[:, None]
    if piece % tile == 0:
        per = piece // tile
        owner = reverse_bits((infos[:, 3] // per) ^ own, configs)
        which = (owner * peers + slot_of) * per + infos[:, 3] % per
        all_tiles = pieces.reshape(peers * count, tile, tile)
    else:
        which = slot_of * count + infos[:, 3]
        order = reverse_bits(jnp.arange(configs, dtype=I32) ^ own, configs)
        all_tiles = pieces[order].swapaxes(0, 1).reshape(peers * count, tile, tile)
    meta = jnp.stack([infos[:, 1] * tile, infos[:, 0] * blocks + infos[:, 2], which], 1)

    moved = {0: near_turned[0]}
    for k in range(1, peers):
        block = far_turned[k - middle] if k >= middle else near_turned[k]
        moved[k] = swap(block, "dom", k)

    weights = jnp.concatenate([w_self, w_neigh], 1)[None]
    for bit in cfg_bits[::-1]:
        weights = jnp.concatenate([weights, swap(weights, "cfg", bit)], 0)
    order = reverse_bits(jnp.arange(configs, dtype=I32) ^ own, configs)
    weights = weights[order].reshape(width, 2 * width)

    near, far = list(range(middle)), list(range(middle, peers))
    partly = sum_edges(at, meta, [moved[k] for k in near], [slot[k] for k in near], all_tiles, None, 0)[0]
    summed = sum_edges(at, meta, [moved[k] for k in far], [slot[k] for k in far], all_tiles, partly, chunks)
    held = hidden = None
    for chunk in range(chunks):
        parts = summed[chunk * peers : (chunk + 1) * peers]
        back = [parts[0]] + [swap(parts[k], "dom", k) for k in range(1, peers)]
        hidden, *held = run_head(
            at, back, feats, cot, weights, hidden, held, chunk, chunks, configs
        )
    keep_s, keep_n, give_s, give_n = held
    factor = float(configs * peers * rows) ** (-0.5)

    def reduce(keep, give, order):
        total = keep + swap(give, "cfg", cfg_bits[0]).astype(F32)
        for bit in cfg_bits[1:]:
            pairs = total.reshape((total.shape[0] // 2, 2) + total.shape[1:])
            side = (own // bit) % 2
            keep = lax.dynamic_index_in_dim(pairs, side, 1, keepdims=False)
            give = lax.dynamic_index_in_dim(pairs, 1 - side, 1, keepdims=False)
            total = keep + swap(give.astype(BF16), "cfg", bit).astype(F32)
        total = total[0]
        for bit in order:
            total = total + swap(total.astype(BF16), "dom", bit).astype(F32)
        return total * factor

    grad_s = reduce(keep_s, give_s, dom_bits)
    grad_n = reduce(keep_n, give_n, dom_bits[1:] + dom_bits[:1])
    return (hidden[None], grad_s, grad_n)


def solution(mesh):
    placed = (
        P("cfg", "dom", None),
        P("cfg", "dom", None),
        P("cfg", None),
        P("cfg", None),
        P("dom", None, None),
        P("dom", None),
        P("dom"),
        P("dom"),
        P("dom"),
    )
    return jax.shard_map(
        local,
        mesh=mesh,
        in_specs=placed,
        out_specs=(P("cfg", "dom", None), P("cfg", None), P("cfg", None)),
        check_vma=False,
    )
```

time: 382 us -> 168 us (0.44)
  waiting for transfers between devices: 285 us -> 63 us
  starting transfers between devices: 13.4 us -> 65.9 us
  matrix products: 23.8 us -> 0 us
  Pallas kernels: 0 us -> 18.8 us
  blocking collectives: 15.1 us -> 0 us
  between operations: 13.9 us -> 0.94 us
  local copies, waits for them, and re-layouts: 19.8 us -> 14.5 us
  other arithmetic: 9.93 us -> 4.66 us
    all_to_all x2 -> x0, waiting for transfers between devices: 163 us -> none  [the longest x1 163 us: local(): lax.all_to_all(outgoing.reshape(peers, per_peer, tile, width), 'dom', spl...]
    psum x1 -> x0, waiting for transfers between devices: 74.7 us -> none  [local(): total_s, total_n = lax.psum((term_s, term_n), 'dom')]
    ppermute x0 -> x38, starting transfers between devices: none -> 65.9 us  [swap(): return lax.ppermute(value, axis, [(i, i ^ bits) for i in range(size)])]
    ppermute x0 -> x38, waiting for transfers between devices: none -> 63 us  [swap(): return lax.ppermute(value, axis, [(i, i ^ bits) for i in range(size)])]
    reduce_scatter x2 -> x0, waiting for transfers between devices: 47.8 us -> none  [the longest x1 27.3 us: local(): lax.psum_scatter(total_s, 'cfg', scatter_dimension=0, tiled=True)]
    dot_general x7 -> x0, matrix products: 23.8 us -> none  [the longest x1 6.53 us: local(): jnp.einsum('es,etd->std', place, partial_value, preferred_element_type=jn...]
    pallas_call x0 -> x7, Pallas kernels: none -> 18.8 us  [the longest x2 11.2 us: run_head(): pl.pallas_call(functools.partial(head_kernel, peers, first, last), out_sh...]
    all_gather x2 -> x0, blocking collectives: 15.1 us -> none  [the longest x1 7.89 us: local(): lax.all_gather(w_neigh, 'cfg', axis=0, tiled=True)]
  transfers between devices with their start and end apart: 5 -> 38, of which waited for: 4 -> 18; matrix products, arithmetic and copies ran while one was open for 8% -> 3% of each run, Pallas kernels for 0% -> 8%
where the time goes in v1:
time: 168 us
  starting transfers between devices  65.9 us (39%)
  waiting for transfers between devices  63 us (38%)
  Pallas kernels  18.8 us (11%)
  local copies, waits for them, and re-layouts  14.5 us (9%)
  other arithmetic  4.66 us (3%)
    ppermute x38, starting transfers between devices, swap(): return lax.ppermute(value, axis, [(i, i ^ bits) for i in range(size)])  65.9 us
    ppermute x38, waiting for transfers between devices, swap(): return lax.ppermute(value, axis, [(i, i ^ bits) for i in range(size)])  63 us
    unnamed x38, local copies, waits for them, and re-layouts  12.6 us
    pallas_call x2, Pallas kernels, run_head(): pl.pallas_call(functools.partial(head_kernel, peers, first, last), out_sh...  11.2 us
    pallas_call x2, Pallas kernels, sum_edges(): pl.pallas_call(functools.partial(edges_kernel, slots, held is None, chunk...  5.29 us
  transfers between devices with their start and end apart: 38, of which 18 were waited for; matrix products, arithmetic and copies ran while one was open for 3% of the time, Pallas kernels for 8%

profile of v1, /device:TPU:0, one launch (start us, length us, event | category | flops | bytes accessed | tf_op | source)
XLA Modules:
  0.0 167.9 jit_solution(16385261816233085573)
XLA Ops:
  0.7 0.9 copy-done.3
  1.7 0.7 copy-done.4
  3.0 0.7 copy-done.6
  3.6 0.7 copy-done.7
  4.9 4.1 %collective-permute-start = (bf16[1,272,128]{2,1,0:T(8,128)(2,1)S(1)}, bf16[1,272,128]{2,1,0:T(8,128)(2,1)S(1)}, u32[]{:S(2)}, u32[]{:S(2)}) collective-permute-start(bf16[1,272,128]{2,1,0:T(8,128)(2,1)S(1)} %bitcast.34), channel_id=1, source_target_pairs={{0,4},{1,5},{2,6},{3,7},{4,0},{5,1},{6,2},{7,3},{8,12},{9,13},{10,... | collective-permute-start | bytes 208904 | tf_op jit(solution)/shard_map/ppermute | solution.py:18
  9.0 3.8 %collective-permute-done = bf16[1,272,128]{2,1,0:T(8,128)(2,1)S(1)} collective-permute-done((bf16[1,272,128]{2,1,0:T(8,128)(2,1)S(1)}, bf16[1,272,128]{2,1,0:T(8,128)(2,1)S(1)}, u32[]{:S(2)}, u32[]{:S(2)}) %collective-permute-start) | collective-permute-done | bytes 69664 | tf_op jit(solution)/shard_map/ppermute | solution.py:18
  12.8 0.7 collective-permute-start.1
  13.5 4.4 %collective-permute-done.1 = bf16[2,272,128]{2,1,0:T(8,128)(2,1)S(1)} collective-permute-done((bf16[2,272,128]{2,1,0:T(8,128)(2,1)S(1)}, bf16[2,272,128]{2,1,0:T(8,128)(2,1)S(1)}, u32[]{:S(2)}, u32[]{:S(2)}) %collective-permute-start.1) | collective-permute-done | bytes 139296 | tf_op jit(solution)/shard_map/ppermute | solution.py:18
  18.0 1.8 %collective-permute-start.2 = (bf16[4,272,128]{2,1,0:T(8,128)(2,1)S(1)}, bf16[4,272,128]{2,1,0:T(8,128)(2,1)S(1)}, u32[]{:S(2)}, u32[]{:S(2)}) collective-permute-start(bf16[4,272,128]{2,1,0:T(8,128)(2,1)S(1)} %pad_maximum_fusion.7), channel_id=1, source_target_pairs={{0,1},{1,0},{2,3},{3,2},{4,5},{5,4},{6,7},{7,6},{8,9},{9,8},{10,11... | collective-permute-start | bytes 835592 | tf_op jit(solution)/shard_map/ppermute | solution.py:18
  19.8 4.8 %collective-permute-done.2 = bf16[4,272,128]{2,1,0:T(8,128)(2,1)S(1)} collective-permute-done((bf16[4,272,128]{2,1,0:T(8,128)(2,1)S(1)}, bf16[4,272,128]{2,1,0:T(8,128)(2,1)S(1)}, u32[]{:S(2)}, u32[]{:S(2)}) %collective-permute-start.2) | collective-permute-done | bytes 278560 | tf_op jit(solution)/shard_map/ppermute | solution.py:18
  24.7 1.8 %collective-permute-start.7 = (bf16[1,8,256,128]{3,2,1,0:T(8,128)(2,1)S(1)}, bf16[1,8,256,128]{3,2,1,0:T(8,128)(2,1)S(1)}, u32[]{:S(2)}, u32[]{:S(2)}) collective-permute-start(bf16[1,8,256,128]{3,2,1,0:T(8,128)(2,1)S(1)} %fusion), channel_id=1, source_target_pairs={{0,16},{8,24},{16,0},{24,8},{1,17},{9,25},{17,1},{25,9},{2,18},{10... | collective-permute-start | bytes 1572872 | tf_op jit(solution)/shard_map/ppermute | solution.py:18
  26.5 8.3 %collective-permute-done.7 = bf16[1,8,256,128]{3,2,1,0:T(8,128)(2,1)S(1)} collective-permute-done((bf16[1,8,256,128]{3,2,1,0:T(8,128)(2,1)S(1)}, bf16[1,8,256,128]{3,2,1,0:T(8,128)(2,1)S(1)}, u32[]{:S(2)}, u32[]{:S(2)}) %collective-permute-start.7) | collective-permute-done | bytes 524320 | tf_op jit(solution)/shard_map/ppermute | solution.py:18
  34.9 1.6 collective-permute-start.19
  36.5 0.9 shard_map.113
  37.4 3.2 %collective-permute-start.10 = (bf16[64,1536]{1,0:T(8,128)(2,1)S(1)}, bf16[64,1536]{1,0:T(8,128)(2,1)S(1)}, u32[]{:S(2)}, u32[]{:S(2)}) collective-permute-start(bf16[64,1536]{1,0:T(8,128)(2,1)S(1)} %get-tuple-element.41), channel_id=1, source_target_pairs={{0,2},{1,3},{2,0},{3,1},{4,6},{5,7},{6,4},{7,5},{8,10},{9,11},{10,... | collective-permute-start | bytes 589832 | tf_op jit(solution)/shard_map/ppermute | solution.py:18
  40.6 1.0 collective-permute-start.11
  42.2 0.9 shard_map.112
  44.0 2.4 %collective-permute-done.10.refs_2_ = bf16[64,1536]{1,0:T(8,128)(2,1)S(1)} collective-permute-done((bf16[64,1536]{1,0:T(8,128)(2,1)S(1)}, bf16[64,1536]{1,0:T(8,128)(2,1)S(1)}, u32[]{:S(2)}, u32[]{:S(2)}) %collective-permute-start.10) | collective-permute-done | bytes 196640 | tf_op jit(solution)/shard_map/ppermute | solution.py:18
  46.4 4.6 %collective-permute-start.3 = (bf16[64,1536]{1,0:T(8,128)(2,1)S(1)}, bf16[64,1536]{1,0:T(8,128)(2,1)S(1)}, u32[]{:S(2)}, u32[]{:S(2)}) collective-permute-start(bf16[64,1536]{1,0:T(8,128)(2,1)S(1)} %get-tuple-element.35), channel_id=1, source_target_pairs={{0,4},{1,5},{2,6},{3,7},{4,0},{5,1},{6,2},{7,3},{8,12},{9,13},{10,... | collective-permute-start | bytes 589832 | tf_op jit(solution)/shard_map/ppermute | solution.py:18
  51.1 5.1 %collective-permute-start.4 = (bf16[64,1536]{1,0:T(8,128)(2,1)S(1)}, bf16[64,1536]{1,0:T(8,128)(2,1)S(1)}, u32[]{:S(2)}, u32[]{:S(2)}) collective-permute-start(bf16[64,1536]{1,0:T(8,128)(2,1)S(1)} %get-tuple-element.36), channel_id=1, source_target_pairs={{0,5},{1,4},{2,7},{3,6},{4,1},{5,0},{6,3},{7,2},{8,13},{9,12},{10,... | collective-permute-start | bytes 589832 | tf_op jit(solution)/shard_map/ppermute | solution.py:18
  56.2 1.3 collective-permute-start.5
  57.5 3.5 %collective-permute-start.6 = (bf16[64,1536]{1,0:T(8,128)(2,1)S(1)}, bf16[64,1536]{1,0:T(8,128)(2,1)S(1)}, u32[]{:S(2)}, u32[]{:S(2)}) collective-permute-start(bf16[64,1536]{1,0:T(8,128)(2,1)S(1)} %get-tuple-element.38), channel_id=1, source_target_pairs={{0,7},{1,6},{2,5},{3,4},{4,3},{5,2},{6,1},{7,0},{8,15},{9,14},{10,... | collective-permute-start | bytes 589832 | tf_op jit(solution)/shard_map/ppermute | solution.py:18
  61.2 2.2 %shard_map.114.refs_5_ = f32[96,64,128]{2,1,0:T(8,128)S(1)} custom-call(s32[2]{0:T(128)S(1)} %pad_add_fusion.1.at, s32[8,3,32]{2,1,0:T(4,128)S(1)} %pad_add_fusion.meta, bf16[64,1536]{1,0:T(8,128)(2,1)S(1)} %get-tuple-element.39.refs_0_, bf16[64,1536]{1,0:T(8,128)(2,1)S(1)} %collective-permute-done.9.refs_1_, ...), custom_call_target="tpu_custom_call" | custom-call | flops 268435456 | bytes 1835008 | tf_op jit(solution)/shard_map/pallas_call | solution.py:131
  63.4 10.2 %collective-permute-done.3.refs_0_ = bf16[64,1536]{1,0:T(8,128)(2,1)S(1)} collective-permute-done((bf16[64,1536]{1,0:T(8,128)(2,1)S(1)}, bf16[64,1536]{1,0:T(8,128)(2,1)S(1)}, u32[]{:S(2)}, u32[]{:S(2)}) %collective-permute-start.3) | collective-permute-done | bytes 196640 | tf_op jit(solution)/shard_map/ppermute | solution.py:18
  73.5 5.2 %collective-permute-done.4.refs_1_ = bf16[64,1536]{1,0:T(8,128)(2,1)S(1)} collective-permute-done((bf16[64,1536]{1,0:T(8,128)(2,1)S(1)}, bf16[64,1536]{1,0:T(8,128)(2,1)S(1)}, u32[]{:S(2)}, u32[]{:S(2)}) %collective-permute-start.4) | collective-permute-done | bytes 196640 | tf_op jit(solution)/shard_map/ppermute | solution.py:18
  78.8 3.1 %shard_map.115 = (bf16[64,768]{1,0:T(8,128)(2,1)S(1)}, bf16[64,768]{1,0:T(8,128)(2,1)S(1)}, bf16[64,768]{1,0:T(8,128)(2,1)S(1)}, bf16[64,768]{1,0:T(8,128)(2,1)S...) custom-call(s32[2]{0:T(128)S(1)} %pad_add_fusion.1.at, ...), custom_call_target="tpu_custom_call" | custom-call | flops 268435456 | bytes 1835008 | tf_op jit(solution)/shard_map/pallas_call | solution.py:131
  82.3 7.7 %collective-permute-start.22 = (bf16[64,768]{1,0:T(8,128)(2,1)S(1)}, bf16[64,768]{1,0:T(8,128)(2,1)S(1)}, u32[]{:S(2)}, u32[]{:S(2)}) collective-permute-start(bf16[64,768]{1,0:T(8,128)(2,1)S(1)} %get-tuple-element.53), channel_id=1, source_target_pairs={{0,2},{1,3},{2,0},{3,1},{4,6},{5,7},{6,4},{7,5},{8,10},{9,11},{10,... | collective-permute-start | bytes 294920 | tf_op jit(solution)/shard_map/ppermute | solution.py:18
  90.0 0.9 collective-permute-start.23
  90.9 3.8 %collective-permute-start.24 = (bf16[64,768]{1,0:T(8,128)(2,1)S(1)}, bf16[64,768]{1,0:T(8,128)(2,1)S(1)}, u32[]{:S(2)}, u32[]{:S(2)}) collective-permute-start(bf16[64,768]{1,0:T(8,128)(2,1)S(1)} %get-tuple-element.55), channel_id=1, source_target_pairs={{0,4},{1,5},{2,6},{3,7},{4,0},{5,1},{6,2},{7,3},{8,12},{9,13},{10,... | collective-permute-start | bytes 294920 | tf_op jit(solution)/shard_map/ppermute | solution.py:18
  95.5 2.3 %collective-permute-start.26 = (bf16[64,768]{1,0:T(8,128)(2,1)}, bf16[64,768]{1,0:T(8,128)(2,1)}, u32[]{:S(2)}, u32[]{:S(2)}) collective-permute-start(bf16[64,768]{1,0:T(8,128)(2,1)} %get-tuple-element.57), channel_id=1, source_target_pairs={{0,6},{1,7},{2,4},{3,5},{4,2},{5,3},{6,0},{7,1},{8,14},{9,15},{10,... | collective-permute-start | bytes 294920 | tf_op jit(solution)/shard_map/ppermute | solution.py:18
  98.5 2.4 %collective-permute-start.27 = (bf16[64,768]{1,0:T(8,128)(2,1)}, bf16[64,768]{1,0:T(8,128)(2,1)}, u32[]{:S(2)}, u32[]{:S(2)}) collective-permute-start(bf16[64,768]{1,0:T(8,128)(2,1)} %get-tuple-element.58), channel_id=1, source_target_pairs={{0,7},{1,6},{2,5},{3,4},{4,3},{5,2},{6,1},{7,0},{8,15},{9,14},{10,... | collective-permute-start | bytes 294920 | tf_op jit(solution)/shard_map/ppermute | solution.py:18
  102.1 3.1 %collective-permute-done.24.refs_4_ = bf16[64,768]{1,0:T(8,128)(2,1)S(1)} collective-permute-done((bf16[64,768]{1,0:T(8,128)(2,1)S(1)}, bf16[64,768]{1,0:T(8,128)(2,1)S(1)}, u32[]{:S(2)}, u32[]{:S(2)}) %collective-permute-start.24) | collective-permute-done | bytes 98336 | tf_op jit(solution)/shard_map/ppermute | solution.py:18
  105.8 0.7 collective-permute-start.13
  106.5 1.1 pad_maximum_fusion.2
  107.6 1.8 %gather_fusion = bf16[4,128,1024]{2,1,0:T(8,128)(2,1)S(1)} fusion(bf16[4,128,1024]{2,1,0:T(8,128)(2,1)} %pad_maximum_fusion.2, s32[1024]{0:T(1024)S(1)} %pad_clamp_fusion), kind=kCustom, calls=%fused_computation | custom fusion | bytes 2097168 | tf_op jit(solution)/shard_map/gather | solution.py:320
  109.6 3.5 %collective-permute-start.15 = (bf16[64,768]{1,0:T(8,128)(2,1)S(1)}, bf16[64,768]{1,0:T(8,128)(2,1)S(1)}, u32[]{:S(2)}, u32[]{:S(2)}) collective-permute-start(bf16[64,768]{1,0:T(8,128)(2,1)S(1)} %get-tuple-element.47), channel_id=1, source_target_pairs={{0,4},{1,5},{2,6},{3,7},{4,0},{5,1},{6,2},{7,3},{8,12},{9,13},{10,... | collective-permute-start | bytes 294920 | tf_op jit(solution)/shard_map/ppermute | solution.py:18
  113.1 2.4 %collective-permute-start.16 = (bf16[64,768]{1,0:T(8,128)(2,1)S(1)}, bf16[64,768]{1,0:T(8,128)(2,1)S(1)}, u32[]{:S(2)}, u32[]{:S(2)}) collective-permute-start(bf16[64,768]{1,0:T(8,128)(2,1)S(1)} %get-tuple-element.48), channel_id=1, source_target_pairs={{0,5},{1,4},{2,7},{3,6},{4,1},{5,0},{6,3},{7,2},{8,13},{9,12},{10,... | collective-permute-start | bytes 294920 | tf_op jit(solution)/shard_map/ppermute | solution.py:18
  115.5 2.7 %collective-permute-start.17 = (bf16[64,768]{1,0:T(8,128)(2,1)S(1)}, bf16[64,768]{1,0:T(8,128)(2,1)S(1)}, u32[]{:S(2)}, u32[]{:S(2)}) collective-permute-start(bf16[64,768]{1,0:T(8,128)(2,1)S(1)} %get-tuple-element.49), channel_id=1, source_target_pairs={{0,6},{1,7},{2,4},{3,5},{4,2},{5,3},{6,0},{7,1},{8,14},{9,15},{10,... | collective-permute-start | bytes 294920 | tf_op jit(solution)/shard_map/ppermute | solution.py:18
  118.2 1.3 collective-permute-start.18
  119.5 1.4 copy-done.1
  121.0 0.9 copy-done.10
  121.8 0.9 copy-done.12
  122.7 0.9 copy-done.14
  123.6 0.9 copy-done.16
  124.5 5.7 %shard_map.116 = (bf16[1536,512]{1,0:T(8,128)(2,1)}, f32[512,512]{1,0:T(8,128)S(1)}, f32[512,512]{1,0:T(8,128)S(1)}) custom-call(s32[2]{0:T(128)S(1)} %pad_add_fusion.1.at, bf16[64,768]{1,0:T(8,128)(2,1)S(1)} %get-tuple-element.51.refs_0_, bf16[64,768]{1,0:T(8,128)(2,1)S(1)} %copy-done.10, bf16[64,768]{1,0:T(8,128)(2,1)S(1)} %copy-done.12, ...), custom_call_target="tpu_custom_call" | custom-call | flops 1610612736 | bytes 3145728 | tf_op jit(solution)/shard_map/pallas_call | solution.py:223
  130.3 5.5 %shard_map.117 = (bf16[1536,512]{1,0:T(8,128)(2,1)}, f32[2,128,512]{2,1,0:T(8,128)S(1)}, f32[2,128,512]{2,1,0:T(8,128)S(1)}, bf16[2,128,512]{2,1,0:T(8,128)(2,1)S(1)}, bf16[2,128,512]{2,1,0:T(8,128)(2,1)}) custom-call(s32[2]{0:T(128)S(1)} %pad_add_fusion.1.at, bf16[64,768]{1,0:T(8,128)(2,1)S(1)} %get-tuple-element.43.refs_0_, ...), custom_call_target="tpu_custom_call", output_to_operand_aliasing={{0}: (12, {})} | custom-call | flops 1610612736 | bytes 3145728 | tf_op jit(solution)/shard_map/pallas_call | solution.py:223
  135.8 0.8 copy-done.2
  136.6 0.7 copy-done.8
  137.8 1.2 collective-permute-done.33
  139.0 1.1 convert_add_fusion
  140.2 2.2 %collective-permute-start.34 = (bf16[1,128,512]{2,1,0:T(8,128)(2,1)S(1)}, bf16[1,128,512]{2,1,0:T(8,128)(2,1)S(1)}, u32[]{:S(2)}, u32[]{:S(2)}) collective-permute-start(bf16[1,128,512]{2,1,0:T(8,128)(2,1)S(1)} %dynamic-slice_convert_fusion), channel_id=1, source_target_pairs={{0,16},{8,24},{16,0},{24,8},{1,17},{9,25},{17,1},{25,9},{2,18},{10... | collective-permute-start | bytes 393224 | tf_op jit(solution)/shard_map/ppermute | solution.py:18
  142.6 4.1 %collective-permute-done.34 = bf16[1,128,512]{2,1,0:T(8,128)(2,1)S(1)} collective-permute-done((bf16[1,128,512]{2,1,0:T(8,128)(2,1)S(1)}, bf16[1,128,512]{2,1,0:T(8,128)(2,1)S(1)}, u32[]{:S(2)}, u32[]{:S(2)}) %collective-permute-start.34) | collective-permute-done | bytes 131104 | tf_op jit(solution)/shard_map/ppermute | solution.py:18
  146.9 2.1 %collective-permute-done.29 = bf16[1,128,512]{2,1,0:T(8,128)(2,1)S(1)} collective-permute-done((bf16[1,128,512]{2,1,0:T(8,128)(2,1)S(1)}, bf16[1,128,512]{2,1,0:T(8,128)(2,1)S(1)}, u32[]{:S(2)}, u32[]{:S(2)}) %collective-permute-start.29) | collective-permute-done | bytes 131104 | tf_op jit(solution)/shard_map/ppermute | solution.py:18
  149.0 0.9 collective-permute-start.30
  150.0 1.8 %collective-permute-done.35 = bf16[128,512]{1,0:T(8,128)(2,1)S(1)} collective-permute-done((bf16[128,512]{1,0:T(8,128)(2,1)S(1)}, bf16[128,512]{1,0:T(8,128)(2,1)S(1)}, u32[]{:S(2)}, u32[]{:S(2)}) %collective-permute-start.35) | collective-permute-done | bytes 131104 | tf_op jit(solution)/shard_map/ppermute | solution.py:18
  151.9 1.1 collective-permute-start.36
  153.0 1.1 collective-permute-done.30
  154.1 1.0 collective-permute-start.31
  155.1 4.0 %collective-permute-done.36 = bf16[128,512]{1,0:T(8,128)(2,1)S(1)} collective-permute-done((bf16[128,512]{1,0:T(8,128)(2,1)S(1)}, bf16[128,512]{1,0:T(8,128)(2,1)S(1)}, u32[]{:S(2)}, u32[]{:S(2)}) %collective-permute-start.36) | collective-permute-done | bytes 131104 | tf_op jit(solution)/shard_map/ppermute | solution.py:18
  159.1 1.3 collective-permute-start.37
  160.8 3.3 %collective-permute-done.37 = bf16[128,512]{1,0:T(8,128)(2,1)S(1)} collective-permute-done((bf16[128,512]{1,0:T(8,128)(2,1)S(1)}, bf16[128,512]{1,0:T(8,128)(2,1)S(1)}, u32[]{:S(2)}, u32[]{:S(2)}) %collective-permute-start.37) | collective-permute-done | bytes 131104 | tf_op jit(solution)/shard_map/ppermute | solution.py:18
  164.2 0.8 add_multiply_fusion
  164.9 2.2 %collective-permute-done.32 = bf16[128,512]{1,0:T(8,128)(2,1)S(1)} collective-permute-done((bf16[128,512]{1,0:T(8,128)(2,1)S(1)}, bf16[128,512]{1,0:T(8,128)(2,1)S(1)}, u32[]{:S(2)}, u32[]{:S(2)}) %collective-permute-start.32) | collective-permute-done | bytes 131104 | tf_op jit(solution)/shard_map/ppermute | solution.py:18
  167.1 0.8 add_multiply_fusion.1
  (84 shorter events, 8.6 us)
Async XLA Ops:
  0.7 1.0 copy-start.3
  1.7 0.7 copy-start.4
  2.3 0.7 copy-start.5
  3.0 0.7 copy-start.6
  3.6 0.7 copy-start.7
  4.3 30.6 %copy-start.17 = (bf16[128,512]{1,0:T(8,128)(2,1)S(1)}, bf16[128,512]{1,0:T(8,128)(2,1)}, u32[]{:S(2)}) copy-start(bf16[128,512]{1,0:T(8,128)(2,1)} %param.12) | copy-start | bytes 393220
  4.3 30.6 %copy-start.18 = (bf16[128,512]{1,0:T(8,128)(2,1)S(1)}, bf16[128,512]{1,0:T(8,128)(2,1)}, u32[]{:S(2)}) copy-start(bf16[128,512]{1,0:T(8,128)(2,1)} %param.11) | copy-start | bytes 393220
  4.9 7.9 %collective-permute-start = (bf16[1,272,128]{2,1,0:T(8,128)(2,1)S(1)}, bf16[1,272,128]{2,1,0:T(8,128)(2,1)S(1)}, u32[]{:S(2)}, u32[]{:S(2)}) collective-permute-start(bf16[1,272,128]{2,1,0:T(8,128)(2,1)S(1)} %bitcast.34), channel_id=1, source_target_pairs={{0,4},{1,5},{2,6},{3,7},{4,0},{5,1},{6,2},{7,3},{8,12},{9,13},{10,... | collective-permute-start | bytes 208904 | tf_op jit(solution)/shard_map/ppermute | solution.py:18
  12.8 23.7 %copy-start = (bf16[1,1536,512]{2,1,0:T(8,128)(2,1)S(1)}, bf16[1,1536,512]{2,1,0:T(8,128)(2,1)}, u32[]{:S(2)}) copy-start(bf16[1,1536,512]{2,1,0:T(8,128)(2,1)} %param.9) | copy-start | bytes 4718596
  12.8 5.1 %collective-permute-start.1 = (bf16[2,272,128]{2,1,0:T(8,128)(2,1)S(1)}, bf16[2,272,128]{2,1,0:T(8,128)(2,1)S(1)}, u32[]{:S(2)}, u32[]{:S(2)}) collective-permute-start(bf16[2,272,128]{2,1,0:T(8,128)(2,1)S(1)} %pad_maximum_fusion.8), channel_id=1, source_target_pairs={{0,2},{1,3},{2,0},{3,1},{4,6},{5,7},{6,4},{7,5},{8,10},{9,11},{10,... | collective-permute-start | bytes 417800 | tf_op jit(solution)/shard_map/ppermute | solution.py:18
  18.0 6.6 %collective-permute-start.2 = (bf16[4,272,128]{2,1,0:T(8,128)(2,1)S(1)}, bf16[4,272,128]{2,1,0:T(8,128)(2,1)S(1)}, u32[]{:S(2)}, u32[]{:S(2)}) collective-permute-start(bf16[4,272,128]{2,1,0:T(8,128)(2,1)S(1)} %pad_maximum_fusion.7), channel_id=1, source_target_pairs={{0,1},{1,0},{2,3},{3,2},{4,5},{5,4},{6,7},{7,6},{8,9},{9,8},{10,11... | collective-permute-start | bytes 835592 | tf_op jit(solution)/shard_map/ppermute | solution.py:18
  24.7 10.1 %collective-permute-start.7 = (bf16[1,8,256,128]{3,2,1,0:T(8,128)(2,1)S(1)}, bf16[1,8,256,128]{3,2,1,0:T(8,128)(2,1)S(1)}, u32[]{:S(2)}, u32[]{:S(2)}) collective-permute-start(bf16[1,8,256,128]{3,2,1,0:T(8,128)(2,1)S(1)} %fusion), channel_id=1, source_target_pairs={{0,16},{8,24},{16,0},{24,8},{1,17},{9,25},{17,1},{25,9},{2,18},{10... | collective-permute-start | bytes 1572872 | tf_op jit(solution)/shard_map/ppermute | solution.py:18
  34.8 22.7 %collective-permute-start.8 = (bf16[2,8,256,128]{3,2,1,0:T(8,128)(2,1)S(1)}, bf16[2,8,256,128]{3,2,1,0:T(8,128)(2,1)S(1)}, u32[]{:S(2)}, u32[]{:S(2)}) collective-permute-start(bf16[2,8,256,128]{3,2,1,0:T(8,128)(2,1)S(1)} %pad_maximum_fusion.1), channel_id=1, source_target_pairs={{0,8},{8,0},{16,24},{24,16},{1,9},{9,1},{17,25},{25,17},{2,10},{10... | collective-permute-start | bytes 3145736 | tf_op jit(solution)/shard_map/ppermute | solution.py:18
  34.9 8.8 %collective-permute-start.19 = (bf16[1,128,1024]{2,1,0:T(8,128)(2,1)S(1)}, bf16[1,128,1024]{2,1,0:T(8,128)(2,1)S(1)}, u32[]{:S(2)}, u32[]{:S(2)}) collective-permute-start(bf16[1,128,1024]{2,1,0:T(8,128)(2,1)S(1)} %maximum_bitcast_fusion), channel_id=1, source_target_pairs={{0,16},{8,24},{16,0},{24,8},{1,17},{9,25},{17,1},{25,9},{2,18},{10... | collective-permute-start | bytes 786440 | tf_op jit(solution)/shard_map/ppermute | solution.py:18
  37.4 9.0 %collective-permute-start.10 = (bf16[64,1536]{1,0:T(8,128)(2,1)S(1)}, bf16[64,1536]{1,0:T(8,128)(2,1)S(1)}, u32[]{:S(2)}, u32[]{:S(2)}) collective-permute-start(bf16[64,1536]{1,0:T(8,128)(2,1)S(1)} %get-tuple-element.41), channel_id=1, source_target_pairs={{0,2},{1,3},{2,0},{3,1},{4,6},{5,7},{6,4},{7,5},{8,10},{9,11},{10,... | collective-permute-start | bytes 589832 | tf_op jit(solution)/shard_map/ppermute | solution.py:18
  40.6 10.5 %collective-permute-start.11 = (bf16[64,1536]{1,0:T(8,128)(2,1)S(1)}, bf16[64,1536]{1,0:T(8,128)(2,1)S(1)}, u32[]{:S(2)}, u32[]{:S(2)}) collective-permute-start(bf16[64,1536]{1,0:T(8,128)(2,1)S(1)} %get-tuple-element.42), channel_id=1, source_target_pairs={{0,3},{1,2},{2,1},{3,0},{4,7},{5,6},{6,5},{7,4},{8,11},{9,10},{10,... | collective-permute-start | bytes 589832 | tf_op jit(solution)/shard_map/ppermute | solution.py:18
  41.6 14.6 %collective-permute-start.9 = (bf16[64,1536]{1,0:T(8,128)(2,1)S(1)}, bf16[64,1536]{1,0:T(8,128)(2,1)S(1)}, u32[]{:S(2)}, u32[]{:S(2)}) collective-permute-start(bf16[64,1536]{1,0:T(8,128)(2,1)S(1)} %get-tuple-element.40), channel_id=1, source_target_pairs={{0,1},{1,0},{2,3},{3,2},{4,5},{5,4},{6,7},{7,6},{8,9},{9,8},{10,11... | collective-permute-start | bytes 589832 | tf_op jit(solution)/shard_map/ppermute | solution.py:18
  43.8 51.0 %collective-permute-start.20 = (bf16[2,128,1024]{2,1,0:T(8,128)(2,1)S(1)}, bf16[2,128,1024]{2,1,0:T(8,128)(2,1)S(1)}, u32[]{:S(2)}, u32[]{:S(2)}) collective-permute-start(bf16[2,128,1024]{2,1,0:T(8,128)(2,1)S(1)} %pad_maximum_fusion.6), channel_id=1, source_target_pairs={{0,8},{8,0},{16,24},{24,16},{1,9},{9,1},{17,25},{25,17},{2,10},{10... | collective-permute-start | bytes 1572872 | tf_op jit(solution)/shard_map/ppermute | solution.py:18
  46.4 27.2 %collective-permute-start.3 = (bf16[64,1536]{1,0:T(8,128)(2,1)S(1)}, bf16[64,1536]{1,0:T(8,128)(2,1)S(1)}, u32[]{:S(2)}, u32[]{:S(2)}) collective-permute-start(bf16[64,1536]{1,0:T(8,128)(2,1)S(1)} %get-tuple-element.35), channel_id=1, source_target_pairs={{0,4},{1,5},{2,6},{3,7},{4,0},{5,1},{6,2},{7,3},{8,12},{9,13},{10,... | collective-permute-start | bytes 589832 | tf_op jit(solution)/shard_map/ppermute | solution.py:18
  51.1 27.6 %collective-permute-start.4 = (bf16[64,1536]{1,0:T(8,128)(2,1)S(1)}, bf16[64,1536]{1,0:T(8,128)(2,1)S(1)}, u32[]{:S(2)}, u32[]{:S(2)}) collective-permute-start(bf16[64,1536]{1,0:T(8,128)(2,1)S(1)} %get-tuple-element.36), channel_id=1, source_target_pairs={{0,5},{1,4},{2,7},{3,6},{4,1},{5,0},{6,3},{7,2},{8,13},{9,12},{10,... | collective-permute-start | bytes 589832 | tf_op jit(solution)/shard_map/ppermute | solution.py:18
  56.2 22.6 %collective-permute-start.5 = (bf16[64,1536]{1,0:T(8,128)(2,1)S(1)}, bf16[64,1536]{1,0:T(8,128)(2,1)S(1)}, u32[]{:S(2)}, u32[]{:S(2)}) collective-permute-start(bf16[64,1536]{1,0:T(8,128)(2,1)S(1)} %get-tuple-element.37), channel_id=1, source_target_pairs={{0,6},{1,7},{2,4},{3,5},{4,2},{5,3},{6,0},{7,1},{8,14},{9,15},{10,... | collective-permute-start | bytes 589832 | tf_op jit(solution)/shard_map/ppermute | solution.py:18
  57.5 21.3 %collective-permute-start.6 = (bf16[64,1536]{1,0:T(8,128)(2,1)S(1)}, bf16[64,1536]{1,0:T(8,128)(2,1)S(1)}, u32[]{:S(2)}, u32[]{:S(2)}) collective-permute-start(bf16[64,1536]{1,0:T(8,128)(2,1)S(1)} %get-tuple-element.38), channel_id=1, source_target_pairs={{0,7},{1,6},{2,5},{3,4},{4,3},{5,2},{6,1},{7,0},{8,15},{9,14},{10,... | collective-permute-start | bytes 589832 | tf_op jit(solution)/shard_map/ppermute | solution.py:18
  81.9 12.9 %collective-permute-start.21 = (bf16[64,768]{1,0:T(8,128)(2,1)S(1)}, bf16[64,768]{1,0:T(8,128)(2,1)S(1)}, u32[]{:S(2)}, u32[]{:S(2)}) collective-permute-start(bf16[64,768]{1,0:T(8,128)(2,1)S(1)} %get-tuple-element.52), channel_id=1, source_target_pairs={{0,1},{1,0},{2,3},{3,2},{4,5},{5,4},{6,7},{7,6},{8,9},{9,8},{10,11... | collective-permute-start | bytes 294920 | tf_op jit(solution)/shard_map/ppermute | solution.py:18
  82.3 15.5 %collective-permute-start.22 = (bf16[64,768]{1,0:T(8,128)(2,1)S(1)}, bf16[64,768]{1,0:T(8,128)(2,1)S(1)}, u32[]{:S(2)}, u32[]{:S(2)}) collective-permute-start(bf16[64,768]{1,0:T(8,128)(2,1)S(1)} %get-tuple-element.53), channel_id=1, source_target_pairs={{0,2},{1,3},{2,0},{3,1},{4,6},{5,7},{6,4},{7,5},{8,10},{9,11},{10,... | collective-permute-start | bytes 294920 | tf_op jit(solution)/shard_map/ppermute | solution.py:18
  90.0 10.9 %collective-permute-start.23 = (bf16[64,768]{1,0:T(8,128)(2,1)S(1)}, bf16[64,768]{1,0:T(8,128)(2,1)S(1)}, u32[]{:S(2)}, u32[]{:S(2)}) collective-permute-start(bf16[64,768]{1,0:T(8,128)(2,1)S(1)} %get-tuple-element.54), channel_id=1, source_target_pairs={{0,3},{1,2},{2,1},{3,0},{4,7},{5,6},{6,5},{7,4},{8,11},{9,10},{10,... | collective-permute-start | bytes 294920 | tf_op jit(solution)/shard_map/ppermute | solution.py:18
  90.9 14.2 %collective-permute-start.24 = (bf16[64,768]{1,0:T(8,128)(2,1)S(1)}, bf16[64,768]{1,0:T(8,128)(2,1)S(1)}, u32[]{:S(2)}, u32[]{:S(2)}) collective-permute-start(bf16[64,768]{1,0:T(8,128)(2,1)S(1)} %get-tuple-element.55), channel_id=1, source_target_pairs={{0,4},{1,5},{2,6},{3,7},{4,0},{5,1},{6,2},{7,3},{8,12},{9,13},{10,... | collective-permute-start | bytes 294920 | tf_op jit(solution)/shard_map/ppermute | solution.py:18
  94.8 14.7 %collective-permute-start.25 = (bf16[64,768]{1,0:T(8,128)(2,1)}, bf16[64,768]{1,0:T(8,128)(2,1)}, u32[]{:S(2)}, u32[]{:S(2)}) collective-permute-start(bf16[64,768]{1,0:T(8,128)(2,1)} %get-tuple-element.56), channel_id=1, source_target_pairs={{0,5},{1,4},{2,7},{3,6},{4,1},{5,0},{6,3},{7,2},{8,13},{9,12},{10,... | collective-permute-start | bytes 294920 | tf_op jit(solution)/shard_map/ppermute | solution.py:18
  94.9 0.6 copy-start.9
  95.5 14.1 %collective-permute-start.26 = (bf16[64,768]{1,0:T(8,128)(2,1)}, bf16[64,768]{1,0:T(8,128)(2,1)}, u32[]{:S(2)}, u32[]{:S(2)}) collective-permute-start(bf16[64,768]{1,0:T(8,128)(2,1)} %get-tuple-element.57), channel_id=1, source_target_pairs={{0,6},{1,7},{2,4},{3,5},{4,2},{5,3},{6,0},{7,1},{8,14},{9,15},{10,... | collective-permute-start | bytes 294920 | tf_op jit(solution)/shard_map/ppermute | solution.py:18
  97.8 0.7 copy-start.11
  98.5 14.6 %collective-permute-start.27 = (bf16[64,768]{1,0:T(8,128)(2,1)}, bf16[64,768]{1,0:T(8,128)(2,1)}, u32[]{:S(2)}, u32[]{:S(2)}) collective-permute-start(bf16[64,768]{1,0:T(8,128)(2,1)} %get-tuple-element.58), channel_id=1, source_target_pairs={{0,7},{1,6},{2,5},{3,4},{4,3},{5,2},{6,1},{7,0},{8,15},{9,14},{10,... | collective-permute-start | bytes 294920 | tf_op jit(solution)/shard_map/ppermute | solution.py:18
  100.9 0.6 copy-start.13
  101.5 14.0 %collective-permute-start.12 = (bf16[64,768]{1,0:T(8,128)(2,1)}, bf16[64,768]{1,0:T(8,128)(2,1)S(1)}, u32[]{:S(2)}, u32[]{:S(2)}) collective-permute-start(bf16[64,768]{1,0:T(8,128)(2,1)} %get-tuple-element.44), channel_id=1, source_target_pairs={{0,1},{1,0},{2,3},{3,2},{4,5},{5,4},{6,7},{7,6},{8,9},{9,8},{10,11... | collective-permute-start | bytes 294920 | tf_op jit(solution)/shard_map/ppermute | solution.py:18
  105.2 0.6 copy-start.15
  105.8 12.4 %collective-permute-start.13 = (bf16[64,768]{1,0:T(8,128)(2,1)}, bf16[64,768]{1,0:T(8,128)(2,1)S(1)}, u32[]{:S(2)}, u32[]{:S(2)}) collective-permute-start(bf16[64,768]{1,0:T(8,128)(2,1)} %get-tuple-element.45), channel_id=1, source_target_pairs={{0,2},{1,3},{2,0},{3,1},{4,6},{5,7},{6,4},{7,5},{8,10},{9,11},{10,... | collective-permute-start | bytes 294920 | tf_op jit(solution)/shard_map/ppermute | solution.py:18
  109.5 20.8 %collective-permute-start.14 = (bf16[64,768]{1,0:T(8,128)(2,1)S(1)}, bf16[64,768]{1,0:T(8,128)(2,1)S(1)}, u32[]{:S(2)}, u32[]{:S(2)}) collective-permute-start(bf16[64,768]{1,0:T(8,128)(2,1)S(1)} %get-tuple-element.46), channel_id=1, source_target_pairs={{0,3},{1,2},{2,1},{3,0},{4,7},{5,6},{6,5},{7,4},{8,11},{9,10},{10,... | collective-permute-start | bytes 294920 | tf_op jit(solution)/shard_map/ppermute | solution.py:18
  109.6 20.7 %collective-permute-start.15 = (bf16[64,768]{1,0:T(8,128)(2,1)S(1)}, bf16[64,768]{1,0:T(8,128)(2,1)S(1)}, u32[]{:S(2)}, u32[]{:S(2)}) collective-permute-start(bf16[64,768]{1,0:T(8,128)(2,1)S(1)} %get-tuple-element.47), channel_id=1, source_target_pairs={{0,4},{1,5},{2,6},{3,7},{4,0},{5,1},{6,2},{7,3},{8,12},{9,13},{10,... | collective-permute-start | bytes 294920 | tf_op jit(solution)/shard_map/ppermute | solution.py:18
  113.1 17.2 %collective-permute-start.16 = (bf16[64,768]{1,0:T(8,128)(2,1)S(1)}, bf16[64,768]{1,0:T(8,128)(2,1)S(1)}, u32[]{:S(2)}, u32[]{:S(2)}) collective-permute-start(bf16[64,768]{1,0:T(8,128)(2,1)S(1)} %get-tuple-element.48), channel_id=1, source_target_pairs={{0,5},{1,4},{2,7},{3,6},{4,1},{5,0},{6,3},{7,2},{8,13},{9,12},{10,... | collective-permute-start | bytes 294920 | tf_op jit(solution)/shard_map/ppermute | solution.py:18
  115.5 14.7 %collective-permute-start.17 = (bf16[64,768]{1,0:T(8,128)(2,1)S(1)}, bf16[64,768]{1,0:T(8,128)(2,1)S(1)}, u32[]{:S(2)}, u32[]{:S(2)}) collective-permute-start(bf16[64,768]{1,0:T(8,128)(2,1)S(1)} %get-tuple-element.49), channel_id=1, source_target_pairs={{0,6},{1,7},{2,4},{3,5},{4,2},{5,3},{6,0},{7,1},{8,14},{9,15},{10,... | collective-permute-start | bytes 294920 | tf_op jit(solution)/shard_map/ppermute | solution.py:18
  118.2 12.0 %collective-permute-start.18 = (bf16[64,768]{1,0:T(8,128)(2,1)S(1)}, bf16[64,768]{1,0:T(8,128)(2,1)S(1)}, u32[]{:S(2)}, u32[]{:S(2)}) collective-permute-start(bf16[64,768]{1,0:T(8,128)(2,1)S(1)} %get-tuple-element.50), channel_id=1, source_target_pairs={{0,7},{1,6},{2,5},{3,4},{4,3},{5,2},{6,1},{7,0},{8,15},{9,14},{10,... | collective-permute-start | bytes 294920 | tf_op jit(solution)/shard_map/ppermute | solution.py:18
  119.5 1.4 copy-start.1
  120.9 0.9 copy-start.10
  121.8 0.9 copy-start.12
  122.7 0.9 copy-start.14
  123.6 0.9 copy-start.16
  135.8 0.8 copy-start.2
  136.6 0.7 copy-start.8
  137.3 1.7 %collective-permute-start.33 = (bf16[2,128,512]{2,1,0:T(8,128)(2,1)}, bf16[2,128,512]{2,1,0:T(8,128)(2,1)S(1)}, u32[]{:S(2)}, u32[]{:S(2)}) collective-permute-start(bf16[2,128,512]{2,1,0:T(8,128)(2,1)} %get-tuple-element.66), channel_id=1, source_target_pairs={{0,8},{8,0},{16,24},{24,16},{1,9},{9,1},{17,25},{25,17},{2,10},{10... | collective-permute-start | bytes 786440 | tf_op jit(solution)/shard_map/ppermute | solution.py:18
  137.3 5.1 %collective-permute-start.28 = (bf16[2,128,512]{2,1,0:T(8,128)(2,1)}, bf16[2,128,512]{2,1,0:T(8,128)(2,1)S(1)}, u32[]{:S(2)}, u32[]{:S(2)}) collective-permute-start(bf16[2,128,512]{2,1,0:T(8,128)(2,1)} %copy-done.8), channel_id=1, source_target_pairs={{0,8},{8,0},{16,24},{24,16},{1,9},{9,1},{17,25},{25,17},{2,10},{10... | collective-permute-start | bytes 786440 | tf_op jit(solution)/shard_map/ppermute | solution.py:18
  140.2 6.6 %collective-permute-start.34 = (bf16[1,128,512]{2,1,0:T(8,128)(2,1)S(1)}, bf16[1,128,512]{2,1,0:T(8,128)(2,1)S(1)}, u32[]{:S(2)}, u32[]{:S(2)}) collective-permute-start(bf16[1,128,512]{2,1,0:T(8,128)(2,1)S(1)} %dynamic-slice_convert_fusion), channel_id=1, source_target_pairs={{0,16},{8,24},{16,0},{24,8},{1,17},{9,25},{17,1},{25,9},{2,18},{10... | collective-permute-start | bytes 393224 | tf_op jit(solution)/shard_map/ppermute | solution.py:18
  142.5 6.5 %collective-permute-start.29 = (bf16[1,128,512]{2,1,0:T(8,128)(2,1)S(1)}, bf16[1,128,512]{2,1,0:T(8,128)(2,1)S(1)}, u32[]{:S(2)}, u32[]{:S(2)}) collective-permute-start(bf16[1,128,512]{2,1,0:T(8,128)(2,1)S(1)} %dynamic-slice_convert_fusion.1), channel_id=1, source_target_pairs={{0,16},{8,24},{16,0},{24,8},{1,17},{9,25},{17,1},{25,9},{2,18},{10... | collective-permute-start | bytes 393224 | tf_op jit(solution)/shard_map/ppermute | solution.py:18
  146.8 5.0 %collective-permute-start.35 = (bf16[128,512]{1,0:T(8,128)(2,1)S(1)}, bf16[128,512]{1,0:T(8,128)(2,1)S(1)}, u32[]{:S(2)}, u32[]{:S(2)}) collective-permute-start(bf16[128,512]{1,0:T(8,128)(2,1)S(1)} %bitcast_convert_fusion), channel_id=1, source_target_pairs={{0,2},{1,3},{2,0},{3,1},{4,6},{5,7},{6,4},{7,5},{8,10},{9,11},{10,... | collective-permute-start | bytes 393224 | tf_op jit(solution)/shard_map/ppermute | solution.py:18
  149.0 5.0 %collective-permute-start.30 = (bf16[128,512]{1,0:T(8,128)(2,1)S(1)}, bf16[128,512]{1,0:T(8,128)(2,1)S(1)}, u32[]{:S(2)}, u32[]{:S(2)}) collective-permute-start(bf16[128,512]{1,0:T(8,128)(2,1)S(1)} %bitcast_convert_fusion.1), channel_id=1, source_target_pairs={{0,1},{1,0},{2,3},{3,2},{4,5},{5,4},{6,7},{7,6},{8,9},{9,8},{10,11... | collective-permute-start | bytes 393224 | tf_op jit(solution)/shard_map/ppermute | solution.py:18
  151.9 7.2 %collective-permute-start.36 = (bf16[128,512]{1,0:T(8,128)(2,1)S(1)}, bf16[128,512]{1,0:T(8,128)(2,1)S(1)}, u32[]{:S(2)}, u32[]{:S(2)}) collective-permute-start(bf16[128,512]{1,0:T(8,128)(2,1)S(1)} %get-tuple-element.67), channel_id=1, source_target_pairs={{0,4},{1,5},{2,6},{3,7},{4,0},{5,1},{6,2},{7,3},{8,12},{9,13},{10,... | collective-permute-start | bytes 393224 | tf_op jit(solution)/shard_map/ppermute | solution.py:18
  154.1 6.3 %collective-permute-start.31 = (bf16[128,512]{1,0:T(8,128)(2,1)S(1)}, bf16[128,512]{1,0:T(8,128)(2,1)S(1)}, u32[]{:S(2)}, u32[]{:S(2)}) collective-permute-start(bf16[128,512]{1,0:T(8,128)(2,1)S(1)} %get-tuple-element.69), channel_id=1, source_target_pairs={{0,2},{1,3},{2,0},{3,1},{4,6},{5,7},{6,4},{7,5},{8,10},{9,11},{10,... | collective-permute-start | bytes 393224 | tf_op jit(solution)/shard_map/ppermute | solution.py:18
  159.1 5.0 %collective-permute-start.37 = (bf16[128,512]{1,0:T(8,128)(2,1)S(1)}, bf16[128,512]{1,0:T(8,128)(2,1)S(1)}, u32[]{:S(2)}, u32[]{:S(2)}) collective-permute-start(bf16[128,512]{1,0:T(8,128)(2,1)S(1)} %fusion.2), channel_id=1, source_target_pairs={{0,1},{1,0},{2,3},{3,2},{4,5},{5,4},{6,7},{7,6},{8,9},{9,8},{10,11... | collective-permute-start | bytes 393224 | tf_op jit(solution)/shard_map/ppermute | solution.py:18
  160.5 6.7 %collective-permute-start.32 = (bf16[128,512]{1,0:T(8,128)(2,1)S(1)}, bf16[128,512]{1,0:T(8,128)(2,1)S(1)}, u32[]{:S(2)}, u32[]{:S(2)}) collective-permute-start(bf16[128,512]{1,0:T(8,128)(2,1)S(1)} %fusion.1), channel_id=1, source_target_pairs={{0,4},{1,5},{2,6},{3,7},{4,0},{5,1},{6,2},{7,3},{8,12},{9,13},{10,... | collective-permute-start | bytes 393224 | tf_op jit(solution)/shard_map/ppermute | solution.py:18

commit v2 on v1

--- a/solution.py
+++ b/solution.py
@@ -10,6 +10,7 @@
 
 BF16, F32, I32 = jnp.bfloat16, jnp.float32, jnp.int32
 WHOLE = pl.BlockSpec(memory_space=pltpu.VMEM)
+STAYS = pl.BlockSpec(memory_space=pltpu.HBM)
 LANES = 128
 
 
@@ -24,20 +25,28 @@
     return [1 << k for k in range(size.bit_length() - 1)]
 
 
-def pack_kernel(at, tiles_ref, peer_ref, src_ref, dst_ref, tile_ref, packed_ref, turned_ref, info_ref):
-    count, tile, _ = tiles_ref.shape
+def pack_kernel(at, tiles_hbm, peer, src, dst, name, packed_ref, tiles_ref, turned_ref, lists_ref, info_ref, sem):
+    per, tile, _ = tiles_ref.shape
     piece = packed_ref.shape[0] - info_ref.shape[0]
-    edges = src_ref.shape[1]
-    if piece % tile == 0:
-        for i in range(piece // tile):
-            packed_ref[i * tile : (i + 1) * tile] = tiles_ref[at[1] * (piece // tile) + i].T
+    edges = src.shape[1]
+    first = at[1] * per if per < tiles_hbm.shape[0] else 0
+    fetches = [pltpu.make_async_copy(tiles_hbm.at[pl.ds(first, per)], tiles_ref, sem.at[0])]
+    for row, ref in enumerate((peer, src, dst, name)):
+        fetches.append(pltpu.make_async_copy(ref, lists_ref.at[row], sem.at[1 + row]))
+    for fetch in fetches:
+        fetch.start()
+    info_ref[...] = jnp.zeros_like(info_ref)
+    for fetch in fetches:
+        fetch.wait()
+    if per < tiles_hbm.shape[0]:
+        for i in range(per):
+            packed_ref[i * tile : (i + 1) * tile] = tiles_ref[i].T
     else:
-        for i in range(count):
+        for i in range(per):
             turned_ref[i * tile : (i + 1) * tile] = tiles_ref[i].T
         packed_ref[:piece] = turned_ref[pl.ds(pl.multiple_of(at[1] * piece, piece), piece)]
-    info_ref[...] = jnp.zeros_like(info_ref)
-    for row, ref in enumerate((peer_ref, src_ref, dst_ref, tile_ref)):
-        info_ref[row : row + 1, :edges] = ref[...].astype(F32)
+    for row in range(4):
+        info_ref[row : row + 1, :edges] = lists_ref[row].astype(F32)
     packed_ref[piece:] = info_ref[...].astype(BF16)
 
 
@@ -147,97 +156,134 @@
     )(at, meta, *operands)
 
 
-def head_kernel(peers, first, last, at, *refs):
+def head_kernel(peers, base, first, last, at, *refs):
     a_refs = refs[:peers]
     feats_ref, cot_ref, weights_ref = refs[peers : peers + 3]
     refs = refs[peers + 3 :]
     if not first:
-        held_s, held_n = refs[1:3]
+        held = refs[1:3]
         refs = refs[3:]
+    count = 5 if last else 3
+    out_ref, *sum_refs = refs[:count]
+    agg_ref, x_ref, c_ref, w_ref, pre_ref, made_ref, grad_ref, *refs = refs[count:]
+    totals, in_sem, out_sem = refs[:2], refs[2], refs[3]
     if last:
-        out_ref, keep_s, keep_n, give_s, give_n, agg_ref, sum_s, sum_n = refs
-    else:
-        out_ref, sum_s, sum_n, agg_ref = refs
-    width = feats_ref.shape[1]
-    step = feats_ref.shape[0]
-    i = pl.program_id(0)
-
-    @pl.when(i == 0)
-    def _():
-        part = width // peers
-        for k in range(peers):
-            agg_ref[pl.ds(pl.multiple_of((at[0] ^ k) * part, part), part)] = a_refs[k][...]
-        sum_s[...] = jnp.zeros_like(sum_s) if first else held_s[...]
-        sum_n[...] = jnp.zeros_like(sum_n) if first else held_n[...]
-
-    feats = feats_ref[...]
-    agg = agg_ref[:, pl.ds(pl.multiple_of(i * step, step), step)]
+        gives = refs[4:6]
+    width, span = agg_ref.shape
+    part = width // peers
+    step = 256 if span % 256 == 0 else 128
+    stores = []
+
+    def fetch(source, place, slot):
+        copy = pltpu.make_async_copy(source, place, in_sem.at[slot])
+        copy.start()
+        return copy
+
+    def store(source, place):
+        copy = pltpu.make_async_copy(source, place, out_sem.at[len(stores)])
+        copy.start()
+        stores.append(copy)
+
+    own_rows = pl.ds(base, span)
+    early = [fetch(feats_ref.at[own_rows], x_ref, peers), fetch(weights_ref, w_ref, peers + 1)]
+    parts = []
+    for k in range(peers):
+        place = agg_ref.at[pl.ds(pl.multiple_of((at[0] ^ k) * part, part), part)]
+        parts.append(fetch(a_refs[k], place, k))
+    parts.append(fetch(cot_ref.at[own_rows], c_ref, peers + 2))
+    late = []
+    if not first:
+        late = [fetch(ref, total, peers + 3 + i) for i, (ref, total) in enumerate(zip(held, totals))]
+    for copy in early:
+        copy.wait()
+    pre_ref[...] = jnp.dot(x_ref[...], w_ref[:, :width], preferred_element_type=F32)
+    for copy in parts:
+        copy.wait()
+
     over_rows = (((0,), (0,)), ((), ()))
-    pre = jnp.dot(feats, weights_ref[:, :width], preferred_element_type=F32)
-    pre += lax.dot_general(agg, weights_ref[:, width:], over_rows, preferred_element_type=F32)
-    scale = lax.rsqrt(jnp.mean(pre * pre, -1, keepdims=True) + 1e-05)
-    normed = pre * scale
-    gate = jax.nn.sigmoid(normed)
-    out_ref[...] = (normed * gate).astype(BF16)
-    slope = cot_ref[...].astype(F32) * (gate * (1.0 + normed * (1.0 - gate)))
-    grad = scale * (slope - normed * jnp.mean(slope * normed, -1, keepdims=True))
-    grad = grad.astype(BF16)
-    sum_s[...] += lax.dot_general(feats, grad, over_rows, preferred_element_type=F32)
-    sum_n[...] += jnp.dot(agg, grad, preferred_element_type=F32)
-
-    if last:
-
-        @pl.when(i == pl.num_programs(0) - 1)
-        def _():
-            pairs, share, _ = keep_s.shape
-            side = at[1] % 2
-            for total, keep, give in ((sum_s, keep_s, give_s), (sum_n, keep_n, give_n)):
-                for pair in range(pairs):
-                    here = pl.multiple_of((2 * pair + side) * share, share)
-                    there = pl.multiple_of((2 * pair + 1 - side) * share, share)
-                    keep[pair] = total[pl.ds(here, share)]
-                    give[pair] = total[pl.ds(there, share)].astype(BF16)
-
-
-def run_head(at, parts, feats, cot, weights, hidden, held, chunk, chunks, configs):
+    for i in range(span // step):
+        here = slice(i * step, (i + 1) * step)
+        pre = pre_ref[here] + lax.dot_general(
+            agg_ref[:, here], w_ref[:, width:], over_rows, preferred_element_type=F32
+        )
+        scale = lax.rsqrt(jnp.mean(pre * pre, -1, keepdims=True) + 1e-05)
+        normed = pre * scale
+        gate = jax.nn.sigmoid(normed)
+        made_ref[here] = (normed * gate).astype(BF16)
+        store(made_ref.at[here], out_ref.at[base + i * step : base + (i + 1) * step])
+        slope = c_ref[here].astype(F32)
+        slope = slope * (gate * (1.0 + normed * (1.0 - gate)))
+        grad = scale * (slope - normed * jnp.mean(slope * normed, -1, keepdims=True))
+        grad_ref[here] = grad.astype(BF16)
+
+    for copy in late:
+        copy.wait()
+    grad = grad_ref[...]
+    for i, total in enumerate(totals):
+        if i == 0:
+            term = lax.dot_general(x_ref[...], grad, over_rows, preferred_element_type=F32)
+        else:
+            term = jnp.dot(agg_ref[...], grad, preferred_element_type=F32)
+        total[...] = term if first else total[...] + term
+        if not last:
+            store(total, sum_refs[i])
+            continue
+        keep, give = sum_refs[i], sum_refs[2 + i]
+        pairs, share, _ = keep.shape
+        side = at[1] % 2
+        for pair in range(pairs):
+            here = pl.multiple_of((2 * pair + side) * share, share)
+            there = pl.multiple_of((2 * pair + 1 - side) * share, share)
+            gives[i][pair] = total[pl.ds(there, share)].astype(BF16)
+            store(total.at[pl.ds(here, share)], keep.at[pair])
+        store(gives[i], give)
+    for copy in stores:
+        copy.wait()
+
+
+def run_head(at, parts, feats, cot, weights, hidden, held, base, span, configs):
+    peers = len(parts)
     rows, width = feats.shape
-    span = rows // chunks
+    first, last = base == 0, base + span == rows
     step = 256 if span % 256 == 0 else 128
-    steps = span // step
-    base = chunk * steps
-    by_rows = pl.BlockSpec((step, width), lambda i, at: (base + i, 0))
-    first, last = chunk == 0, chunk == chunks - 1
     shapes = [jax.ShapeDtypeStruct((rows, width), BF16)]
-    out_specs = [by_rows]
     sums = (width, width)
-    scratch = [pltpu.VMEM((width, span), BF16)]
-    peers = len(parts)
+    scratch = [
+        pltpu.VMEM((width, span), BF16),
+        pltpu.VMEM((span, width), BF16),
+        pltpu.VMEM((span, width), BF16),
+        pltpu.VMEM((width, 2 * width), BF16),
+        pltpu.VMEM((span, width), F32),
+        pltpu.VMEM((span, width), BF16),
+        pltpu.VMEM((span, width), BF16),
+        pltpu.VMEM(sums, F32),
+        pltpu.VMEM(sums, F32),
+        pltpu.SemaphoreType.DMA((peers + 5,)),
+        pltpu.SemaphoreType.DMA((span // step + (2 + configs if last else 2),)),
+    ]
     if last:
         share = (configs // 2, width // configs, width)
         shapes += [jax.ShapeDtypeStruct(share, F32)] * 2 + [jax.ShapeDtypeStruct(share, BF16)] * 2
-        out_specs += [WHOLE] * 4
-        scratch += [pltpu.VMEM(sums, F32)] * 2
+        scratch += [pltpu.VMEM(share, BF16)] * 2
     else:
         shapes += [jax.ShapeDtypeStruct(sums, F32)] * 2
-        out_specs += [WHOLE] * 2
+    operands = [*parts, feats, cot, weights] + ([] if first else [hidden, *held])
     return pl.pallas_call(
-        functools.partial(head_kernel, peers, first, last),
+        functools.partial(head_kernel, peers, base, first, last),
         out_shape=shapes,
         grid_spec=pltpu.PrefetchScalarGridSpec(
             num_scalar_prefetch=1,
-            grid=(steps,),
-            in_specs=[WHOLE] * peers
-            + [by_rows, by_rows, WHOLE]
-            + ([] if first else [pl.BlockSpec(memory_space=pl.ANY), WHOLE, WHOLE]),
-            out_specs=out_specs,
+            grid=(),
+            in_specs=[STAYS] * len(operands),
+            out_specs=[STAYS] * len(shapes),
             scratch_shapes=scratch,
         ),
         input_output_aliases={} if first else {peers + 4: 0},
-        compiler_params=pltpu.CompilerParams(vmem_limit_bytes=24 << 20),
+        compiler_params=pltpu.CompilerParams(vmem_limit_bytes=60 << 20),
         cost_estimate=pl.CostEstimate(
             flops=8 * span * width * width, bytes_accessed=8 * span * width, transcendentals=span * width
         ),
-    )(at, *parts, feats, cot, weights, *(() if first else (hidden, *held)))
+    )(at, *operands)
 
 
 def local(features, cotangent, w_self, w_neigh, tiles, edge_peer, edge_src, edge_dst, edge_tile):
@@ -262,26 +308,28 @@
     middle = peers // 2
 
     piece = count * tile // configs
-    packed = pl.pallas_call(
+    per = piece // tile if piece % tile == 0 else count
+    pack = pl.pallas_call(
         pack_kernel,
         out_shape=jax.ShapeDtypeStruct((piece + 16, tile), BF16),
         grid_spec=pltpu.PrefetchScalarGridSpec(
             num_scalar_prefetch=1,
             grid=(),
-            in_specs=[WHOLE] * 5,
+            in_specs=[STAYS] * 5,
             out_specs=WHOLE,
-            scratch_shapes=[pltpu.VMEM((count * tile, tile), BF16), pltpu.VMEM((16, tile), F32)],
-        ),
-        compiler_params=pltpu.CompilerParams(vmem_limit_bytes=8 << 20),
+            scratch_shapes=[
+                pltpu.VMEM((per, tile, tile), BF16),
+                pltpu.VMEM((count * tile, tile), BF16),
+                pltpu.VMEM((4, 1, edges), I32),
+                pltpu.VMEM((16, tile), F32),
+                pltpu.SemaphoreType.DMA((5,)),
+            ],
+        ),
+        compiler_params=pltpu.CompilerParams(vmem_limit_bytes=60 << 20),
         name="pack",
-    )(
-        at,
-        tiles,
-        edge_peer.reshape(1, edges),
-        edge_src.reshape(1, edges),
-        edge_dst.reshape(1, edges),
-        edge_tile.reshape(1, edges),
     )
+    lists = [each.reshape(1, edges) for each in (edge_peer, edge_src, edge_dst, edge_tile)]
+    packed = pack(at, tiles, *lists)
     far_turned = turn_half(at, feats, peers, 1)
     near_turned = turn_half(at, feats, peers, 0)
 
@@ -298,7 +346,6 @@
     infos = held[:, piece : piece + 4, :edges].astype(I32)
     slot_of = jnp.arange(peers, dtype=I32)[:, None]
     if piece % tile == 0:
-        per = piece // tile
         owner = reverse_bits((infos[:, 3] // per) ^ own, configs)
         which = (owner * peers + slot_of) * per + infos[:, 3] % per
         all_tiles = pieces.reshape(peers * count, tile, tile)
@@ -323,11 +370,12 @@
     partly = sum_edges(at, meta, [moved[k] for k in near], [slot[k] for k in near], all_tiles, None, 0)[0]
     summed = sum_edges(at, meta, [moved[k] for k in far], [slot[k] for k in far], all_tiles, partly, chunks)
     held = hidden = None
+    span = rows // chunks
     for chunk in range(chunks):
         parts = summed[chunk * peers : (chunk + 1) * peers]
         back = [parts[0]] + [swap(parts[k], "dom", k) for k in range(1, peers)]
         hidden, *held = run_head(
-            at, back, feats, cot, weights, hidden, held, chunk, chunks, configs
+            at, back, feats, cot, weights, hidden, held, chunk * span, span, configs
         )
     keep_s, keep_n, give_s, give_n = held
     factor = float(configs * peers * rows) ** (-0.5)

time: 168 us -> 168 us (level)
  local copies, waits for them, and re-layouts: 14.5 us -> 3.72 us
  starting transfers between devices: 65.9 us -> 74.8 us
  waiting for transfers between devices: 63 us -> 59.2 us
  other arithmetic: 4.66 us -> 7.86 us
  Pallas kernels: 18.8 us -> 20.7 us
    unnamed x38 -> x42, local copies, waits for them, and re-layouts: 12.6 us -> 2.04 us
    ppermute x38, starting transfers between devices: 65.9 us -> 74.8 us  [swap(): return lax.ppermute(value, axis, [(i, i ^ bits) for i in range(size)])]
    ppermute x38, waiting for transfers between devices: 63 us -> 59.2 us  [swap(): return lax.ppermute(value, axis, [(i, i ^ bits) for i in range(size)])]
    pallas_call x3, Pallas kernels: 11.8 us -> 14.3 us  [the longest x2 11.9 us: run_head(): pl.pallas_call(functools.partial(head_kernel, peers, base, first, last),...]
    concatenate x2, other arithmetic: 0.04 us -> 1.81 us  [layer(): held = jnp.concatenate([held, swap(held, 'dom', bit)], 0)]
  transfers between devices with their start and end apart: 38 -> 38, of which waited for: 18 -> 19; matrix products, arithmetic and copies ran while one was open for 3% -> 3% of each run, Pallas kernels for 8% -> 7%
where the time goes in v2:
time: 168 us; the launch traced here: 167 us
  starting transfers between devices  74.8 us (45%)
  waiting for transfers between devices  59.2 us (35%)
  Pallas kernels  20.7 us (12%)
  other arithmetic  7.86 us (5%)
  local copies, waits for them, and re-layouts  3.72 us (2%)
    ppermute x38, starting transfers between devices, swap(): return lax.ppermute(value, axis, [(i, i ^ bits) for i in range(size)])  74.8 us
    ppermute x38, waiting for transfers between devices, swap(): return lax.ppermute(value, axis, [(i, i ^ bits) for i in range(size)])  59.2 us
    pallas_call x2, Pallas kernels, run_head(): pl.pallas_call(functools.partial(head_kernel, peers, base, first, last),...  11.9 us
    pallas_call x2, Pallas kernels, sum_edges(): pl.pallas_call(functools.partial(edges_kernel, slots, held is None, chunk...  4.62 us
  transfers between devices with their start and end apart: 38, of which 19 were waited for; matrix products, arithmetic and copies ran while one was open for 3% of the time, Pallas kernels for 7%

profile of v2, /device:TPU:0, one launch (start us, length us, event | category | flops | bytes accessed | tf_op | source)
XLA Modules:
  0.0 167.3 jit_solution(9374247288672394791)
XLA Ops:
  0.6 0.6 pad_add_fusion.1.at
  1.2 2.4 %pack.1 = bf16[272,128]{1,0:T(8,128)(2,1)} custom-call(s32[2]{0:T(128)} %pad_add_fusion.1.at, bf16[8,128,128]{2,1,0:T(8,128)(2,1)} %tiles_hbm.1, s32[1,32]{1,0:T(1,128)} %bitcast.42, s32[1,32]{1,0:T(1,128)} %bitcast.43, s32[1,32]{1,0:T(1,128)} %bitcast.44, s32[1,32]{1,0:T(1,128)} %bitcast.45), custom_call_target="tpu_custom_call" | custom-call | tf_op jit(solution)/shard_map/pack/pallas_call | solution.py:332
  3.6 4.1 %collective-permute-start = (bf16[1,272,128]{2,1,0:T(8,128)(2,1)}, bf16[1,272,128]{2,1,0:T(8,128)(2,1)S(1)}, u32[]{:S(2)}, u32[]{:S(2)}) collective-permute-start(bf16[1,272,128]{2,1,0:T(8,128)(2,1)} %bitcast.34), channel_id=1, source_target_pairs={{0,4},{1,5},{2,6},{3,7},{4,0},{5,1},{6,2},{7,3},{8,12},{9,13},{10,... | collective-permute-start | bytes 208904 | tf_op jit(solution)/shard_map/ppermute | solution.py:19
  7.8 4.0 %collective-permute-done = bf16[1,272,128]{2,1,0:T(8,128)(2,1)S(1)} collective-permute-done((bf16[1,272,128]{2,1,0:T(8,128)(2,1)}, bf16[1,272,128]{2,1,0:T(8,128)(2,1)S(1)}, u32[]{:S(2)}, u32[]{:S(2)}) %collective-permute-start) | collective-permute-done | bytes 69664 | tf_op jit(solution)/shard_map/ppermute | solution.py:19
  11.8 0.9 pad_maximum_fusion.8
  12.7 0.8 collective-permute-start.1
  13.5 4.3 %collective-permute-done.1 = bf16[2,272,128]{2,1,0:T(8,128)(2,1)S(1)} collective-permute-done((bf16[2,272,128]{2,1,0:T(8,128)(2,1)S(1)}, bf16[2,272,128]{2,1,0:T(8,128)(2,1)S(1)}, u32[]{:S(2)}, u32[]{:S(2)}) %collective-permute-start.1) | collective-permute-done | bytes 139296 | tf_op jit(solution)/shard_map/ppermute | solution.py:19
  17.8 0.9 pad_maximum_fusion.7
  18.7 1.8 %collective-permute-start.2 = (bf16[4,272,128]{2,1,0:T(8,128)(2,1)S(1)}, bf16[4,272,128]{2,1,0:T(8,128)(2,1)S(1)}, u32[]{:S(2)}, u32[]{:S(2)}) collective-permute-start(bf16[4,272,128]{2,1,0:T(8,128)(2,1)S(1)} %pad_maximum_fusion.7), channel_id=1, source_target_pairs={{0,1},{1,0},{2,3},{3,2},{4,5},{5,4},{6,7},{7,6},{8,9},{9,8},{10,11... | collective-permute-start | bytes 835592 | tf_op jit(solution)/shard_map/ppermute | solution.py:19
  20.5 4.8 %collective-permute-done.2 = bf16[4,272,128]{2,1,0:T(8,128)(2,1)S(1)} collective-permute-done((bf16[4,272,128]{2,1,0:T(8,128)(2,1)S(1)}, bf16[4,272,128]{2,1,0:T(8,128)(2,1)S(1)}, u32[]{:S(2)}, u32[]{:S(2)}) %collective-permute-start.2) | collective-permute-done | bytes 278560 | tf_op jit(solution)/shard_map/ppermute | solution.py:19
  25.3 0.9 fusion
  26.2 1.8 %collective-permute-start.7 = (bf16[1,8,256,128]{3,2,1,0:T(8,128)(2,1)S(1)}, bf16[1,8,256,128]{3,2,1,0:T(8,128)(2,1)S(1)}, u32[]{:S(2)}, u32[]{:S(2)}) collective-permute-start(bf16[1,8,256,128]{3,2,1,0:T(8,128)(2,1)S(1)} %fusion), channel_id=1, source_target_pairs={{0,16},{8,24},{16,0},{24,8},{1,17},{9,25},{17,1},{25,9},{2,18},{10... | collective-permute-start | bytes 1572872 | tf_op jit(solution)/shard_map/ppermute | solution.py:19
  28.0 8.4 %collective-permute-done.7 = bf16[1,8,256,128]{3,2,1,0:T(8,128)(2,1)S(1)} collective-permute-done((bf16[1,8,256,128]{3,2,1,0:T(8,128)(2,1)S(1)}, bf16[1,8,256,128]{3,2,1,0:T(8,128)(2,1)S(1)}, u32[]{:S(2)}, u32[]{:S(2)}) %collective-permute-start.7) | collective-permute-done | bytes 524320 | tf_op jit(solution)/shard_map/ppermute | solution.py:19
  36.6 1.6 collective-permute-start.19
  38.2 0.9 shard_map.113
  39.1 3.2 %collective-permute-start.10 = (bf16[64,1536]{1,0:T(8,128)(2,1)S(1)}, bf16[64,1536]{1,0:T(8,128)(2,1)S(1)}, u32[]{:S(2)}, u32[]{:S(2)}) collective-permute-start(bf16[64,1536]{1,0:T(8,128)(2,1)S(1)} %get-tuple-element.41), channel_id=1, source_target_pairs={{0,2},{1,3},{2,0},{3,1},{4,6},{5,7},{6,4},{7,5},{8,10},{9,11},{10,... | collective-permute-start | bytes 589832 | tf_op jit(solution)/shard_map/ppermute | solution.py:19
  42.3 1.0 collective-permute-start.11
  43.3 0.5 collective-permute-start.9
  43.8 0.9 shard_map.112
  44.7 0.6 collective-permute-done.19
  45.6 2.4 %collective-permute-done.10.refs_2_ = bf16[64,1536]{1,0:T(8,128)(2,1)S(1)} collective-permute-done((bf16[64,1536]{1,0:T(8,128)(2,1)S(1)}, bf16[64,1536]{1,0:T(8,128)(2,1)S(1)}, u32[]{:S(2)}, u32[]{:S(2)}) %collective-permute-start.10) | collective-permute-done | bytes 196640 | tf_op jit(solution)/shard_map/ppermute | solution.py:19
  48.1 4.5 %collective-permute-start.3 = (bf16[64,1536]{1,0:T(8,128)(2,1)S(1)}, bf16[64,1536]{1,0:T(8,128)(2,1)S(1)}, u32[]{:S(2)}, u32[]{:S(2)}) collective-permute-start(bf16[64,1536]{1,0:T(8,128)(2,1)S(1)} %get-tuple-element.35), channel_id=1, source_target_pairs={{0,4},{1,5},{2,6},{3,7},{4,0},{5,1},{6,2},{7,3},{8,12},{9,13},{10,... | collective-permute-start | bytes 589832 | tf_op jit(solution)/shard_map/ppermute | solution.py:19
  52.8 4.9 %collective-permute-start.4 = (bf16[64,1536]{1,0:T(8,128)(2,1)S(1)}, bf16[64,1536]{1,0:T(8,128)(2,1)S(1)}, u32[]{:S(2)}, u32[]{:S(2)}) collective-permute-start(bf16[64,1536]{1,0:T(8,128)(2,1)S(1)} %get-tuple-element.36), channel_id=1, source_target_pairs={{0,5},{1,4},{2,7},{3,6},{4,1},{5,0},{6,3},{7,2},{8,13},{9,12},{10,... | collective-permute-start | bytes 589832 | tf_op jit(solution)/shard_map/ppermute | solution.py:19
  57.8 1.3 collective-permute-start.5
  59.1 3.5 %collective-permute-start.6 = (bf16[64,1536]{1,0:T(8,128)(2,1)S(1)}, bf16[64,1536]{1,0:T(8,128)(2,1)S(1)}, u32[]{:S(2)}, u32[]{:S(2)}) collective-permute-start(bf16[64,1536]{1,0:T(8,128)(2,1)S(1)} %get-tuple-element.38), channel_id=1, source_target_pairs={{0,7},{1,6},{2,5},{3,4},{4,3},{5,2},{6,1},{7,0},{8,15},{9,14},{10,... | collective-permute-start | bytes 589832 | tf_op jit(solution)/shard_map/ppermute | solution.py:19
  62.7 2.2 %shard_map.114.refs_5_ = f32[96,64,128]{2,1,0:T(8,128)S(1)} custom-call(s32[2]{0:T(128)S(1)} %copy-done.2, s32[8,3,32]{2,1,0:T(4,128)S(1)} %pad_add_fusion.meta, bf16[64,1536]{1,0:T(8,128)(2,1)S(1)} %get-tuple-element.39.refs_0_, bf16[64,1536]{1,0:T(8,128)(2,1)S(1)} %collective-permute-done.9.refs_1_, bf16[64,1536]{1,0:T(8,128)(2,1)S(1)} %collective-permute-done.10.refs_2_, ...), custom_call_target="tpu_custom_call" | custom-call | flops 268435456 | bytes 1835008 | tf_op jit(solution)/shard_map/pallas_call | solution.py:140
  64.9 10.2 %collective-permute-done.3.refs_0_ = bf16[64,1536]{1,0:T(8,128)(2,1)S(1)} collective-permute-done((bf16[64,1536]{1,0:T(8,128)(2,1)S(1)}, bf16[64,1536]{1,0:T(8,128)(2,1)S(1)}, u32[]{:S(2)}, u32[]{:S(2)}) %collective-permute-start.3) | collective-permute-done | bytes 196640 | tf_op jit(solution)/shard_map/ppermute | solution.py:19
  75.1 5.2 %collective-permute-done.4.refs_1_ = bf16[64,1536]{1,0:T(8,128)(2,1)S(1)} collective-permute-done((bf16[64,1536]{1,0:T(8,128)(2,1)S(1)}, bf16[64,1536]{1,0:T(8,128)(2,1)S(1)}, u32[]{:S(2)}, u32[]{:S(2)}) %collective-permute-start.4) | collective-permute-done | bytes 196640 | tf_op jit(solution)/shard_map/ppermute | solution.py:19
  80.3 2.4 %shard_map.115 = (bf16[64,768]{1,0:T(8,128)(2,1)S(1)}, bf16[64,768]{1,0:T(8,128)(2,1)S(1)}, bf16[64,768]{1,0:T(8,128)(2,1)S(1)}, bf16[64,768]{1,0:T(8,128)(2,1)S...) custom-call(s32[2]{0:T(128)S(1)} %copy-done.2, ...), custom_call_target="tpu_custom_call" | custom-call | flops 268435456 | bytes 1835008 | tf_op jit(solution)/shard_map/pallas_call | solution.py:140
  82.8 0.6 copy-done.1
  83.4 0.6 copy-done.3
  84.5 7.7 %collective-permute-start.22 = (bf16[64,768]{1,0:T(8,128)(2,1)S(1)}, bf16[64,768]{1,0:T(8,128)(2,1)S(1)}, u32[]{:S(2)}, u32[]{:S(2)}) collective-permute-start(bf16[64,768]{1,0:T(8,128)(2,1)S(1)} %get-tuple-element.53), channel_id=1, source_target_pairs={{0,2},{1,3},{2,0},{3,1},{4,6},{5,7},{6,4},{7,5},{8,10},{9,11},{10,... | collective-permute-start | bytes 294920 | tf_op jit(solution)/shard_map/ppermute | solution.py:19
  92.2 0.9 collective-permute-start.23
  93.1 3.8 %collective-permute-start.24 = (bf16[64,768]{1,0:T(8,128)(2,1)S(1)}, bf16[64,768]{1,0:T(8,128)(2,1)S(1)}, u32[]{:S(2)}, u32[]{:S(2)}) collective-permute-start(bf16[64,768]{1,0:T(8,128)(2,1)S(1)} %get-tuple-element.55), channel_id=1, source_target_pairs={{0,4},{1,5},{2,6},{3,7},{4,0},{5,1},{6,2},{7,3},{8,12},{9,13},{10,... | collective-permute-start | bytes 294920 | tf_op jit(solution)/shard_map/ppermute | solution.py:19
  97.1 2.3 %collective-permute-start.26 = (bf16[64,768]{1,0:T(8,128)(2,1)S(1)}, bf16[64,768]{1,0:T(8,128)(2,1)S(1)}, u32[]{:S(2)}, u32[]{:S(2)}) collective-permute-start(bf16[64,768]{1,0:T(8,128)(2,1)S(1)} %get-tuple-element.57), channel_id=1, source_target_pairs={{0,6},{1,7},{2,4},{3,5},{4,2},{5,3},{6,0},{7,1},{8,14},{9,15},{10,... | collective-permute-start | bytes 294920 | tf_op jit(solution)/shard_map/ppermute | solution.py:19
  99.4 2.4 %collective-permute-start.27 = (bf16[64,768]{1,0:T(8,128)(2,1)S(1)}, bf16[64,768]{1,0:T(8,128)(2,1)S(1)}, u32[]{:S(2)}, u32[]{:S(2)}) collective-permute-start(bf16[64,768]{1,0:T(8,128)(2,1)S(1)} %get-tuple-element.58), channel_id=1, source_target_pairs={{0,7},{1,6},{2,5},{3,4},{4,3},{5,2},{6,1},{7,0},{8,15},{9,14},{10,... | collective-permute-start | bytes 294920 | tf_op jit(solution)/shard_map/ppermute | solution.py:19
  101.8 0.6 collective-permute-start.12
  102.4 5.0 %collective-permute-done.24.refs_4_ = bf16[64,768]{1,0:T(8,128)(2,1)S(1)} collective-permute-done((bf16[64,768]{1,0:T(8,128)(2,1)S(1)}, bf16[64,768]{1,0:T(8,128)(2,1)S(1)}, u32[]{:S(2)}, u32[]{:S(2)}) %collective-permute-start.24) | collective-permute-done | bytes 98336 | tf_op jit(solution)/shard_map/ppermute | solution.py:19
  107.4 0.7 collective-permute-start.13
  108.2 1.6 gather_fusion
  109.8 1.4 collective-permute-done.25.refs_5_
  111.3 3.2 %collective-permute-start.15 = (bf16[64,768]{1,0:T(8,128)(2,1)S(1)}, bf16[64,768]{1,0:T(8,128)(2,1)S(1)}, u32[]{:S(2)}, u32[]{:S(2)}) collective-permute-start(bf16[64,768]{1,0:T(8,128)(2,1)S(1)} %get-tuple-element.47), channel_id=1, source_target_pairs={{0,4},{1,5},{2,6},{3,7},{4,0},{5,1},{6,2},{7,3},{8,12},{9,13},{10,... | collective-permute-start | bytes 294920 | tf_op jit(solution)/shard_map/ppermute | solution.py:19
  114.5 3.4 %collective-permute-start.16 = (bf16[64,768]{1,0:T(8,128)(2,1)S(1)}, bf16[64,768]{1,0:T(8,128)(2,1)S(1)}, u32[]{:S(2)}, u32[]{:S(2)}) collective-permute-start(bf16[64,768]{1,0:T(8,128)(2,1)S(1)} %get-tuple-element.48), channel_id=1, source_target_pairs={{0,5},{1,4},{2,7},{3,6},{4,1},{5,0},{6,3},{7,2},{8,13},{9,12},{10,... | collective-permute-start | bytes 294920 | tf_op jit(solution)/shard_map/ppermute | solution.py:19
  117.9 0.8 collective-permute-start.17
  118.7 3.2 %collective-permute-start.18 = (bf16[64,768]{1,0:T(8,128)(2,1)S(1)}, bf16[64,768]{1,0:T(8,128)(2,1)S(1)}, u32[]{:S(2)}, u32[]{:S(2)}) collective-permute-start(bf16[64,768]{1,0:T(8,128)(2,1)S(1)} %get-tuple-element.50), channel_id=1, source_target_pairs={{0,7},{1,6},{2,5},{3,4},{4,3},{5,2},{6,1},{7,0},{8,15},{9,14},{10,... | collective-permute-start | bytes 294920 | tf_op jit(solution)/shard_map/ppermute | solution.py:19
  121.9 5.8 %shard_map.116 = (bf16[1536,512]{1,0:T(8,128)(2,1)}, f32[512,512]{1,0:T(8,128)}, f32[512,512]{1,0:T(8,128)}) custom-call(s32[2]{0:T(128)} %pad_add_fusion.1.at, bf16[64,768]{1,0:T(8,128)(2,1)} %copy-done.3, bf16[64,768]{1,0:T(8,128)(2,1)} %copy-done.14, bf16[64,768]{1,0:T(8,128)(2,1)} %copy-done.15, bf16[64,768]{1,0:T(8,128)(2,1)} %copy-done.16, ...), custom_call_target="tpu_custom_call" | custom-call | flops 1610612736 | bytes 3145728 | tf_op jit(solution)/shard_map/pallas_call | solution.py:271
  129.0 6.1 %shard_map.117 = (bf16[1536,512]{1,0:T(8,128)(2,1)}, f32[2,128,512]{2,1,0:T(8,128)}, f32[2,128,512]{2,1,0:T(8,128)}, bf16[2,128,512]{2,1,0:T(8,128)(2,1)}, bf16[2,128,512]{2,1,0:T(8,128)(2,1)}) custom-call(s32[2]{0:T(128)} %pad_add_fusion.1.at, bf16[64,768]{1,0:T(8,128)(2,1)} %copy-done.1, ...), custom_call_target="tpu_custom_call", output_to_operand_aliasing={{0}: (12, {})} | custom-call | flops 1610612736 | bytes 3145728 | tf_op jit(solution)/shard_map/pallas_call | solution.py:271
  135.7 1.2 collective-permute-done.33
  137.0 1.1 convert_add_fusion
  138.1 1.6 collective-permute-start.34
  139.7 1.1 convert_add_fusion.1
  140.9 0.6 collective-permute-start.29
  141.4 2.6 %collective-permute-done.34 = bf16[1,128,512]{2,1,0:T(8,128)(2,1)S(1)} collective-permute-done((bf16[1,128,512]{2,1,0:T(8,128)(2,1)S(1)}, bf16[1,128,512]{2,1,0:T(8,128)(2,1)S(1)}, u32[]{:S(2)}, u32[]{:S(2)}) %collective-permute-start.34) | collective-permute-done | bytes 131104 | tf_op jit(solution)/shard_map/ppermute | solution.py:19
  144.1 3.4 %collective-permute-start.35 = (bf16[128,512]{1,0:T(8,128)(2,1)S(1)}, bf16[128,512]{1,0:T(8,128)(2,1)S(1)}, u32[]{:S(2)}, u32[]{:S(2)}) collective-permute-start(bf16[128,512]{1,0:T(8,128)(2,1)S(1)} %bitcast_convert_fusion), channel_id=1, source_target_pairs={{0,2},{1,3},{2,0},{3,1},{4,6},{5,7},{6,4},{7,5},{8,10},{9,11},{10,... | collective-permute-start | bytes 393224 | tf_op jit(solution)/shard_map/ppermute | solution.py:19
  147.6 1.4 collective-permute-start.30
  148.9 1.5 collective-permute-done.35
  150.5 2.6 %collective-permute-start.36 = (bf16[128,512]{1,0:T(8,128)(2,1)S(1)}, bf16[128,512]{1,0:T(8,128)(2,1)S(1)}, u32[]{:S(2)}, u32[]{:S(2)}) collective-permute-start(bf16[128,512]{1,0:T(8,128)(2,1)S(1)} %get-tuple-element.67), channel_id=1, source_target_pairs={{0,4},{1,5},{2,6},{3,7},{4,0},{5,1},{6,2},{7,3},{8,12},{9,13},{10,... | collective-permute-start | bytes 393224 | tf_op jit(solution)/shard_map/ppermute | solution.py:19
  153.1 2.0 %collective-permute-start.31 = (bf16[128,512]{1,0:T(8,128)(2,1)S(1)}, bf16[128,512]{1,0:T(8,128)(2,1)S(1)}, u32[]{:S(2)}, u32[]{:S(2)}) collective-permute-start(bf16[128,512]{1,0:T(8,128)(2,1)S(1)} %get-tuple-element.69), channel_id=1, source_target_pairs={{0,2},{1,3},{2,0},{3,1},{4,6},{5,7},{6,4},{7,5},{8,10},{9,11},{10,... | collective-permute-start | bytes 393224 | tf_op jit(solution)/shard_map/ppermute | solution.py:19
  155.1 1.4 collective-permute-done.36
  156.5 1.4 collective-permute-start.37
  158.4 2.6 %collective-permute-start.32 = (bf16[128,512]{1,0:T(8,128)(2,1)S(1)}, bf16[128,512]{1,0:T(8,128)(2,1)S(1)}, u32[]{:S(2)}, u32[]{:S(2)}) collective-permute-start(bf16[128,512]{1,0:T(8,128)(2,1)S(1)} %fusion.1), channel_id=1, source_target_pairs={{0,4},{1,5},{2,6},{3,7},{4,0},{5,1},{6,2},{7,3},{8,12},{9,13},{10,... | collective-permute-start | bytes 393224 | tf_op jit(solution)/shard_map/ppermute | solution.py:19
  161.5 0.8 add_multiply_fusion
  162.3 4.2 %collective-permute-done.32 = bf16[128,512]{1,0:T(8,128)(2,1)S(1)} collective-permute-done((bf16[128,512]{1,0:T(8,128)(2,1)S(1)}, bf16[128,512]{1,0:T(8,128)(2,1)S(1)}, u32[]{:S(2)}, u32[]{:S(2)}) %collective-permute-start.32) | collective-permute-done | bytes 131104 | tf_op jit(solution)/shard_map/ppermute | solution.py:19
  166.5 0.8 add_multiply_fusion.1
  (88 shorter events, 4.6 us)
Async XLA Ops:
  1.2 35.3 %copy-start.5 = (bf16[128,512]{1,0:T(8,128)(2,1)S(1)}, bf16[128,512]{1,0:T(8,128)(2,1)}, u32[]{:S(2)}) copy-start(bf16[128,512]{1,0:T(8,128)(2,1)} %param.12) | copy-start | bytes 393220
  1.2 35.3 %copy-start.6 = (bf16[128,512]{1,0:T(8,128)(2,1)S(1)}, bf16[128,512]{1,0:T(8,128)(2,1)}, u32[]{:S(2)}) copy-start(bf16[128,512]{1,0:T(8,128)(2,1)} %param.11) | copy-start | bytes 393220
  3.6 8.1 %collective-permute-start = (bf16[1,272,128]{2,1,0:T(8,128)(2,1)}, bf16[1,272,128]{2,1,0:T(8,128)(2,1)S(1)}, u32[]{:S(2)}, u32[]{:S(2)}) collective-permute-start(bf16[1,272,128]{2,1,0:T(8,128)(2,1)} %bitcast.34), channel_id=1, source_target_pairs={{0,4},{1,5},{2,6},{3,7},{4,0},{5,1},{6,2},{7,3},{8,12},{9,13},{10,... | collective-permute-start | bytes 208904 | tf_op jit(solution)/shard_map/ppermute | solution.py:19
  12.7 25.5 %copy-start = (bf16[1,1536,512]{2,1,0:T(8,128)(2,1)S(1)}, bf16[1,1536,512]{2,1,0:T(8,128)(2,1)}, u32[]{:S(2)}) copy-start(bf16[1,1536,512]{2,1,0:T(8,128)(2,1)} %param.9) | copy-start | bytes 4718596
  12.7 25.5 %copy-start.2 = (s32[2]{0:T(128)S(1)}, s32[2]{0:T(128)}, u32[]{:S(2)}) copy-start(s32[2]{0:T(128)} %pad_add_fusion.1.at) | copy-start | bytes 28
  12.7 5.1 %collective-permute-start.1 = (bf16[2,272,128]{2,1,0:T(8,128)(2,1)S(1)}, bf16[2,272,128]{2,1,0:T(8,128)(2,1)S(1)}, u32[]{:S(2)}, u32[]{:S(2)}) collective-permute-start(bf16[2,272,128]{2,1,0:T(8,128)(2,1)S(1)} %pad_maximum_fusion.8), channel_id=1, source_target_pairs={{0,2},{1,3},{2,0},{3,1},{4,6},{5,7},{6,4},{7,5},{8,10},{9,11},{10,... | collective-permute-start | bytes 417800 | tf_op jit(solution)/shard_map/ppermute | solution.py:19
  18.7 6.6 %collective-permute-start.2 = (bf16[4,272,128]{2,1,0:T(8,128)(2,1)S(1)}, bf16[4,272,128]{2,1,0:T(8,128)(2,1)S(1)}, u32[]{:S(2)}, u32[]{:S(2)}) collective-permute-start(bf16[4,272,128]{2,1,0:T(8,128)(2,1)S(1)} %pad_maximum_fusion.7), channel_id=1, source_target_pairs={{0,1},{1,0},{2,3},{3,2},{4,5},{5,4},{6,7},{7,6},{8,9},{9,8},{10,11... | collective-permute-start | bytes 835592 | tf_op jit(solution)/shard_map/ppermute | solution.py:19
  26.2 10.2 %collective-permute-start.7 = (bf16[1,8,256,128]{3,2,1,0:T(8,128)(2,1)S(1)}, bf16[1,8,256,128]{3,2,1,0:T(8,128)(2,1)S(1)}, u32[]{:S(2)}, u32[]{:S(2)}) collective-permute-start(bf16[1,8,256,128]{3,2,1,0:T(8,128)(2,1)S(1)} %fusion), channel_id=1, source_target_pairs={{0,16},{8,24},{16,0},{24,8},{1,17},{9,25},{17,1},{25,9},{2,18},{10... | collective-permute-start | bytes 1572872 | tf_op jit(solution)/shard_map/ppermute | solution.py:19
  36.5 22.6 %collective-permute-start.8 = (bf16[2,8,256,128]{3,2,1,0:T(8,128)(2,1)S(1)}, bf16[2,8,256,128]{3,2,1,0:T(8,128)(2,1)S(1)}, u32[]{:S(2)}, u32[]{:S(2)}) collective-permute-start(bf16[2,8,256,128]{3,2,1,0:T(8,128)(2,1)S(1)} %pad_maximum_fusion.1), channel_id=1, source_target_pairs={{0,8},{8,0},{16,24},{24,16},{1,9},{9,1},{17,25},{25,17},{2,10},{10... | collective-permute-start | bytes 3145736 | tf_op jit(solution)/shard_map/ppermute | solution.py:19
  36.6 8.8 %collective-permute-start.19 = (bf16[1,128,1024]{2,1,0:T(8,128)(2,1)S(1)}, bf16[1,128,1024]{2,1,0:T(8,128)(2,1)S(1)}, u32[]{:S(2)}, u32[]{:S(2)}) collective-permute-start(bf16[1,128,1024]{2,1,0:T(8,128)(2,1)S(1)} %maximum_bitcast_fusion), channel_id=1, source_target_pairs={{0,16},{8,24},{16,0},{24,8},{1,17},{9,25},{17,1},{25,9},{2,18},{10... | collective-permute-start | bytes 786440 | tf_op jit(solution)/shard_map/ppermute | solution.py:19
  38.2 7.3 %copy-start.4 = (bf16[272,128]{1,0:T(8,128)(2,1)S(1)}, bf16[272,128]{1,0:T(8,128)(2,1)}, u32[]{:S(2)}) copy-start(bf16[272,128]{1,0:T(8,128)(2,1)} %pack.1) | copy-start | bytes 208900
  39.1 9.0 %collective-permute-start.10 = (bf16[64,1536]{1,0:T(8,128)(2,1)S(1)}, bf16[64,1536]{1,0:T(8,128)(2,1)S(1)}, u32[]{:S(2)}, u32[]{:S(2)}) collective-permute-start(bf16[64,1536]{1,0:T(8,128)(2,1)S(1)} %get-tuple-element.41), channel_id=1, source_target_pairs={{0,2},{1,3},{2,0},{3,1},{4,6},{5,7},{6,4},{7,5},{8,10},{9,11},{10,... | collective-permute-start | bytes 589832 | tf_op jit(solution)/shard_map/ppermute | solution.py:19
  42.3 10.5 %collective-permute-start.11 = (bf16[64,1536]{1,0:T(8,128)(2,1)S(1)}, bf16[64,1536]{1,0:T(8,128)(2,1)S(1)}, u32[]{:S(2)}, u32[]{:S(2)}) collective-permute-start(bf16[64,1536]{1,0:T(8,128)(2,1)S(1)} %get-tuple-element.42), channel_id=1, source_target_pairs={{0,3},{1,2},{2,1},{3,0},{4,7},{5,6},{6,5},{7,4},{8,11},{9,10},{10,... | collective-permute-start | bytes 589832 | tf_op jit(solution)/shard_map/ppermute | solution.py:19
  43.3 14.5 %collective-permute-start.9 = (bf16[64,1536]{1,0:T(8,128)(2,1)S(1)}, bf16[64,1536]{1,0:T(8,128)(2,1)S(1)}, u32[]{:S(2)}, u32[]{:S(2)}) collective-permute-start(bf16[64,1536]{1,0:T(8,128)(2,1)S(1)} %get-tuple-element.40), channel_id=1, source_target_pairs={{0,1},{1,0},{2,3},{3,2},{4,5},{5,4},{6,7},{7,6},{8,9},{9,8},{10,11... | collective-permute-start | bytes 589832 | tf_op jit(solution)/shard_map/ppermute | solution.py:19
  45.4 51.5 %collective-permute-start.20 = (bf16[2,128,1024]{2,1,0:T(8,128)(2,1)S(1)}, bf16[2,128,1024]{2,1,0:T(8,128)(2,1)S(1)}, u32[]{:S(2)}, u32[]{:S(2)}) collective-permute-start(bf16[2,128,1024]{2,1,0:T(8,128)(2,1)S(1)} %pad_maximum_fusion.6), channel_id=1, source_target_pairs={{0,8},{8,0},{16,24},{24,16},{1,9},{9,1},{17,25},{25,17},{2,10},{10... | collective-permute-start | bytes 1572872 | tf_op jit(solution)/shard_map/ppermute | solution.py:19
  48.1 27.1 %collective-permute-start.3 = (bf16[64,1536]{1,0:T(8,128)(2,1)S(1)}, bf16[64,1536]{1,0:T(8,128)(2,1)S(1)}, u32[]{:S(2)}, u32[]{:S(2)}) collective-permute-start(bf16[64,1536]{1,0:T(8,128)(2,1)S(1)} %get-tuple-element.35), channel_id=1, source_target_pairs={{0,4},{1,5},{2,6},{3,7},{4,0},{5,1},{6,2},{7,3},{8,12},{9,13},{10,... | collective-permute-start | bytes 589832 | tf_op jit(solution)/shard_map/ppermute | solution.py:19
  52.8 27.5 %collective-permute-start.4 = (bf16[64,1536]{1,0:T(8,128)(2,1)S(1)}, bf16[64,1536]{1,0:T(8,128)(2,1)S(1)}, u32[]{:S(2)}, u32[]{:S(2)}) collective-permute-start(bf16[64,1536]{1,0:T(8,128)(2,1)S(1)} %get-tuple-element.36), channel_id=1, source_target_pairs={{0,5},{1,4},{2,7},{3,6},{4,1},{5,0},{6,3},{7,2},{8,13},{9,12},{10,... | collective-permute-start | bytes 589832 | tf_op jit(solution)/shard_map/ppermute | solution.py:19
  57.8 22.6 %collective-permute-start.5 = (bf16[64,1536]{1,0:T(8,128)(2,1)S(1)}, bf16[64,1536]{1,0:T(8,128)(2,1)S(1)}, u32[]{:S(2)}, u32[]{:S(2)}) collective-permute-start(bf16[64,1536]{1,0:T(8,128)(2,1)S(1)} %get-tuple-element.37), channel_id=1, source_target_pairs={{0,6},{1,7},{2,4},{3,5},{4,2},{5,3},{6,0},{7,1},{8,14},{9,15},{10,... | collective-permute-start | bytes 589832 | tf_op jit(solution)/shard_map/ppermute | solution.py:19
  59.1 21.3 %collective-permute-start.6 = (bf16[64,1536]{1,0:T(8,128)(2,1)S(1)}, bf16[64,1536]{1,0:T(8,128)(2,1)S(1)}, u32[]{:S(2)}, u32[]{:S(2)}) collective-permute-start(bf16[64,1536]{1,0:T(8,128)(2,1)S(1)} %get-tuple-element.38), channel_id=1, source_target_pairs={{0,7},{1,6},{2,5},{3,4},{4,3},{5,2},{6,1},{7,0},{8,15},{9,14},{10,... | collective-permute-start | bytes 589832 | tf_op jit(solution)/shard_map/ppermute | solution.py:19
  82.8 0.6 copy-start.1
  83.4 0.6 copy-start.3
  84.1 13.0 %collective-permute-start.21 = (bf16[64,768]{1,0:T(8,128)(2,1)S(1)}, bf16[64,768]{1,0:T(8,128)(2,1)S(1)}, u32[]{:S(2)}, u32[]{:S(2)}) collective-permute-start(bf16[64,768]{1,0:T(8,128)(2,1)S(1)} %get-tuple-element.52), channel_id=1, source_target_pairs={{0,1},{1,0},{2,3},{3,2},{4,5},{5,4},{6,7},{7,6},{8,9},{9,8},{10,11... | collective-permute-start | bytes 294920 | tf_op jit(solution)/shard_map/ppermute | solution.py:19
  84.5 14.9 %collective-permute-start.22 = (bf16[64,768]{1,0:T(8,128)(2,1)S(1)}, bf16[64,768]{1,0:T(8,128)(2,1)S(1)}, u32[]{:S(2)}, u32[]{:S(2)}) collective-permute-start(bf16[64,768]{1,0:T(8,128)(2,1)S(1)} %get-tuple-element.53), channel_id=1, source_target_pairs={{0,2},{1,3},{2,0},{3,1},{4,6},{5,7},{6,4},{7,5},{8,10},{9,11},{10,... | collective-permute-start | bytes 294920 | tf_op jit(solution)/shard_map/ppermute | solution.py:19
  92.2 9.6 %collective-permute-start.23 = (bf16[64,768]{1,0:T(8,128)(2,1)S(1)}, bf16[64,768]{1,0:T(8,128)(2,1)S(1)}, u32[]{:S(2)}, u32[]{:S(2)}) collective-permute-start(bf16[64,768]{1,0:T(8,128)(2,1)S(1)} %get-tuple-element.54), channel_id=1, source_target_pairs={{0,3},{1,2},{2,1},{3,0},{4,7},{5,6},{6,5},{7,4},{8,11},{9,10},{10,... | collective-permute-start | bytes 294920 | tf_op jit(solution)/shard_map/ppermute | solution.py:19
  93.1 14.3 %collective-permute-start.24 = (bf16[64,768]{1,0:T(8,128)(2,1)S(1)}, bf16[64,768]{1,0:T(8,128)(2,1)S(1)}, u32[]{:S(2)}, u32[]{:S(2)}) collective-permute-start(bf16[64,768]{1,0:T(8,128)(2,1)S(1)} %get-tuple-element.55), channel_id=1, source_target_pairs={{0,4},{1,5},{2,6},{3,7},{4,0},{5,1},{6,2},{7,3},{8,12},{9,13},{10,... | collective-permute-start | bytes 294920 | tf_op jit(solution)/shard_map/ppermute | solution.py:19
  97.0 14.3 %collective-permute-start.25 = (bf16[64,768]{1,0:T(8,128)(2,1)S(1)}, bf16[64,768]{1,0:T(8,128)(2,1)S(1)}, u32[]{:S(2)}, u32[]{:S(2)}) collective-permute-start(bf16[64,768]{1,0:T(8,128)(2,1)S(1)} %get-tuple-element.56), channel_id=1, source_target_pairs={{0,5},{1,4},{2,7},{3,6},{4,1},{5,0},{6,3},{7,2},{8,13},{9,12},{10,... | collective-permute-start | bytes 294920 | tf_op jit(solution)/shard_map/ppermute | solution.py:19
  97.0 12.8 %copy-start.14 = (bf16[64,768]{1,0:T(8,128)(2,1)}, bf16[64,768]{1,0:T(8,128)(2,1)S(1)}, u32[]{:S(2)}) copy-start(bf16[64,768]{1,0:T(8,128)(2,1)S(1)} %collective-permute-done.21.refs_1_) | copy-start | bytes 294916
  97.1 14.2 %collective-permute-start.26 = (bf16[64,768]{1,0:T(8,128)(2,1)S(1)}, bf16[64,768]{1,0:T(8,128)(2,1)S(1)}, u32[]{:S(2)}, u32[]{:S(2)}) collective-permute-start(bf16[64,768]{1,0:T(8,128)(2,1)S(1)} %get-tuple-element.57), channel_id=1, source_target_pairs={{0,6},{1,7},{2,4},{3,5},{4,2},{5,3},{6,0},{7,1},{8,14},{9,15},{10,... | collective-permute-start | bytes 294920 | tf_op jit(solution)/shard_map/ppermute | solution.py:19
  99.4 10.4 %copy-start.15 = (bf16[64,768]{1,0:T(8,128)(2,1)}, bf16[64,768]{1,0:T(8,128)(2,1)S(1)}, u32[]{:S(2)}) copy-start(bf16[64,768]{1,0:T(8,128)(2,1)S(1)} %collective-permute-done.22.refs_2_) | copy-start | bytes 294916
  99.4 15.1 %collective-permute-start.27 = (bf16[64,768]{1,0:T(8,128)(2,1)S(1)}, bf16[64,768]{1,0:T(8,128)(2,1)S(1)}, u32[]{:S(2)}, u32[]{:S(2)}) collective-permute-start(bf16[64,768]{1,0:T(8,128)(2,1)S(1)} %get-tuple-element.58), channel_id=1, source_target_pairs={{0,7},{1,6},{2,5},{3,4},{4,3},{5,2},{6,1},{7,0},{8,15},{9,14},{10,... | collective-permute-start | bytes 294920 | tf_op jit(solution)/shard_map/ppermute | solution.py:19
  101.8 8.1 %copy-start.16 = (bf16[64,768]{1,0:T(8,128)(2,1)}, bf16[64,768]{1,0:T(8,128)(2,1)S(1)}, u32[]{:S(2)}) copy-start(bf16[64,768]{1,0:T(8,128)(2,1)S(1)} %collective-permute-done.23.refs_3_) | copy-start | bytes 294916
  101.8 16.1 %collective-permute-start.12 = (bf16[64,768]{1,0:T(8,128)(2,1)S(1)}, bf16[64,768]{1,0:T(8,128)(2,1)S(1)}, u32[]{:S(2)}, u32[]{:S(2)}) collective-permute-start(bf16[64,768]{1,0:T(8,128)(2,1)S(1)} %get-tuple-element.44), channel_id=1, source_target_pairs={{0,1},{1,0},{2,3},{3,2},{4,5},{5,4},{6,7},{7,6},{8,9},{9,8},{10,11... | collective-permute-start | bytes 294920 | tf_op jit(solution)/shard_map/ppermute | solution.py:19
  107.4 2.4 %copy-start.17 = (bf16[64,768]{1,0:T(8,128)(2,1)}, bf16[64,768]{1,0:T(8,128)(2,1)S(1)}, u32[]{:S(2)}) copy-start(bf16[64,768]{1,0:T(8,128)(2,1)S(1)} %collective-permute-done.24.refs_4_) | copy-start | bytes 294916
  107.4 11.3 %collective-permute-start.13 = (bf16[64,768]{1,0:T(8,128)(2,1)S(1)}, bf16[64,768]{1,0:T(8,128)(2,1)S(1)}, u32[]{:S(2)}, u32[]{:S(2)}) collective-permute-start(bf16[64,768]{1,0:T(8,128)(2,1)S(1)} %get-tuple-element.45), channel_id=1, source_target_pairs={{0,2},{1,3},{2,0},{3,1},{4,6},{5,7},{6,4},{7,5},{8,10},{9,11},{10,... | collective-permute-start | bytes 294920 | tf_op jit(solution)/shard_map/ppermute | solution.py:19
  111.2 10.7 %copy-start.18 = (bf16[64,768]{1,0:T(8,128)(2,1)}, bf16[64,768]{1,0:T(8,128)(2,1)S(1)}, u32[]{:S(2)}) copy-start(bf16[64,768]{1,0:T(8,128)(2,1)S(1)} %collective-permute-done.25.refs_5_) | copy-start | bytes 294916
  111.2 16.6 %collective-permute-start.14 = (bf16[64,768]{1,0:T(8,128)(2,1)S(1)}, bf16[64,768]{1,0:T(8,128)(2,1)S(1)}, u32[]{:S(2)}, u32[]{:S(2)}) collective-permute-start(bf16[64,768]{1,0:T(8,128)(2,1)S(1)} %get-tuple-element.46), channel_id=1, source_target_pairs={{0,3},{1,2},{2,1},{3,0},{4,7},{5,6},{6,5},{7,4},{8,11},{9,10},{10,... | collective-permute-start | bytes 294920 | tf_op jit(solution)/shard_map/ppermute | solution.py:19
  111.2 10.7 %copy-start.19 = (bf16[64,768]{1,0:T(8,128)(2,1)}, bf16[64,768]{1,0:T(8,128)(2,1)S(1)}, u32[]{:S(2)}) copy-start(bf16[64,768]{1,0:T(8,128)(2,1)S(1)} %collective-permute-done.26.refs_6_) | copy-start | bytes 294916
  111.3 16.6 %collective-permute-start.15 = (bf16[64,768]{1,0:T(8,128)(2,1)S(1)}, bf16[64,768]{1,0:T(8,128)(2,1)S(1)}, u32[]{:S(2)}, u32[]{:S(2)}) collective-permute-start(bf16[64,768]{1,0:T(8,128)(2,1)S(1)} %get-tuple-element.47), channel_id=1, source_target_pairs={{0,4},{1,5},{2,6},{3,7},{4,0},{5,1},{6,2},{7,3},{8,12},{9,13},{10,... | collective-permute-start | bytes 294920 | tf_op jit(solution)/shard_map/ppermute | solution.py:19
  114.5 7.5 %copy-start.20 = (bf16[64,768]{1,0:T(8,128)(2,1)}, bf16[64,768]{1,0:T(8,128)(2,1)S(1)}, u32[]{:S(2)}) copy-start(bf16[64,768]{1,0:T(8,128)(2,1)S(1)} %collective-permute-done.27.refs_7_) | copy-start | bytes 294916
  114.5 13.8 %collective-permute-start.16 = (bf16[64,768]{1,0:T(8,128)(2,1)S(1)}, bf16[64,768]{1,0:T(8,128)(2,1)S(1)}, u32[]{:S(2)}, u32[]{:S(2)}) collective-permute-start(bf16[64,768]{1,0:T(8,128)(2,1)S(1)} %get-tuple-element.48), channel_id=1, source_target_pairs={{0,5},{1,4},{2,7},{3,6},{4,1},{5,0},{6,3},{7,2},{8,13},{9,12},{10,... | collective-permute-start | bytes 294920 | tf_op jit(solution)/shard_map/ppermute | solution.py:19
  117.9 9.9 %copy-start.7 = (bf16[64,768]{1,0:T(8,128)(2,1)}, bf16[64,768]{1,0:T(8,128)(2,1)S(1)}, u32[]{:S(2)}) copy-start(bf16[64,768]{1,0:T(8,128)(2,1)S(1)} %collective-permute-done.12.refs_1_) | copy-start | bytes 294916
  117.9 10.4 %collective-permute-start.17 = (bf16[64,768]{1,0:T(8,128)(2,1)S(1)}, bf16[64,768]{1,0:T(8,128)(2,1)S(1)}, u32[]{:S(2)}, u32[]{:S(2)}) collective-permute-start(bf16[64,768]{1,0:T(8,128)(2,1)S(1)} %get-tuple-element.49), channel_id=1, source_target_pairs={{0,6},{1,7},{2,4},{3,5},{4,2},{5,3},{6,0},{7,1},{8,14},{9,15},{10,... | collective-permute-start | bytes 294920 | tf_op jit(solution)/shard_map/ppermute | solution.py:19
  118.7 9.1 %copy-start.8 = (bf16[64,768]{1,0:T(8,128)(2,1)}, bf16[64,768]{1,0:T(8,128)(2,1)S(1)}, u32[]{:S(2)}) copy-start(bf16[64,768]{1,0:T(8,128)(2,1)S(1)} %collective-permute-done.13.refs_2_) | copy-start | bytes 294916
  118.7 9.6 %collective-permute-start.18 = (bf16[64,768]{1,0:T(8,128)(2,1)S(1)}, bf16[64,768]{1,0:T(8,128)(2,1)S(1)}, u32[]{:S(2)}, u32[]{:S(2)}) collective-permute-start(bf16[64,768]{1,0:T(8,128)(2,1)S(1)} %get-tuple-element.50), channel_id=1, source_target_pairs={{0,7},{1,6},{2,5},{3,4},{4,3},{5,2},{6,1},{7,0},{8,15},{9,14},{10,... | collective-permute-start | bytes 294920 | tf_op jit(solution)/shard_map/ppermute | solution.py:19
  127.8 0.6 copy-start.9
  127.8 0.7 copy-start.10
  128.3 0.7 copy-start.11
  128.3 0.7 copy-start.12
  128.3 0.7 copy-start.13
  135.1 1.8 %collective-permute-start.33 = (bf16[2,128,512]{2,1,0:T(8,128)(2,1)}, bf16[2,128,512]{2,1,0:T(8,128)(2,1)S(1)}, u32[]{:S(2)}, u32[]{:S(2)}) collective-permute-start(bf16[2,128,512]{2,1,0:T(8,128)(2,1)} %get-tuple-element.66), channel_id=1, source_target_pairs={{0,8},{8,0},{16,24},{24,16},{1,9},{9,1},{17,25},{25,17},{2,10},{10... | collective-permute-start | bytes 786440 | tf_op jit(solution)/shard_map/ppermute | solution.py:19
  135.3 4.4 %collective-permute-start.28 = (bf16[2,128,512]{2,1,0:T(8,128)(2,1)}, bf16[2,128,512]{2,1,0:T(8,128)(2,1)S(1)}, u32[]{:S(2)}, u32[]{:S(2)}) collective-permute-start(bf16[2,128,512]{2,1,0:T(8,128)(2,1)} %get-tuple-element.64), channel_id=1, source_target_pairs={{0,8},{8,0},{16,24},{24,16},{1,9},{9,1},{17,25},{25,17},{2,10},{10... | collective-permute-start | bytes 786440 | tf_op jit(solution)/shard_map/ppermute | solution.py:19
  138.1 5.9 %collective-permute-start.34 = (bf16[1,128,512]{2,1,0:T(8,128)(2,1)S(1)}, bf16[1,128,512]{2,1,0:T(8,128)(2,1)S(1)}, u32[]{:S(2)}, u32[]{:S(2)}) collective-permute-start(bf16[1,128,512]{2,1,0:T(8,128)(2,1)S(1)} %dynamic-slice_convert_fusion), channel_id=1, source_target_pairs={{0,16},{8,24},{16,0},{24,8},{1,17},{9,25},{17,1},{25,9},{2,18},{10... | collective-permute-start | bytes 393224 | tf_op jit(solution)/shard_map/ppermute | solution.py:19
  140.9 6.7 %collective-permute-start.29 = (bf16[1,128,512]{2,1,0:T(8,128)(2,1)S(1)}, bf16[1,128,512]{2,1,0:T(8,128)(2,1)S(1)}, u32[]{:S(2)}, u32[]{:S(2)}) collective-permute-start(bf16[1,128,512]{2,1,0:T(8,128)(2,1)S(1)} %dynamic-slice_convert_fusion.1), channel_id=1, source_target_pairs={{0,16},{8,24},{16,0},{24,8},{1,17},{9,25},{17,1},{25,9},{2,18},{10... | collective-permute-start | bytes 393224 | tf_op jit(solution)/shard_map/ppermute | solution.py:19
  144.1 6.4 %collective-permute-start.35 = (bf16[128,512]{1,0:T(8,128)(2,1)S(1)}, bf16[128,512]{1,0:T(8,128)(2,1)S(1)}, u32[]{:S(2)}, u32[]{:S(2)}) collective-permute-start(bf16[128,512]{1,0:T(8,128)(2,1)S(1)} %bitcast_convert_fusion), channel_id=1, source_target_pairs={{0,2},{1,3},{2,0},{3,1},{4,6},{5,7},{6,4},{7,5},{8,10},{9,11},{10,... | collective-permute-start | bytes 393224 | tf_op jit(solution)/shard_map/ppermute | solution.py:19
  147.6 5.5 %collective-permute-start.30 = (bf16[128,512]{1,0:T(8,128)(2,1)S(1)}, bf16[128,512]{1,0:T(8,128)(2,1)S(1)}, u32[]{:S(2)}, u32[]{:S(2)}) collective-permute-start(bf16[128,512]{1,0:T(8,128)(2,1)S(1)} %bitcast_convert_fusion.1), channel_id=1, source_target_pairs={{0,1},{1,0},{2,3},{3,2},{4,5},{5,4},{6,7},{7,6},{8,9},{9,8},{10,11... | collective-permute-start | bytes 393224 | tf_op jit(solution)/shard_map/ppermute | solution.py:19
  150.5 6.0 %collective-permute-start.36 = (bf16[128,512]{1,0:T(8,128)(2,1)S(1)}, bf16[128,512]{1,0:T(8,128)(2,1)S(1)}, u32[]{:S(2)}, u32[]{:S(2)}) collective-permute-start(bf16[128,512]{1,0:T(8,128)(2,1)S(1)} %get-tuple-element.67), channel_id=1, source_target_pairs={{0,4},{1,5},{2,6},{3,7},{4,0},{5,1},{6,2},{7,3},{8,12},{9,13},{10,... | collective-permute-start | bytes 393224 | tf_op jit(solution)/shard_map/ppermute | solution.py:19
  153.1 5.3 %collective-permute-start.31 = (bf16[128,512]{1,0:T(8,128)(2,1)S(1)}, bf16[128,512]{1,0:T(8,128)(2,1)S(1)}, u32[]{:S(2)}, u32[]{:S(2)}) collective-permute-start(bf16[128,512]{1,0:T(8,128)(2,1)S(1)} %get-tuple-element.69), channel_id=1, source_target_pairs={{0,2},{1,3},{2,0},{3,1},{4,6},{5,7},{6,4},{7,5},{8,10},{9,11},{10,... | collective-permute-start | bytes 393224 | tf_op jit(solution)/shard_map/ppermute | solution.py:19
  156.5 5.0 %collective-permute-start.37 = (bf16[128,512]{1,0:T(8,128)(2,1)S(1)}, bf16[128,512]{1,0:T(8,128)(2,1)S(1)}, u32[]{:S(2)}, u32[]{:S(2)}) collective-permute-start(bf16[128,512]{1,0:T(8,128)(2,1)S(1)} %fusion.2), channel_id=1, source_target_pairs={{0,1},{1,0},{2,3},{3,2},{4,5},{5,4},{6,7},{7,6},{8,9},{9,8},{10,11... | collective-permute-start | bytes 393224 | tf_op jit(solution)/shard_map/ppermute | solution.py:19
  158.4 8.1 %collective-permute-start.32 = (bf16[128,512]{1,0:T(8,128)(2,1)S(1)}, bf16[128,512]{1,0:T(8,128)(2,1)S(1)}, u32[]{:S(2)}, u32[]{:S(2)}) collective-permute-start(bf16[128,512]{1,0:T(8,128)(2,1)S(1)} %fusion.1), channel_id=1, source_target_pairs={{0,4},{1,5},{2,6},{3,7},{4,0},{5,1},{6,2},{7,3},{8,12},{9,13},{10,... | collective-permute-start | bytes 393224 | tf_op jit(solution)/shard_map/ppermute | solution.py:19

commit v3 on v2

--- a/solution.py
+++ b/solution.py
@@ -25,11 +25,12 @@
     return [1 << k for k in range(size.bit_length() - 1)]
 
 
-def pack_kernel(at, tiles_hbm, peer, src, dst, name, packed_ref, tiles_ref, turned_ref, lists_ref, info_ref, sem):
+def pack_kernel(tiles_hbm, peer, src, dst, name, packed_ref, tiles_ref, turned_ref, lists_ref, info_ref, sem):
     per, tile, _ = tiles_ref.shape
     piece = packed_ref.shape[0] - info_ref.shape[0]
     edges = src.shape[1]
-    first = at[1] * per if per < tiles_hbm.shape[0] else 0
+    own = lax.axis_index("cfg")
+    first = own * per if per < tiles_hbm.shape[0] else 0
     fetches = [pltpu.make_async_copy(tiles_hbm.at[pl.ds(first, per)], tiles_ref, sem.at[0])]
     for row, ref in enumerate((peer, src, dst, name)):
         fetches.append(pltpu.make_async_copy(ref, lists_ref.at[row], sem.at[1 + row]))
@@ -44,7 +45,7 @@
     else:
         for i in range(per):
             turned_ref[i * tile : (i + 1) * tile] = tiles_ref[i].T
-        packed_ref[:piece] = turned_ref[pl.ds(pl.multiple_of(at[1] * piece, piece), piece)]
+        packed_ref[:piece] = turned_ref[pl.ds(pl.multiple_of(own * piece, piece), piece)]
     for row in range(4):
         info_ref[row : row + 1, :edges] = lists_ref[row].astype(F32)
     packed_ref[piece:] = info_ref[...].astype(BF16)
@@ -90,7 +91,7 @@
     return out
 
 
-def edges_kernel(slots, first, chunks, at, meta, *refs):
+def edges_kernel(slots, first, spans, at, meta, *refs):
     x_refs = refs[: len(slots)]
     tiles_ref = refs[len(slots)]
     rest = refs[len(slots) + 1 :]
@@ -98,7 +99,7 @@
     edges = meta.shape[2]
     _, rows = x_refs[0].shape
     blocks = rows // tile
-    if first and chunks:
+    if first and spans:
         out_refs, acc_ref = rest[:-1], rest[-1]
         acc_ref[...] = jnp.zeros_like(acc_ref)
     elif first:
@@ -116,29 +117,30 @@
                 values.append(value.astype(BF16).astype(F32))
             for i, value in enumerate(values):
                 acc_ref[meta[slot, 1, base + i]] += value
-    span = blocks // max(chunks, 1)
     peers = meta.shape[0]
-    for chunk in range(chunks):
+    begin = 0
+    for chunk, span in enumerate(spans):
         for k in range(peers):
-            start = (at[0] ^ k) * blocks + chunk * span
+            start = (at[0] ^ k) * blocks + begin
             for block in range(span):
                 out_refs[chunk * peers + k][:, block * tile : (block + 1) * tile] = acc_ref[
                     start + block
                 ].astype(BF16)
-
-
-def sum_edges(at, meta, xs, slots, tiles, held, chunks):
+        begin += span
+
+
+def sum_edges(at, meta, xs, slots, tiles, held, spans):
     part, rows = xs[0].shape
     peers, _, edges = meta.shape
     total = (peers * (rows // LANES), part, LANES)
-    if chunks:
-        shapes = [jax.ShapeDtypeStruct((part, rows // chunks), BF16)] * (chunks * peers)
+    if spans:
+        shapes = [jax.ShapeDtypeStruct((part, n * LANES), BF16) for n in spans for _ in range(peers)]
         scratch = [pltpu.VMEM(total, F32)]
     else:
         shapes, scratch = [jax.ShapeDtypeStruct(total, F32)], []
     operands = list(xs) + [tiles] + ([] if held is None else [held])
     return pl.pallas_call(
-        functools.partial(edges_kernel, slots, held is None, chunks),
+        functools.partial(edges_kernel, slots, held is None, spans),
         out_shape=shapes,
         grid_spec=pltpu.PrefetchScalarGridSpec(
             num_scalar_prefetch=2,
@@ -303,7 +305,8 @@
     own = lax.axis_index("cfg")
     at = jnp.stack([lax.axis_index("dom"), own]).astype(I32)
     blocks = rows // tile
-    chunks = 2 if blocks % 2 == 0 else 1
+    spans = [blocks - blocks // 2, blocks // 2] if blocks > 2 else [blocks]
+    chunks = len(spans)
     dom_bits, cfg_bits = bits_of("dom"), bits_of("cfg")
     middle = peers // 2
 
@@ -313,7 +316,7 @@
         pack_kernel,
         out_shape=jax.ShapeDtypeStruct((piece + 16, tile), BF16),
         grid_spec=pltpu.PrefetchScalarGridSpec(
-            num_scalar_prefetch=1,
+            num_scalar_prefetch=0,
             grid=(),
             in_specs=[STAYS] * 5,
             out_specs=WHOLE,
@@ -329,14 +332,14 @@
         name="pack",
     )
     lists = [each.reshape(1, edges) for each in (edge_peer, edge_src, edge_dst, edge_tile)]
-    packed = pack(at, tiles, *lists)
+    packed = pack(tiles, *lists)
     far_turned = turn_half(at, feats, peers, 1)
     near_turned = turn_half(at, feats, peers, 0)
 
-    held, offsets = packed[None], [0]
-    for bit in dom_bits[::-1]:
-        held = jnp.concatenate([held, swap(held, "dom", bit)], 0)
-        offsets = offsets + [k ^ bit for k in offsets]
+    evens = [k for k in range(peers) if k % 2 == 0]
+    held = jnp.stack([packed] + [swap(packed, "dom", k) for k in evens[1:]])
+    held = jnp.concatenate([held, swap(held, "dom", 1)], 0)
+    offsets = evens + [k + 1 for k in evens]
     slot = {k: offsets.index(k) for k in range(peers)}
     quarters = held[:, :piece]
     pieces = jnp.concatenate([quarters[None], swap(quarters[None], "cfg", cfg_bits[-1])], 0)
@@ -367,28 +370,30 @@
     weights = weights[order].reshape(width, 2 * width)
 
     near, far = list(range(middle)), list(range(middle, peers))
-    partly = sum_edges(at, meta, [moved[k] for k in near], [slot[k] for k in near], all_tiles, None, 0)[0]
-    summed = sum_edges(at, meta, [moved[k] for k in far], [slot[k] for k in far], all_tiles, partly, chunks)
+    partly = sum_edges(at, meta, [moved[k] for k in near], [slot[k] for k in near], all_tiles, None, [])[0]
+    summed = sum_edges(at, meta, [moved[k] for k in far], [slot[k] for k in far], all_tiles, partly, spans)
     held = hidden = None
-    span = rows // chunks
     for chunk in range(chunks):
         parts = summed[chunk * peers : (chunk + 1) * peers]
         back = [parts[0]] + [swap(parts[k], "dom", k) for k in range(1, peers)]
         hidden, *held = run_head(
-            at, back, feats, cot, weights, hidden, held, chunk * span, span, configs
+            at, back, feats, cot, weights, hidden, held, sum(spans[:chunk]) * tile, spans[chunk] * tile, configs
         )
     keep_s, keep_n, give_s, give_n = held
     factor = float(configs * peers * rows) ** (-0.5)
 
     def reduce(keep, give, order):
-        total = keep + swap(give, "cfg", cfg_bits[0]).astype(F32)
+        here = [keep, swap(give, "cfg", cfg_bits[0])]
         for bit in cfg_bits[1:]:
-            pairs = total.reshape((total.shape[0] // 2, 2) + total.shape[1:])
             side = (own // bit) % 2
-            keep = lax.dynamic_index_in_dim(pairs, side, 1, keepdims=False)
-            give = lax.dynamic_index_in_dim(pairs, 1 - side, 1, keepdims=False)
-            total = keep + swap(give.astype(BF16), "cfg", bit).astype(F32)
-        total = total[0]
+
+            def pick(which):
+                halves = [each.reshape((each.shape[0] // 2, 2) + each.shape[1:]) for each in here]
+                halves = [lax.dynamic_index_in_dim(each, which, 1, keepdims=False) for each in halves]
+                return halves[0] + halves[1].astype(F32)
+
+            here = [pick(side), swap(pick(1 - side).astype(BF16), "cfg", bit)]
+        total = (here[0] + here[1].astype(F32))[0]
         for bit in order:
             total = total + swap(total.astype(BF16), "dom", bit).astype(F32)
         return total * factor

time: 168 us -> 163 us (0.970)
  starting transfers between devices: 74.8 us -> 68.3 us
  local copies, waits for them, and re-layouts: 3.72 us -> 5.46 us
    ppermute x38 -> x39, starting transfers between devices: 74.8 us -> 68.3 us  [swap(): return lax.ppermute(value, axis, [(i, i ^ bits) for i in range(size)])]
    add x2 -> x0, other arithmetic: 2.23 us -> none  [reduce(): total = keep + swap(give, 'cfg', cfg_bits[0]).astype(F32)]
    convert_element_type x0 -> x2, other arithmetic: none -> 1.95 us  [reduce(): here = [pick(side), swap(pick(1 - side).astype(BF16), 'cfg', bit)]]
    concatenate x2 -> x0, other arithmetic: 1.81 us -> none  [layer(): held = jnp.concatenate([held, swap(held, 'dom', bit)], 0)]
    unnamed x42 -> x48, local copies, waits for them, and re-layouts: 2.04 us -> 3.77 us
    ppermute x38 -> x39, waiting for transfers between devices: 59.2 us -> 58.8 us  [swap(): return lax.ppermute(value, axis, [(i, i ^ bits) for i in range(size)])]
  transfers between devices with their start and end apart: 38 -> 39, of which waited for: 19 -> 17; matrix products, arithmetic and copies ran while one was open for 3% -> 6% of each run, Pallas kernels for 7% -> 8%
where the time goes in v3:
time: 163 us
  starting transfers between devices  68.3 us (42%)
  waiting for transfers between devices  58.8 us (36%)
  Pallas kernels  19.9 us (12%)
  other arithmetic  9.21 us (6%)
  local copies, waits for them, and re-layouts  5.46 us (3%)
    ppermute x39, starting transfers between devices, swap(): return lax.ppermute(value, axis, [(i, i ^ bits) for i in range(size)])  68.3 us
    ppermute x39, waiting for transfers between devices, swap(): return lax.ppermute(value, axis, [(i, i ^ bits) for i in range(size)])  58.8 us
    pallas_call x2, Pallas kernels, run_head(): pl.pallas_call(functools.partial(head_kernel, peers, base, first, last),...  12 us
    pallas_call x2, Pallas kernels, sum_edges(): pl.pallas_call(functools.partial(edges_kernel, slots, held is None, spans...  4.64 us
    unnamed x48, local copies, waits for them, and re-layouts  3.77 us
  transfers between devices with their start and end apart: 39, of which 17 were waited for; matrix products, arithmetic and copies ran while one was open for 6% of the time, Pallas kernels for 8%

profile of v3, /device:TPU:0, one launch (start us, length us, event | category | flops | bytes accessed | tf_op | source)
XLA Modules:
  0.0 162.7 jit_solution(10233726544578321095)
XLA Ops:
  0.6 1.6 pack.1
  2.2 3.1 %collective-permute-start = (bf16[272,128]{1,0:T(8,128)(2,1)}, bf16[272,128]{1,0:T(8,128)(2,1)S(1)}, u32[]{:S(2)}, u32[]{:S(2)}) collective-permute-start(bf16[272,128]{1,0:T(8,128)(2,1)} %pack.1), channel_id=1, source_target_pairs={{0,2},{1,3},{2,0},{3,1},{4,6},{5,7},{6,4},{7,5},{8,10},{9,11},{10,... | collective-permute-start | bytes 208904 | tf_op jit(solution)/shard_map/ppermute | solution.py:19
  5.4 2.6 %collective-permute-start.1 = (bf16[272,128]{1,0:T(8,128)(2,1)}, bf16[272,128]{1,0:T(8,128)(2,1)S(1)}, u32[]{:S(2)}, u32[]{:S(2)}) collective-permute-start(bf16[272,128]{1,0:T(8,128)(2,1)} %pack.1), channel_id=1, source_target_pairs={{0,4},{1,5},{2,6},{3,7},{4,0},{5,1},{6,2},{7,3},{8,12},{9,13},{10,... | collective-permute-start | bytes 208904 | tf_op jit(solution)/shard_map/ppermute | solution.py:19
  8.0 1.0 constant_dynamic-update-slice_fusion.4
  8.9 4.2 %collective-permute-done.1 = bf16[272,128]{1,0:T(8,128)(2,1)S(1)} collective-permute-done((bf16[272,128]{1,0:T(8,128)(2,1)}, bf16[272,128]{1,0:T(8,128)(2,1)S(1)}, u32[]{:S(2)}, u32[]{:S(2)}) %collective-permute-start.1) | collective-permute-done | bytes 69664 | tf_op jit(solution)/shard_map/ppermute | solution.py:19
  13.1 1.3 collective-permute-done.2
  14.4 0.9 pad_maximum_fusion.4
  15.3 1.6 collective-permute-start.3
  16.9 5.0 %collective-permute-done.3 = bf16[4,272,128]{2,1,0:T(8,128)(2,1)S(1)} collective-permute-done((bf16[4,272,128]{2,1,0:T(8,128)(2,1)S(1)}, bf16[4,272,128]{2,1,0:T(8,128)(2,1)S(1)}, u32[]{:S(2)}, u32[]{:S(2)}) %collective-permute-start.3) | collective-permute-done | bytes 278560 | tf_op jit(solution)/shard_map/ppermute | solution.py:19
  22.1 0.8 copy-done.4
  22.8 1.5 collective-permute-start.8
  24.3 9.5 %collective-permute-done.8 = bf16[1,8,256,128]{3,2,1,0:T(8,128)(2,1)S(1)} collective-permute-done((bf16[1,8,256,128]{3,2,1,0:T(8,128)(2,1)S(1)}, bf16[1,8,256,128]{3,2,1,0:T(8,128)(2,1)S(1)}, u32[]{:S(2)}, u32[]{:S(2)}) %collective-permute-start.8) | collective-permute-done | bytes 524320 | tf_op jit(solution)/shard_map/ppermute | solution.py:19
  33.8 1.1 pad_maximum_fusion.1
  34.9 1.6 collective-permute-start.20
  36.6 0.9 shard_map.113
  37.5 1.6 collective-permute-start.10
  39.0 1.3 collective-permute-start.11
  40.3 0.7 collective-permute-start.12
  41.0 0.9 shard_map.112
  41.9 1.8 %collective-permute-done.20 = bf16[1,128,1024]{2,1,0:T(8,128)(2,1)S(1)} collective-permute-done((bf16[1,128,1024]{2,1,0:T(8,128)(2,1)S(1)}, bf16[1,128,1024]{2,1,0:T(8,128)(2,1)S(1)}, u32[]{:S(2)}, u32[]{:S(2)}) %collective-permute-start.20) | collective-permute-done | bytes 262176 | tf_op jit(solution)/shard_map/ppermute | solution.py:19
  43.8 0.7 slice_convert_fusion
  44.7 3.2 %collective-permute-start.4 = (bf16[64,1536]{1,0:T(8,128)(2,1)S(1)}, bf16[64,1536]{1,0:T(8,128)(2,1)S(1)}, u32[]{:S(2)}, u32[]{:S(2)}) collective-permute-start(bf16[64,1536]{1,0:T(8,128)(2,1)S(1)} %get-tuple-element.35), channel_id=1, source_target_pairs={{0,4},{1,5},{2,6},{3,7},{4,0},{5,1},{6,2},{7,3},{8,12},{9,13},{10,... | collective-permute-start | bytes 589832 | tf_op jit(solution)/shard_map/ppermute | solution.py:19
  47.9 2.0 %collective-permute-start.5 = (bf16[64,1536]{1,0:T(8,128)(2,1)S(1)}, bf16[64,1536]{1,0:T(8,128)(2,1)S(1)}, u32[]{:S(2)}, u32[]{:S(2)}) collective-permute-start(bf16[64,1536]{1,0:T(8,128)(2,1)S(1)} %get-tuple-element.36), channel_id=1, source_target_pairs={{0,5},{1,4},{2,7},{3,6},{4,1},{5,0},{6,3},{7,2},{8,13},{9,12},{10,... | collective-permute-start | bytes 589832 | tf_op jit(solution)/shard_map/ppermute | solution.py:19
  49.9 5.9 %collective-permute-start.6 = (bf16[64,1536]{1,0:T(8,128)(2,1)S(1)}, bf16[64,1536]{1,0:T(8,128)(2,1)S(1)}, u32[]{:S(2)}, u32[]{:S(2)}) collective-permute-start(bf16[64,1536]{1,0:T(8,128)(2,1)S(1)} %get-tuple-element.37), channel_id=1, source_target_pairs={{0,6},{1,7},{2,4},{3,5},{4,2},{5,3},{6,0},{7,1},{8,14},{9,15},{10,... | collective-permute-start | bytes 589832 | tf_op jit(solution)/shard_map/ppermute | solution.py:19
  55.9 1.8 %collective-permute-start.7 = (bf16[64,1536]{1,0:T(8,128)(2,1)S(1)}, bf16[64,1536]{1,0:T(8,128)(2,1)S(1)}, u32[]{:S(2)}, u32[]{:S(2)}) collective-permute-start(bf16[64,1536]{1,0:T(8,128)(2,1)S(1)} %get-tuple-element.38), channel_id=1, source_target_pairs={{0,7},{1,6},{2,5},{3,4},{4,3},{5,2},{6,1},{7,0},{8,15},{9,14},{10,... | collective-permute-start | bytes 589832 | tf_op jit(solution)/shard_map/ppermute | solution.py:19
  57.7 1.4 pad_maximum_fusion
  59.1 2.2 %shard_map.114.refs_5_ = f32[96,64,128]{2,1,0:T(8,128)S(1)} custom-call(s32[2]{0:T(128)S(1)} %pad_add_fusion.1.at, s32[8,3,32]{2,1,0:T(4,128)S(1)} %pad_add_fusion.meta, bf16[64,1536]{1,0:T(8,128)(2,1)S(1)} %get-tuple-element.39.refs_0_, bf16[64,1536]{1,0:T(8,128)(2,1)S(1)} %collective-permute-done.10.refs_1_, ...), custom_call_target="tpu_custom_call" | custom-call | flops 268435456 | bytes 1835008 | tf_op jit(solution)/shard_map/pallas_call | solution.py:142
  61.3 9.3 %collective-permute-done.4.refs_0_ = bf16[64,1536]{1,0:T(8,128)(2,1)S(1)} collective-permute-done((bf16[64,1536]{1,0:T(8,128)(2,1)S(1)}, bf16[64,1536]{1,0:T(8,128)(2,1)S(1)}, u32[]{:S(2)}, u32[]{:S(2)}) %collective-permute-start.4) | collective-permute-done | bytes 196640 | tf_op jit(solution)/shard_map/ppermute | solution.py:19
  70.5 5.1 %collective-permute-done.5.refs_1_ = bf16[64,1536]{1,0:T(8,128)(2,1)S(1)} collective-permute-done((bf16[64,1536]{1,0:T(8,128)(2,1)S(1)}, bf16[64,1536]{1,0:T(8,128)(2,1)S(1)}, u32[]{:S(2)}, u32[]{:S(2)}) %collective-permute-start.5) | collective-permute-done | bytes 196640 | tf_op jit(solution)/shard_map/ppermute | solution.py:19
  75.6 2.5 %shard_map.115 = (bf16[64,768]{1,0:T(8,128)(2,1)S(1)}, bf16[64,768]{1,0:T(8,128)(2,1)S(1)}, bf16[64,768]{1,0:T(8,128)(2,1)S(1)}, bf16[64,768]{1,0:T(8,128)(2,1)S...) custom-call(s32[2]{0:T(128)S(1)} %pad_add_fusion.1.at, ...), custom_call_target="tpu_custom_call" | custom-call | flops 268435456 | bytes 1835008 | tf_op jit(solution)/shard_map/pallas_call | solution.py:142
  80.0 8.8 %collective-permute-start.23 = (bf16[64,768]{1,0:T(8,128)(2,1)S(1)}, bf16[64,768]{1,0:T(8,128)(2,1)S(1)}, u32[]{:S(2)}, u32[]{:S(2)}) collective-permute-start(bf16[64,768]{1,0:T(8,128)(2,1)S(1)} %get-tuple-element.53), channel_id=1, source_target_pairs={{0,2},{1,3},{2,0},{3,1},{4,6},{5,7},{6,4},{7,5},{8,10},{9,11},{10,... | collective-permute-start | bytes 294920 | tf_op jit(solution)/shard_map/ppermute | solution.py:19
  88.8 0.9 collective-permute-start.24
  89.6 1.1 collective-permute-start.25
  90.8 1.9 %collective-permute-start.26 = (bf16[64,768]{1,0:T(8,128)(2,1)S(1)}, bf16[64,768]{1,0:T(8,128)(2,1)S(1)}, u32[]{:S(2)}, u32[]{:S(2)}) collective-permute-start(bf16[64,768]{1,0:T(8,128)(2,1)S(1)} %get-tuple-element.56), channel_id=1, source_target_pairs={{0,5},{1,4},{2,7},{3,6},{4,1},{5,0},{6,3},{7,2},{8,13},{9,12},{10,... | collective-permute-start | bytes 294920 | tf_op jit(solution)/shard_map/ppermute | solution.py:19
  92.7 1.5 collective-permute-start.27
  94.2 3.2 %collective-permute-start.28 = (bf16[64,768]{1,0:T(8,128)(2,1)S(1)}, bf16[64,768]{1,0:T(8,128)(2,1)S(1)}, u32[]{:S(2)}, u32[]{:S(2)}) collective-permute-start(bf16[64,768]{1,0:T(8,128)(2,1)S(1)} %get-tuple-element.58), channel_id=1, source_target_pairs={{0,7},{1,6},{2,5},{3,4},{4,3},{5,2},{6,1},{7,0},{8,15},{9,14},{10,... | collective-permute-start | bytes 294920 | tf_op jit(solution)/shard_map/ppermute | solution.py:19
  98.0 6.4 %collective-permute-done.25.refs_4_ = bf16[64,768]{1,0:T(8,128)(2,1)S(1)} collective-permute-done((bf16[64,768]{1,0:T(8,128)(2,1)S(1)}, bf16[64,768]{1,0:T(8,128)(2,1)S(1)}, u32[]{:S(2)}, u32[]{:S(2)}) %collective-permute-start.25) | collective-permute-done | bytes 98336 | tf_op jit(solution)/shard_map/ppermute | solution.py:19
  104.5 1.6 gather_fusion
  106.6 1.8 %collective-permute-start.15 = (bf16[64,768]{1,0:T(8,128)(2,1)S(1)}, bf16[64,768]{1,0:T(8,128)(2,1)S(1)}, u32[]{:S(2)}, u32[]{:S(2)}) collective-permute-start(bf16[64,768]{1,0:T(8,128)(2,1)S(1)} %get-tuple-element.46), channel_id=1, source_target_pairs={{0,3},{1,2},{2,1},{3,0},{4,7},{5,6},{6,5},{7,4},{8,11},{9,10},{10,... | collective-permute-start | bytes 294920 | tf_op jit(solution)/shard_map/ppermute | solution.py:19
  108.4 0.8 collective-permute-start.16
  109.2 2.8 %collective-permute-start.17 = (bf16[64,768]{1,0:T(8,128)(2,1)S(1)}, bf16[64,768]{1,0:T(8,128)(2,1)S(1)}, u32[]{:S(2)}, u32[]{:S(2)}) collective-permute-start(bf16[64,768]{1,0:T(8,128)(2,1)S(1)} %get-tuple-element.48), channel_id=1, source_target_pairs={{0,5},{1,4},{2,7},{3,6},{4,1},{5,0},{6,3},{7,2},{8,13},{9,12},{10,... | collective-permute-start | bytes 294920 | tf_op jit(solution)/shard_map/ppermute | solution.py:19
  112.1 2.9 %collective-permute-start.18 = (bf16[64,768]{1,0:T(8,128)(2,1)S(1)}, bf16[64,768]{1,0:T(8,128)(2,1)S(1)}, u32[]{:S(2)}, u32[]{:S(2)}) collective-permute-start(bf16[64,768]{1,0:T(8,128)(2,1)S(1)} %get-tuple-element.49), channel_id=1, source_target_pairs={{0,6},{1,7},{2,4},{3,5},{4,2},{5,3},{6,0},{7,1},{8,14},{9,15},{10,... | collective-permute-start | bytes 294920 | tf_op jit(solution)/shard_map/ppermute | solution.py:19
  115.0 1.2 collective-permute-start.19
  116.3 5.9 %shard_map.116 = (bf16[1536,512]{1,0:T(8,128)(2,1)}, f32[512,512]{1,0:T(8,128)}, f32[512,512]{1,0:T(8,128)}) custom-call(s32[2]{0:T(128)} %copy-done.2, bf16[64,768]{1,0:T(8,128)(2,1)} %copy-done.3, bf16[64,768]{1,0:T(8,128)(2,1)} %copy-done.15, bf16[64,768]{1,0:T(8,128)(2,1)} %copy-done.16, bf16[64,768]{1,0:T(8,128)(2,1)} %copy-done.17, ...), custom_call_target="tpu_custom_call" | custom-call | flops 1610612736 | bytes 3145728 | tf_op jit(solution)/shard_map/pallas_call | solution.py:273
  122.2 2.4 %collective-permute-done.17.refs_5_ = bf16[64,768]{1,0:T(8,128)(2,1)S(1)} collective-permute-done((bf16[64,768]{1,0:T(8,128)(2,1)S(1)}, bf16[64,768]{1,0:T(8,128)(2,1)S(1)}, u32[]{:S(2)}, u32[]{:S(2)}) %collective-permute-start.17) | collective-permute-done | bytes 98336 | tf_op jit(solution)/shard_map/ppermute | solution.py:19
  125.3 6.1 %shard_map.117 = (bf16[1536,512]{1,0:T(8,128)(2,1)}, f32[2,128,512]{2,1,0:T(8,128)}, f32[2,128,512]{2,1,0:T(8,128)}, bf16[2,128,512]{2,1,0:T(8,128)(2,1)}, bf16[2,128,512]{2,1,0:T(8,128)(2,1)}) custom-call(s32[2]{0:T(128)} %copy-done.2, bf16[64,768]{1,0:T(8,128)(2,1)} %copy-done.1, bf16[64,768]{1,0:T(8,128)(2,1)} %copy-done.8, ...), custom_call_target="tpu_custom_call", output_to_operand_aliasing={{0}: (12, {})} | custom-call | flops 1610612736 | bytes 3145728 | tf_op jit(solution)/shard_map/pallas_call | solution.py:273
  132.0 1.2 collective-permute-done.34
  133.2 1.0 add_convert_fusion
  134.2 1.6 collective-permute-start.35
  135.8 1.0 add_convert_fusion.1
  137.4 3.0 %collective-permute-done.35 = bf16[1,128,512]{2,1,0:T(8,128)(2,1)S(1)} collective-permute-done((bf16[1,128,512]{2,1,0:T(8,128)(2,1)S(1)}, bf16[1,128,512]{2,1,0:T(8,128)(2,1)S(1)}, u32[]{:S(2)}, u32[]{:S(2)}) %collective-permute-start.35) | collective-permute-done | bytes 131104 | tf_op jit(solution)/shard_map/ppermute | solution.py:19
  140.4 1.0 bitcast_convert_fusion
  141.4 2.7 %collective-permute-start.36 = (bf16[128,512]{1,0:T(8,128)(2,1)S(1)}, bf16[128,512]{1,0:T(8,128)(2,1)S(1)}, u32[]{:S(2)}, u32[]{:S(2)}) collective-permute-start(bf16[128,512]{1,0:T(8,128)(2,1)S(1)} %get-tuple-element.67), channel_id=1, source_target_pairs={{0,2},{1,3},{2,0},{3,1},{4,6},{5,7},{6,4},{7,5},{8,10},{9,11},{10,... | collective-permute-start | bytes 393224 | tf_op jit(solution)/shard_map/ppermute | solution.py:19
  144.2 1.1 collective-permute-start.31
  145.3 1.8 %collective-permute-done.36 = bf16[128,512]{1,0:T(8,128)(2,1)S(1)} collective-permute-done((bf16[128,512]{1,0:T(8,128)(2,1)S(1)}, bf16[128,512]{1,0:T(8,128)(2,1)S(1)}, u32[]{:S(2)}, u32[]{:S(2)}) %collective-permute-start.36) | collective-permute-done | bytes 131104 | tf_op jit(solution)/shard_map/ppermute | solution.py:19
  147.1 2.4 %collective-permute-start.37 = (bf16[128,512]{1,0:T(8,128)(2,1)S(1)}, bf16[128,512]{1,0:T(8,128)(2,1)S(1)}, u32[]{:S(2)}, u32[]{:S(2)}) collective-permute-start(bf16[128,512]{1,0:T(8,128)(2,1)S(1)} %fusion.3), channel_id=1, source_target_pairs={{0,4},{1,5},{2,6},{3,7},{4,0},{5,1},{6,2},{7,3},{8,12},{9,13},{10,... | collective-permute-start | bytes 393224 | tf_op jit(solution)/shard_map/ppermute | solution.py:19
  149.5 1.0 collective-permute-start.32
  150.5 2.5 %collective-permute-done.37 = bf16[128,512]{1,0:T(8,128)(2,1)S(1)} collective-permute-done((bf16[128,512]{1,0:T(8,128)(2,1)S(1)}, bf16[128,512]{1,0:T(8,128)(2,1)S(1)}, u32[]{:S(2)}, u32[]{:S(2)}) %collective-permute-start.37) | collective-permute-done | bytes 131104 | tf_op jit(solution)/shard_map/ppermute | solution.py:19
  153.1 1.1 collective-permute-start.38
  154.6 2.2 %collective-permute-start.33 = (bf16[128,512]{1,0:T(8,128)(2,1)S(1)}, bf16[128,512]{1,0:T(8,128)(2,1)S(1)}, u32[]{:S(2)}, u32[]{:S(2)}) collective-permute-start(bf16[128,512]{1,0:T(8,128)(2,1)S(1)} %fusion), channel_id=1, source_target_pairs={{0,4},{1,5},{2,6},{3,7},{4,0},{5,1},{6,2},{7,3},{8,12},{9,13},{10,... | collective-permute-start | bytes 393224 | tf_op jit(solution)/shard_map/ppermute | solution.py:19
  156.8 1.3 collective-permute-done.38
  158.1 0.8 add_multiply_fusion
  158.9 3.1 %collective-permute-done.33 = bf16[128,512]{1,0:T(8,128)(2,1)S(1)} collective-permute-done((bf16[128,512]{1,0:T(8,128)(2,1)S(1)}, bf16[128,512]{1,0:T(8,128)(2,1)S(1)}, u32[]{:S(2)}, u32[]{:S(2)}) %collective-permute-start.33) | collective-permute-done | bytes 131104 | tf_op jit(solution)/shard_map/ppermute | solution.py:19
  161.9 0.8 add_multiply_fusion.1
  (94 shorter events, 6.1 us)
Async XLA Ops:
  2.2 6.7 %collective-permute-start = (bf16[272,128]{1,0:T(8,128)(2,1)}, bf16[272,128]{1,0:T(8,128)(2,1)S(1)}, u32[]{:S(2)}, u32[]{:S(2)}) collective-permute-start(bf16[272,128]{1,0:T(8,128)(2,1)} %pack.1), channel_id=1, source_target_pairs={{0,2},{1,3},{2,0},{3,1},{4,6},{5,7},{6,4},{7,5},{8,10},{9,11},{10,... | collective-permute-start | bytes 208904 | tf_op jit(solution)/shard_map/ppermute | solution.py:19
  5.4 7.8 %collective-permute-start.1 = (bf16[272,128]{1,0:T(8,128)(2,1)}, bf16[272,128]{1,0:T(8,128)(2,1)S(1)}, u32[]{:S(2)}, u32[]{:S(2)}) collective-permute-start(bf16[272,128]{1,0:T(8,128)(2,1)} %pack.1), channel_id=1, source_target_pairs={{0,4},{1,5},{2,6},{3,7},{4,0},{5,1},{6,2},{7,3},{8,12},{9,13},{10,... | collective-permute-start | bytes 208904 | tf_op jit(solution)/shard_map/ppermute | solution.py:19
  7.9 6.4 %collective-permute-start.2 = (bf16[272,128]{1,0:T(8,128)(2,1)}, bf16[272,128]{1,0:T(8,128)(2,1)S(1)}, u32[]{:S(2)}, u32[]{:S(2)}) collective-permute-start(bf16[272,128]{1,0:T(8,128)(2,1)} %pack.1), channel_id=1, source_target_pairs={{0,6},{1,7},{2,4},{3,5},{4,2},{5,3},{6,0},{7,1},{8,14},{9,15},{10,... | collective-permute-start | bytes 208904 | tf_op jit(solution)/shard_map/ppermute | solution.py:19
  15.3 19.6 %copy-start.6 = (bf16[128,512]{1,0:T(8,128)(2,1)S(1)}, bf16[128,512]{1,0:T(8,128)(2,1)}, u32[]{:S(2)}) copy-start(bf16[128,512]{1,0:T(8,128)(2,1)} %param.12) | copy-start | bytes 393220
  15.3 19.6 %copy-start.7 = (bf16[128,512]{1,0:T(8,128)(2,1)S(1)}, bf16[128,512]{1,0:T(8,128)(2,1)}, u32[]{:S(2)}) copy-start(bf16[128,512]{1,0:T(8,128)(2,1)} %param.11) | copy-start | bytes 393220
  15.3 6.7 %collective-permute-start.3 = (bf16[4,272,128]{2,1,0:T(8,128)(2,1)S(1)}, bf16[4,272,128]{2,1,0:T(8,128)(2,1)S(1)}, u32[]{:S(2)}, u32[]{:S(2)}) collective-permute-start(bf16[4,272,128]{2,1,0:T(8,128)(2,1)S(1)} %pad_maximum_fusion.4), channel_id=1, source_target_pairs={{0,1},{1,0},{2,3},{3,2},{4,5},{5,4},{6,7},{7,6},{8,9},{9,8},{10,11... | collective-permute-start | bytes 835592 | tf_op jit(solution)/shard_map/ppermute | solution.py:19
  16.9 19.7 %copy-start = (bf16[1,1536,512]{2,1,0:T(8,128)(2,1)S(1)}, bf16[1,1536,512]{2,1,0:T(8,128)(2,1)}, u32[]{:S(2)}) copy-start(bf16[1,1536,512]{2,1,0:T(8,128)(2,1)} %param.9) | copy-start | bytes 4718596
  22.0 0.8 copy-start.4
  22.8 11.0 %collective-permute-start.8 = (bf16[1,8,256,128]{3,2,1,0:T(8,128)(2,1)S(1)}, bf16[1,8,256,128]{3,2,1,0:T(8,128)(2,1)S(1)}, u32[]{:S(2)}, u32[]{:S(2)}) collective-permute-start(bf16[1,8,256,128]{3,2,1,0:T(8,128)(2,1)S(1)} %slice_bitcast_fusion), channel_id=1, source_target_pairs={{0,16},{8,24},{16,0},{24,8},{1,17},{9,25},{17,1},{25,9},{2,18},{10... | collective-permute-start | bytes 1572872 | tf_op jit(solution)/shard_map/ppermute | solution.py:19
  34.9 21.0 %collective-permute-start.9 = (bf16[2,8,256,128]{3,2,1,0:T(8,128)(2,1)}, bf16[2,8,256,128]{3,2,1,0:T(8,128)(2,1)}, u32[]{:S(2)}, u32[]{:S(2)}) collective-permute-start(bf16[2,8,256,128]{3,2,1,0:T(8,128)(2,1)} %pad_maximum_fusion.1), channel_id=1, source_target_pairs={{0,8},{8,0},{16,24},{24,16},{1,9},{9,1},{17,25},{25,17},{2,10},{10... | collective-permute-start | bytes 3145736 | tf_op jit(solution)/shard_map/ppermute | solution.py:19
  34.9 8.8 %collective-permute-start.20 = (bf16[1,128,1024]{2,1,0:T(8,128)(2,1)S(1)}, bf16[1,128,1024]{2,1,0:T(8,128)(2,1)S(1)}, u32[]{:S(2)}, u32[]{:S(2)}) collective-permute-start(bf16[1,128,1024]{2,1,0:T(8,128)(2,1)S(1)} %maximum_bitcast_fusion), channel_id=1, source_target_pairs={{0,16},{8,24},{16,0},{24,8},{1,17},{9,25},{17,1},{25,9},{2,18},{10... | collective-permute-start | bytes 786440 | tf_op jit(solution)/shard_map/ppermute | solution.py:19
  36.6 39.1 %copy-start.2 = (s32[2]{0:T(128)}, s32[2]{0:T(128)S(1)}, u32[]{:S(2)}) copy-start(s32[2]{0:T(128)S(1)} %pad_add_fusion.1.at) | copy-start | bytes 28
  37.5 7.2 %collective-permute-start.10 = (bf16[64,1536]{1,0:T(8,128)(2,1)S(1)}, bf16[64,1536]{1,0:T(8,128)(2,1)S(1)}, u32[]{:S(2)}, u32[]{:S(2)}) collective-permute-start(bf16[64,1536]{1,0:T(8,128)(2,1)S(1)} %get-tuple-element.40), channel_id=1, source_target_pairs={{0,1},{1,0},{2,3},{3,2},{4,5},{5,4},{6,7},{7,6},{8,9},{9,8},{10,11... | collective-permute-start | bytes 589832 | tf_op jit(solution)/shard_map/ppermute | solution.py:19
  39.0 8.9 %collective-permute-start.11 = (bf16[64,1536]{1,0:T(8,128)(2,1)S(1)}, bf16[64,1536]{1,0:T(8,128)(2,1)S(1)}, u32[]{:S(2)}, u32[]{:S(2)}) collective-permute-start(bf16[64,1536]{1,0:T(8,128)(2,1)S(1)} %get-tuple-element.41), channel_id=1, source_target_pairs={{0,2},{1,3},{2,0},{3,1},{4,6},{5,7},{6,4},{7,5},{8,10},{9,11},{10,... | collective-permute-start | bytes 589832 | tf_op jit(solution)/shard_map/ppermute | solution.py:19
  40.3 9.6 %collective-permute-start.12 = (bf16[64,1536]{1,0:T(8,128)(2,1)S(1)}, bf16[64,1536]{1,0:T(8,128)(2,1)S(1)}, u32[]{:S(2)}, u32[]{:S(2)}) collective-permute-start(bf16[64,1536]{1,0:T(8,128)(2,1)S(1)} %get-tuple-element.42), channel_id=1, source_target_pairs={{0,3},{1,2},{2,1},{3,0},{4,7},{5,6},{6,5},{7,4},{8,11},{9,10},{10,... | collective-permute-start | bytes 589832 | tf_op jit(solution)/shard_map/ppermute | solution.py:19
  43.8 47.0 %collective-permute-start.21 = (bf16[2,128,1024]{2,1,0:T(8,128)(2,1)S(1)}, bf16[2,128,1024]{2,1,0:T(8,128)(2,1)S(1)}, u32[]{:S(2)}, u32[]{:S(2)}) collective-permute-start(bf16[2,128,1024]{2,1,0:T(8,128)(2,1)S(1)} %pad_maximum_fusion.3), channel_id=1, source_target_pairs={{0,8},{8,0},{16,24},{24,16},{1,9},{9,1},{17,25},{25,17},{2,10},{10... | collective-permute-start | bytes 1572872 | tf_op jit(solution)/shard_map/ppermute | solution.py:19
  44.7 25.9 %collective-permute-start.4 = (bf16[64,1536]{1,0:T(8,128)(2,1)S(1)}, bf16[64,1536]{1,0:T(8,128)(2,1)S(1)}, u32[]{:S(2)}, u32[]{:S(2)}) collective-permute-start(bf16[64,1536]{1,0:T(8,128)(2,1)S(1)} %get-tuple-element.35), channel_id=1, source_target_pairs={{0,4},{1,5},{2,6},{3,7},{4,0},{5,1},{6,2},{7,3},{8,12},{9,13},{10,... | collective-permute-start | bytes 589832 | tf_op jit(solution)/shard_map/ppermute | solution.py:19
  47.9 27.7 %collective-permute-start.5 = (bf16[64,1536]{1,0:T(8,128)(2,1)S(1)}, bf16[64,1536]{1,0:T(8,128)(2,1)S(1)}, u32[]{:S(2)}, u32[]{:S(2)}) collective-permute-start(bf16[64,1536]{1,0:T(8,128)(2,1)S(1)} %get-tuple-element.36), channel_id=1, source_target_pairs={{0,5},{1,4},{2,7},{3,6},{4,1},{5,0},{6,3},{7,2},{8,13},{9,12},{10,... | collective-permute-start | bytes 589832 | tf_op jit(solution)/shard_map/ppermute | solution.py:19
  49.9 25.7 %collective-permute-start.6 = (bf16[64,1536]{1,0:T(8,128)(2,1)S(1)}, bf16[64,1536]{1,0:T(8,128)(2,1)S(1)}, u32[]{:S(2)}, u32[]{:S(2)}) collective-permute-start(bf16[64,1536]{1,0:T(8,128)(2,1)S(1)} %get-tuple-element.37), channel_id=1, source_target_pairs={{0,6},{1,7},{2,4},{3,5},{4,2},{5,3},{6,0},{7,1},{8,14},{9,15},{10,... | collective-permute-start | bytes 589832 | tf_op jit(solution)/shard_map/ppermute | solution.py:19
  55.9 19.8 %collective-permute-start.7 = (bf16[64,1536]{1,0:T(8,128)(2,1)S(1)}, bf16[64,1536]{1,0:T(8,128)(2,1)S(1)}, u32[]{:S(2)}, u32[]{:S(2)}) collective-permute-start(bf16[64,1536]{1,0:T(8,128)(2,1)S(1)} %get-tuple-element.38), channel_id=1, source_target_pairs={{0,7},{1,6},{2,5},{3,4},{4,3},{5,2},{6,1},{7,0},{8,15},{9,14},{10,... | collective-permute-start | bytes 589832 | tf_op jit(solution)/shard_map/ppermute | solution.py:19
  78.1 0.6 copy-start.1
  78.8 0.6 copy-start.3
  79.4 13.3 %collective-permute-start.22 = (bf16[64,768]{1,0:T(8,128)(2,1)S(1)}, bf16[64,768]{1,0:T(8,128)(2,1)S(1)}, u32[]{:S(2)}, u32[]{:S(2)}) collective-permute-start(bf16[64,768]{1,0:T(8,128)(2,1)S(1)} %get-tuple-element.52), channel_id=1, source_target_pairs={{0,1},{1,0},{2,3},{3,2},{4,5},{5,4},{6,7},{7,6},{8,9},{9,8},{10,11... | collective-permute-start | bytes 294920 | tf_op jit(solution)/shard_map/ppermute | solution.py:19
  80.0 14.2 %collective-permute-start.23 = (bf16[64,768]{1,0:T(8,128)(2,1)S(1)}, bf16[64,768]{1,0:T(8,128)(2,1)S(1)}, u32[]{:S(2)}, u32[]{:S(2)}) collective-permute-start(bf16[64,768]{1,0:T(8,128)(2,1)S(1)} %get-tuple-element.53), channel_id=1, source_target_pairs={{0,2},{1,3},{2,0},{3,1},{4,6},{5,7},{6,4},{7,5},{8,10},{9,11},{10,... | collective-permute-start | bytes 294920 | tf_op jit(solution)/shard_map/ppermute | solution.py:19
  88.8 8.6 %collective-permute-start.24 = (bf16[64,768]{1,0:T(8,128)(2,1)S(1)}, bf16[64,768]{1,0:T(8,128)(2,1)S(1)}, u32[]{:S(2)}, u32[]{:S(2)}) collective-permute-start(bf16[64,768]{1,0:T(8,128)(2,1)S(1)} %get-tuple-element.54), channel_id=1, source_target_pairs={{0,3},{1,2},{2,1},{3,0},{4,7},{5,6},{6,5},{7,4},{8,11},{9,10},{10,... | collective-permute-start | bytes 294920 | tf_op jit(solution)/shard_map/ppermute | solution.py:19
  89.6 14.7 %collective-permute-start.25 = (bf16[64,768]{1,0:T(8,128)(2,1)S(1)}, bf16[64,768]{1,0:T(8,128)(2,1)S(1)}, u32[]{:S(2)}, u32[]{:S(2)}) collective-permute-start(bf16[64,768]{1,0:T(8,128)(2,1)S(1)} %get-tuple-element.55), channel_id=1, source_target_pairs={{0,4},{1,5},{2,6},{3,7},{4,0},{5,1},{6,2},{7,3},{8,12},{9,13},{10,... | collective-permute-start | bytes 294920 | tf_op jit(solution)/shard_map/ppermute | solution.py:19
  90.8 15.8 %collective-permute-start.26 = (bf16[64,768]{1,0:T(8,128)(2,1)S(1)}, bf16[64,768]{1,0:T(8,128)(2,1)S(1)}, u32[]{:S(2)}, u32[]{:S(2)}) collective-permute-start(bf16[64,768]{1,0:T(8,128)(2,1)S(1)} %get-tuple-element.56), channel_id=1, source_target_pairs={{0,5},{1,4},{2,7},{3,6},{4,1},{5,0},{6,3},{7,2},{8,13},{9,12},{10,... | collective-permute-start | bytes 294920 | tf_op jit(solution)/shard_map/ppermute | solution.py:19
  92.7 13.4 %copy-start.15 = (bf16[64,768]{1,0:T(8,128)(2,1)}, bf16[64,768]{1,0:T(8,128)(2,1)S(1)}, u32[]{:S(2)}) copy-start(bf16[64,768]{1,0:T(8,128)(2,1)S(1)} %collective-permute-done.22.refs_1_) | copy-start | bytes 294916
  92.7 15.7 %collective-permute-start.27 = (bf16[64,768]{1,0:T(8,128)(2,1)S(1)}, bf16[64,768]{1,0:T(8,128)(2,1)S(1)}, u32[]{:S(2)}, u32[]{:S(2)}) collective-permute-start(bf16[64,768]{1,0:T(8,128)(2,1)S(1)} %get-tuple-element.57), channel_id=1, source_target_pairs={{0,6},{1,7},{2,4},{3,5},{4,2},{5,3},{6,0},{7,1},{8,14},{9,15},{10,... | collective-permute-start | bytes 294920 | tf_op jit(solution)/shard_map/ppermute | solution.py:19
  94.2 11.9 %copy-start.16 = (bf16[64,768]{1,0:T(8,128)(2,1)}, bf16[64,768]{1,0:T(8,128)(2,1)S(1)}, u32[]{:S(2)}) copy-start(bf16[64,768]{1,0:T(8,128)(2,1)S(1)} %collective-permute-done.23.refs_2_) | copy-start | bytes 294916
  94.2 15.0 %collective-permute-start.28 = (bf16[64,768]{1,0:T(8,128)(2,1)S(1)}, bf16[64,768]{1,0:T(8,128)(2,1)S(1)}, u32[]{:S(2)}, u32[]{:S(2)}) collective-permute-start(bf16[64,768]{1,0:T(8,128)(2,1)S(1)} %get-tuple-element.58), channel_id=1, source_target_pairs={{0,7},{1,6},{2,5},{3,4},{4,3},{5,2},{6,1},{7,0},{8,15},{9,14},{10,... | collective-permute-start | bytes 294920 | tf_op jit(solution)/shard_map/ppermute | solution.py:19
  97.4 8.7 %copy-start.17 = (bf16[64,768]{1,0:T(8,128)(2,1)}, bf16[64,768]{1,0:T(8,128)(2,1)S(1)}, u32[]{:S(2)}) copy-start(bf16[64,768]{1,0:T(8,128)(2,1)S(1)} %collective-permute-done.24.refs_3_) | copy-start | bytes 294916
  97.4 14.7 %collective-permute-start.13 = (bf16[64,768]{1,0:T(8,128)(2,1)S(1)}, bf16[64,768]{1,0:T(8,128)(2,1)S(1)}, u32[]{:S(2)}, u32[]{:S(2)}) collective-permute-start(bf16[64,768]{1,0:T(8,128)(2,1)S(1)} %get-tuple-element.44), channel_id=1, source_target_pairs={{0,1},{1,0},{2,3},{3,2},{4,5},{5,4},{6,7},{7,6},{8,9},{9,8},{10,11... | collective-permute-start | bytes 294920 | tf_op jit(solution)/shard_map/ppermute | solution.py:19
  104.4 1.7 %copy-start.18 = (bf16[64,768]{1,0:T(8,128)(2,1)}, bf16[64,768]{1,0:T(8,128)(2,1)S(1)}, u32[]{:S(2)}) copy-start(bf16[64,768]{1,0:T(8,128)(2,1)S(1)} %collective-permute-done.25.refs_4_) | copy-start | bytes 294916
  104.4 10.7 %collective-permute-start.14 = (bf16[64,768]{1,0:T(8,128)(2,1)S(1)}, bf16[64,768]{1,0:T(8,128)(2,1)S(1)}, u32[]{:S(2)}, u32[]{:S(2)}) collective-permute-start(bf16[64,768]{1,0:T(8,128)(2,1)S(1)} %get-tuple-element.45), channel_id=1, source_target_pairs={{0,2},{1,3},{2,0},{3,1},{4,6},{5,7},{6,4},{7,5},{8,10},{9,11},{10,... | collective-permute-start | bytes 294920 | tf_op jit(solution)/shard_map/ppermute | solution.py:19
  106.6 9.7 %copy-start.19 = (bf16[64,768]{1,0:T(8,128)(2,1)}, bf16[64,768]{1,0:T(8,128)(2,1)S(1)}, u32[]{:S(2)}) copy-start(bf16[64,768]{1,0:T(8,128)(2,1)S(1)} %collective-permute-done.26.refs_5_) | copy-start | bytes 294916
  106.6 15.5 %collective-permute-start.15 = (bf16[64,768]{1,0:T(8,128)(2,1)S(1)}, bf16[64,768]{1,0:T(8,128)(2,1)S(1)}, u32[]{:S(2)}, u32[]{:S(2)}) collective-permute-start(bf16[64,768]{1,0:T(8,128)(2,1)S(1)} %get-tuple-element.46), channel_id=1, source_target_pairs={{0,3},{1,2},{2,1},{3,0},{4,7},{5,6},{6,5},{7,4},{8,11},{9,10},{10,... | collective-permute-start | bytes 294920 | tf_op jit(solution)/shard_map/ppermute | solution.py:19
  108.4 7.9 %copy-start.20 = (bf16[64,768]{1,0:T(8,128)(2,1)}, bf16[64,768]{1,0:T(8,128)(2,1)S(1)}, u32[]{:S(2)}) copy-start(bf16[64,768]{1,0:T(8,128)(2,1)S(1)} %collective-permute-done.27.refs_6_) | copy-start | bytes 294916
  108.4 13.8 %collective-permute-start.16 = (bf16[64,768]{1,0:T(8,128)(2,1)S(1)}, bf16[64,768]{1,0:T(8,128)(2,1)S(1)}, u32[]{:S(2)}, u32[]{:S(2)}) collective-permute-start(bf16[64,768]{1,0:T(8,128)(2,1)S(1)} %get-tuple-element.47), channel_id=1, source_target_pairs={{0,4},{1,5},{2,6},{3,7},{4,0},{5,1},{6,2},{7,3},{8,12},{9,13},{10,... | collective-permute-start | bytes 294920 | tf_op jit(solution)/shard_map/ppermute | solution.py:19
  109.2 7.1 %copy-start.21 = (bf16[64,768]{1,0:T(8,128)(2,1)}, bf16[64,768]{1,0:T(8,128)(2,1)S(1)}, u32[]{:S(2)}) copy-start(bf16[64,768]{1,0:T(8,128)(2,1)S(1)} %collective-permute-done.28.refs_7_) | copy-start | bytes 294916
  109.2 15.4 %collective-permute-start.17 = (bf16[64,768]{1,0:T(8,128)(2,1)S(1)}, bf16[64,768]{1,0:T(8,128)(2,1)S(1)}, u32[]{:S(2)}, u32[]{:S(2)}) collective-permute-start(bf16[64,768]{1,0:T(8,128)(2,1)S(1)} %get-tuple-element.48), channel_id=1, source_target_pairs={{0,5},{1,4},{2,7},{3,6},{4,1},{5,0},{6,3},{7,2},{8,13},{9,12},{10,... | collective-permute-start | bytes 294920 | tf_op jit(solution)/shard_map/ppermute | solution.py:19
  112.1 10.1 %copy-start.8 = (bf16[64,768]{1,0:T(8,128)(2,1)}, bf16[64,768]{1,0:T(8,128)(2,1)S(1)}, u32[]{:S(2)}) copy-start(bf16[64,768]{1,0:T(8,128)(2,1)S(1)} %collective-permute-done.13.refs_1_) | copy-start | bytes 294916
  112.1 12.5 %collective-permute-start.18 = (bf16[64,768]{1,0:T(8,128)(2,1)S(1)}, bf16[64,768]{1,0:T(8,128)(2,1)S(1)}, u32[]{:S(2)}, u32[]{:S(2)}) collective-permute-start(bf16[64,768]{1,0:T(8,128)(2,1)S(1)} %get-tuple-element.49), channel_id=1, source_target_pairs={{0,6},{1,7},{2,4},{3,5},{4,2},{5,3},{6,0},{7,1},{8,14},{9,15},{10,... | collective-permute-start | bytes 294920 | tf_op jit(solution)/shard_map/ppermute | solution.py:19
  115.0 7.1 %copy-start.9 = (bf16[64,768]{1,0:T(8,128)(2,1)}, bf16[64,768]{1,0:T(8,128)(2,1)S(1)}, u32[]{:S(2)}) copy-start(bf16[64,768]{1,0:T(8,128)(2,1)S(1)} %collective-permute-done.14.refs_2_) | copy-start | bytes 294916
  115.0 9.6 %collective-permute-start.19 = (bf16[64,768]{1,0:T(8,128)(2,1)S(1)}, bf16[64,768]{1,0:T(8,128)(2,1)S(1)}, u32[]{:S(2)}, u32[]{:S(2)}) collective-permute-start(bf16[64,768]{1,0:T(8,128)(2,1)S(1)} %get-tuple-element.50), channel_id=1, source_target_pairs={{0,7},{1,6},{2,5},{3,4},{4,3},{5,2},{6,1},{7,0},{8,15},{9,14},{10,... | collective-permute-start | bytes 294920 | tf_op jit(solution)/shard_map/ppermute | solution.py:19
  122.2 2.5 %copy-start.10 = (bf16[64,768]{1,0:T(8,128)(2,1)}, bf16[64,768]{1,0:T(8,128)(2,1)S(1)}, u32[]{:S(2)}) copy-start(bf16[64,768]{1,0:T(8,128)(2,1)S(1)} %collective-permute-done.15.refs_3_) | copy-start | bytes 294916
  122.2 2.4 %copy-start.11 = (bf16[64,768]{1,0:T(8,128)(2,1)}, bf16[64,768]{1,0:T(8,128)(2,1)S(1)}, u32[]{:S(2)}) copy-start(bf16[64,768]{1,0:T(8,128)(2,1)S(1)} %collective-permute-done.16.refs_4_) | copy-start | bytes 294916
  124.6 0.7 copy-start.12
  124.6 0.7 copy-start.13
  124.6 0.7 copy-start.14
  131.4 12.7 %copy-start.5 = (f32[2,128,512]{2,1,0:T(8,128)S(1)}, f32[2,128,512]{2,1,0:T(8,128)}, u32[]{:S(2)}) copy-start(f32[2,128,512]{2,1,0:T(8,128)} %get-tuple-element.63) | copy-start | bytes 1572868
  131.4 1.8 %collective-permute-start.34 = (bf16[2,128,512]{2,1,0:T(8,128)(2,1)}, bf16[2,128,512]{2,1,0:T(8,128)(2,1)S(1)}, u32[]{:S(2)}, u32[]{:S(2)}) collective-permute-start(bf16[2,128,512]{2,1,0:T(8,128)(2,1)} %get-tuple-element.66), channel_id=1, source_target_pairs={{0,8},{8,0},{16,24},{24,16},{1,9},{9,1},{17,25},{25,17},{2,10},{10... | collective-permute-start | bytes 786440 | tf_op jit(solution)/shard_map/ppermute | solution.py:19
  131.5 4.3 %collective-permute-start.29 = (bf16[2,128,512]{2,1,0:T(8,128)(2,1)}, bf16[2,128,512]{2,1,0:T(8,128)(2,1)S(1)}, u32[]{:S(2)}, u32[]{:S(2)}) collective-permute-start(bf16[2,128,512]{2,1,0:T(8,128)(2,1)} %get-tuple-element.64), channel_id=1, source_target_pairs={{0,8},{8,0},{16,24},{24,16},{1,9},{9,1},{17,25},{25,17},{2,10},{10... | collective-permute-start | bytes 786440 | tf_op jit(solution)/shard_map/ppermute | solution.py:19
  134.2 6.1 %collective-permute-start.35 = (bf16[1,128,512]{2,1,0:T(8,128)(2,1)S(1)}, bf16[1,128,512]{2,1,0:T(8,128)(2,1)S(1)}, u32[]{:S(2)}, u32[]{:S(2)}) collective-permute-start(bf16[1,128,512]{2,1,0:T(8,128)(2,1)S(1)} %add_convert_fusion), channel_id=1, source_target_pairs={{0,16},{8,24},{16,0},{24,8},{1,17},{9,25},{17,1},{25,9},{2,18},{10... | collective-permute-start | bytes 393224 | tf_op jit(solution)/shard_map/ppermute | solution.py:19
  136.8 7.4 %collective-permute-start.30 = (bf16[1,128,512]{2,1,0:T(8,128)(2,1)S(1)}, bf16[1,128,512]{2,1,0:T(8,128)(2,1)S(1)}, u32[]{:S(2)}, u32[]{:S(2)}) collective-permute-start(bf16[1,128,512]{2,1,0:T(8,128)(2,1)S(1)} %add_convert_fusion.1), channel_id=1, source_target_pairs={{0,16},{8,24},{16,0},{24,8},{1,17},{9,25},{17,1},{25,9},{2,18},{10... | collective-permute-start | bytes 393224 | tf_op jit(solution)/shard_map/ppermute | solution.py:19
  141.4 5.7 %collective-permute-start.36 = (bf16[128,512]{1,0:T(8,128)(2,1)S(1)}, bf16[128,512]{1,0:T(8,128)(2,1)S(1)}, u32[]{:S(2)}, u32[]{:S(2)}) collective-permute-start(bf16[128,512]{1,0:T(8,128)(2,1)S(1)} %get-tuple-element.67), channel_id=1, source_target_pairs={{0,2},{1,3},{2,0},{3,1},{4,6},{5,7},{6,4},{7,5},{8,10},{9,11},{10,... | collective-permute-start | bytes 393224 | tf_op jit(solution)/shard_map/ppermute | solution.py:19
  144.2 5.3 %collective-permute-start.31 = (bf16[128,512]{1,0:T(8,128)(2,1)S(1)}, bf16[128,512]{1,0:T(8,128)(2,1)S(1)}, u32[]{:S(2)}, u32[]{:S(2)}) collective-permute-start(bf16[128,512]{1,0:T(8,128)(2,1)S(1)} %get-tuple-element.69), channel_id=1, source_target_pairs={{0,1},{1,0},{2,3},{3,2},{4,5},{5,4},{6,7},{7,6},{8,9},{9,8},{10,11... | collective-permute-start | bytes 393224 | tf_op jit(solution)/shard_map/ppermute | solution.py:19
  147.1 5.9 %collective-permute-start.37 = (bf16[128,512]{1,0:T(8,128)(2,1)S(1)}, bf16[128,512]{1,0:T(8,128)(2,1)S(1)}, u32[]{:S(2)}, u32[]{:S(2)}) collective-permute-start(bf16[128,512]{1,0:T(8,128)(2,1)S(1)} %fusion.3), channel_id=1, source_target_pairs={{0,4},{1,5},{2,6},{3,7},{4,0},{5,1},{6,2},{7,3},{8,12},{9,13},{10,... | collective-permute-start | bytes 393224 | tf_op jit(solution)/shard_map/ppermute | solution.py:19
  149.5 5.0 %collective-permute-start.32 = (bf16[128,512]{1,0:T(8,128)(2,1)S(1)}, bf16[128,512]{1,0:T(8,128)(2,1)S(1)}, u32[]{:S(2)}, u32[]{:S(2)}) collective-permute-start(bf16[128,512]{1,0:T(8,128)(2,1)S(1)} %fusion.2), channel_id=1, source_target_pairs={{0,2},{1,3},{2,0},{3,1},{4,6},{5,7},{6,4},{7,5},{8,10},{9,11},{10,... | collective-permute-start | bytes 393224 | tf_op jit(solution)/shard_map/ppermute | solution.py:19
  153.1 5.0 %collective-permute-start.38 = (bf16[128,512]{1,0:T(8,128)(2,1)S(1)}, bf16[128,512]{1,0:T(8,128)(2,1)S(1)}, u32[]{:S(2)}, u32[]{:S(2)}) collective-permute-start(bf16[128,512]{1,0:T(8,128)(2,1)S(1)} %fusion.1), channel_id=1, source_target_pairs={{0,1},{1,0},{2,3},{3,2},{4,5},{5,4},{6,7},{7,6},{8,9},{9,8},{10,11... | collective-permute-start | bytes 393224 | tf_op jit(solution)/shard_map/ppermute | solution.py:19
  154.6 7.3 %collective-permute-start.33 = (bf16[128,512]{1,0:T(8,128)(2,1)S(1)}, bf16[128,512]{1,0:T(8,128)(2,1)S(1)}, u32[]{:S(2)}, u32[]{:S(2)}) collective-permute-start(bf16[128,512]{1,0:T(8,128)(2,1)S(1)} %fusion), channel_id=1, source_target_pairs={{0,4},{1,5},{2,6},{3,7},{4,0},{5,1},{6,2},{7,3},{8,12},{9,13},{10,... | collective-permute-start | bytes 393224 | tf_op jit(solution)/shard_map/ppermute | solution.py:19
